TPU v7x, 128 devices: a whole 4x4x4 slice. The times are simulated.
128 devices in a mesh: gx: 16 (over x, y), gy: 8 (over z, core).
Axes of the slice: x: 4, y: 4, z: 4, core: 2. Of those that a mesh axis runs over, the one named last changes fastest.
Arguments:
- efield_vector: float32 [3, 512, 256, 256], P(None, 'gx', 'gy'), may hold values from -6 to 6
- hfield_vector: float32 [3, 512, 256, 256], P(None, 'gx', 'gy'), may hold values from -6 to 6
- dielectric_grid: float32 [512, 256, 256], P('gx', 'gy'), may hold values from 1 to 6
- sigma_grid: float32 [512, 256, 256], P('gx', 'gy'), may hold values from 0 to 0.5
- substance_label: int32 [512, 256, 256], P('gx', 'gy'), may hold values from 0 to 2
- thermal_state: float32 [16384, 8, 256], P(('gx', 'gy')), may hold values from 0 to 2
- wetness_share: float32 [16384, 8, 256], P(('gx', 'gy')), may hold values from 0.1 to 1
- dielectric_line_choice: int32 [16384, 8, 256], P(('gx', 'gy')), may hold values from 0 to 15
- dielectric_lookup_lines: float32 [4, 16], replicated, may hold values from 0.2 to 2
- dispatch_keeper_map: int32 [128, 128], P(('gx', 'gy')), may hold values from 0 to 127, each once within a row
- arrival_position_map: int32 [128, 128], P(('gx', 'gy')), may hold values from 0 to 127, each once within a row
Outputs:
- final_efield: float32 [3, 512, 256, 256], P(None, 'gx', 'gy')
- final_hfield: float32 [3, 512, 256, 256], P(None, 'gx', 'gy')
- permittivity_out: float32 [512, 256, 256], P('gx', 'gy')
- conductivity_out: float32 [512, 256, 256], P('gx', 'gy')
- temperature_out: float32 [16384, 8, 256], P(('gx', 'gy'))
- moisture_out: float32 [16384, 8, 256], P(('gx', 'gy'))
Inputs may be any that keep to these rules, and one draw needn't show every extreme that they name: Each row names every device index once: block k of device s goes to device dispatch_keeper_map[s, k]. `arrival_position_map`: each row names every slot once.
All inputs are finite; a program needn't handle non-finite values.
Results may differ from a plain program's by a relative error of at most 0.00002.
Values sent between devices are 32-bit elements; how exact they have to be, the bound alone decides.
No kernel may reach another device: no remote copies, remote signals or barrier semaphores. Data moves between devices by JAX's collectives and lax.ppermute only.
A program may use at most 128 MiB of HBM per device.

v0:
```python
import jax
import jax.numpy as jnp
from jax import lax
from jax.sharding import PartitionSpec as P

STEPS = 2


TIME_STEP = 0.5
DIFFUSION_FACTOR = 0.2
WARMING_FACTOR = 0.5
BOILING = 1.0
EVAP_RATE = 2.0
VAPOUR_ENTHALPY = 0.8


def passed_along(value, axis, by):
    count = lax.axis_size(axis)
    pairs = [(i, i + by) for i in range(count) if 0 <= i + by < count]
    return lax.ppermute(value, axis, pairs)


def forward_diff(values, border, along):
    extent = values.shape[along]
    nxt = jnp.concatenate(
        [lax.slice_in_dim(values, 1, extent, axis=along), jnp.expand_dims(border, along)],
        axis=along,
    )
    return nxt - values


def backward_diff(values, border, along):
    extent = values.shape[along]
    prev = jnp.concatenate(
        [jnp.expand_dims(border, along), lax.slice_in_dim(values, 0, extent - 1, axis=along)],
        axis=along,
    )
    return values - prev


def lookup(dielectric_lookup_lines, dielectric_line_choice, column):
    moisture_levels = jnp.arange(dielectric_lookup_lines.shape[1], dtype=jnp.int32)
    matches = dielectric_line_choice[None] == moisture_levels[:, None, None, None]
    return jnp.sum(
        jnp.where(matches, dielectric_lookup_lines[column][:, None, None, None], 0.0), axis=0
    )


def thermal_wetness_advance(thermal_state, wetness_share, deposited_wattage, lookup_factors):
    above_depth_entry = jnp.concatenate([thermal_state[..., 1:], thermal_state[..., -1:]], axis=-1)
    beneath_depth_entry = jnp.concatenate(
        [thermal_state[..., :1], thermal_state[..., :-1]], axis=-1
    )
    warmed_voxels = (
        thermal_state
        + DIFFUSION_FACTOR
        * (above_depth_entry - thermal_state + (beneath_depth_entry - thermal_state))
        + WARMING_FACTOR * deposited_wattage
    )
    excess = jnp.maximum(warmed_voxels - BOILING, 0.0)
    vaporised_water = wetness_share * (1.0 - jnp.exp(-EVAP_RATE * excess))
    wetness_refreshed = wetness_share - vaporised_water
    warmth_refreshed = warmed_voxels - VAPOUR_ENTHALPY * vaporised_water
    dielectric_refreshed = 1.0 + lookup_factors[0] + 4.0 * lookup_factors[1] * wetness_refreshed
    sigma_refreshed = 0.1 * lookup_factors[2] + 0.3 * lookup_factors[3] * wetness_refreshed
    return (warmth_refreshed, wetness_refreshed, dielectric_refreshed, sigma_refreshed)


def local(
    efield_vector,
    hfield_vector,
    dielectric_grid,
    sigma_grid,
    substance_label,
    thermal_state,
    wetness_share,
    dielectric_line_choice,
    dielectric_lookup_lines,
    dispatch_keeper_map,
    arrival_position_map,
):
    elec_x, elec_y, elec_z = (efield_vector[0], efield_vector[1], efield_vector[2])
    mag_x, mag_y, mag_z = (hfield_vector[0], hfield_vector[1], hfield_vector[2])
    loss_half = sigma_grid * (0.5 * TIME_STEP) / dielectric_grid
    scale_e = (1.0 - loss_half) / (1.0 + loss_half)
    scale_c = TIME_STEP / dielectric_grid / (1.0 + loss_half)
    zero_z = jnp.zeros_like(elec_x[:, :, 0])
    squares = jnp.zeros_like(dielectric_grid)
    for repeat in range(STEPS):
        border_x = passed_along(jnp.stack([elec_y[0], elec_z[0]]), "gx", -1)
        border_y = passed_along(jnp.stack([elec_x[:, 0], elec_z[:, 0]]), "gy", -1)
        mag_x = mag_x - TIME_STEP * (
            forward_diff(elec_z, border_y[1], 1) - forward_diff(elec_y, zero_z, 2)
        )
        mag_y = mag_y - TIME_STEP * (
            forward_diff(elec_x, zero_z, 2) - forward_diff(elec_z, border_x[1], 0)
        )
        mag_z = mag_z - TIME_STEP * (
            forward_diff(elec_y, border_x[0], 0) - forward_diff(elec_x, border_y[0], 1)
        )
        back_x = passed_along(jnp.stack([mag_y[-1], mag_z[-1]]), "gx", 1)
        back_y = passed_along(jnp.stack([mag_x[:, -1], mag_z[:, -1]]), "gy", 1)
        elec_x = scale_e * elec_x + scale_c * (
            backward_diff(mag_z, back_y[1], 1) - backward_diff(mag_y, zero_z, 2)
        )
        elec_y = scale_e * elec_y + scale_c * (
            backward_diff(mag_x, zero_z, 2) - backward_diff(mag_z, back_x[1], 0)
        )
        elec_z = scale_e * elec_z + scale_c * (
            backward_diff(mag_y, back_x[0], 0) - backward_diff(mag_x, back_y[0], 1)
        )
        squares = squares + (elec_x * elec_x + elec_y * elec_y + elec_z * elec_z)
    deposited_wattage = 0.5 * sigma_grid * squares
    rows_x = lax.axis_size("gx")
    rows_y = lax.axis_size("gy")
    devices = rows_x * rows_y
    depth = deposited_wattage.shape[2]
    width = deposited_wattage.shape[0] * deposited_wattage.shape[1] // devices
    destinations = dispatch_keeper_map[0]
    slots_here = arrival_position_map[0]
    outgoing = deposited_wattage.reshape(devices, width, depth)[jnp.argsort(destinations)]
    arrived = lax.all_to_all(outgoing, ("gx", "gy"), split_axis=0, concat_axis=0, tiled=True)
    wattage_each_tile = arrived[jnp.argsort(slots_here)]
    lookup_factors = [
        lookup(dielectric_lookup_lines, dielectric_line_choice, column) for column in range(4)
    ]
    warmth_refreshed, wetness_refreshed, dielectric_refreshed, sigma_refreshed = (
        thermal_wetness_advance(thermal_state, wetness_share, wattage_each_tile, lookup_factors)
    )
    perm_rows = dielectric_refreshed[slots_here]
    cond_rows = sigma_refreshed[slots_here]
    perm_back, cond_back = (
        lax.all_to_all(perm_rows, ("gx", "gy"), split_axis=0, concat_axis=0, tiled=True),
        lax.all_to_all(cond_rows, ("gx", "gy"), split_axis=0, concat_axis=0, tiled=True),
    )
    perm_cells = perm_back[destinations].reshape(dielectric_grid.shape)
    cond_cells = cond_back[destinations].reshape(sigma_grid.shape)
    product = substance_label == 2
    dielectric_result = jnp.where(product, perm_cells, dielectric_grid)
    sigma_result = jnp.where(product, cond_cells, sigma_grid)
    final_efield = jnp.stack([elec_x, elec_y, elec_z])
    final_hfield = jnp.stack([mag_x, mag_y, mag_z])
    return (
        final_efield,
        final_hfield,
        dielectric_result,
        sigma_result,
        warmth_refreshed,
        wetness_refreshed,
    )


def solution(mesh):
    in_specs = (
        P(None, "gx", "gy", None),
        P(None, "gx", "gy", None),
        P("gx", "gy", None),
        P("gx", "gy", None),
        P("gx", "gy", None),
        P(("gx", "gy"), None, None),
        P(("gx", "gy"), None, None),
        P(("gx", "gy"), None, None),
        P(),
        P(("gx", "gy"), None),
        P(("gx", "gy"), None),
    )
    out_specs = (
        P(None, "gx", "gy", None),
        P(None, "gx", "gy", None),
        P("gx", "gy", None),
        P("gx", "gy", None),
        P(("gx", "gy"), None, None),
        P(("gx", "gy"), None, None),
    )
    return jax.shard_map(local, mesh=mesh, in_specs=in_specs, out_specs=out_specs, check_vma=False)
```

profile of v0, /device:TPU:1, one launch (start us, length us, event | category | flops | bytes accessed | tf_op | source)
XLA Modules:
  0.0 162.5 jit_solution(15241343784807080345)
XLA Ops:
  0.6 2.4 %slice_bitcast_fusion.1 = (f32[32,32,256]{2,1,0:T(8,128)S(1)}, f32[32,32,256]{2,1,0:T(8,128)S(1)}, f32[32,32,256]{2,1,0:T(8,128)S(1)}) fusion(f32[3,32,32,256]{3,2,1,0:T(8,128)} %param.11), kind=kLoop, calls=%fused_computation.80 | loop fusion | bytes 6291456 | tf_op jit(solution)/shard_map/squeeze | solution.py:82
  3.1 3.3 %collective-permute-start.1 = (f32[2,32,256]{2,0,1:T(2,128)S(1)}, f32[2,32,256]{2,0,1:T(2,128)S(1)}, u32[]{:S(2)}, u32[]{:S(2)}) collective-permute-start(f32[2,32,256]{2,0,1:T(2,128)S(1)} %pad_maximum_fusion.3), channel_id=1, source_target_pairs={{1,0},{2,1},{3,2},{4,3},{5,4},{6,5},{7,6},{9,8},{10,9},{11,10},{12... | collective-permute-start | bytes 196616 | tf_op jit(solution)/shard_map/ppermute | solution.py:20
  6.5 1.3 collective-permute-start
  7.8 1.1 slice.313
  8.9 1.3 slice.324
  10.2 1.1 slice.317
  11.3 1.4 slice_bitcast_fusion.3
  12.7 1.6 %fusion.48 = (f32[128,8,255]{2,1,0:T(8,128)}, f32[128,8,255]{2,1,0:T(8,128)}) fusion(f32[128,8,256]{2,1,0:T(8,128)S(1)} %copy-done.1), kind=kLoop, calls=%fused_computation.128 | loop fusion | bytes 4177920 | tf_op jit(solution)/shard_map/slice | solution.py:50
  14.4 1.1 fusion.49
  15.5 1.3 slice.319
  16.8 2.6 %sort.31 = (s32[128]{0:T(128)}, s32[128]{0:T(128)S(1)}) sort(s32[128]{0:T(128)S(1)} %bitcast.127, s32[128]{0:T(128)S(1)} %iota.14), dimensions={0}, to_apply=%region_2.3 | sort | flops 896 | bytes 2048 | tf_op jit(solution)/shard_map/jit(argsort)/sort | solution.py:121
  19.5 2.6 %sort.32 = (s32[128]{0:T(128)}, s32[128]{0:T(128)S(1)}) sort(s32[128]{0:T(128)S(1)} %bitcast.126, s32[128]{0:T(128)S(1)} %iota.15), dimensions={0}, to_apply=%region_3.4 | sort | flops 896 | bytes 2048 | tf_op jit(solution)/shard_map/jit(argsort)/sort | solution.py:123
  22.2 5.2 %fusion.11 = (f32[32,32,256]{2,1,0:T(8,128)S(1)}, f32[32,32,256]{2,1,0:T(8,128)S(1)}, f32[32,32,256]{2,1,0:T(8,128)S(1)}) fusion(f32[1,32,256]{2,1,0:T(8,128)S(1)} %get-tuple-element.58, f32[31,32,256]{2,1,0:T(8,128)} %get-tuple-element.32, f32[32,32,255]{2,1,0:T(8,128)} %slice.324, f32[3,32,32,256]{3,2,1,0:T(8,128)} %param.12, ...), kind=kLoop, calls=%fused_computation.29 | loop fusion | flops 4980736 | bytes 15720448 | tf_op jit(solution)/shard_map/sub | solution.py:95
  27.9 3.7 %collective-permute-start.2 = (f32[2,32,256]{2,0,1:T(2,128)S(1)}, f32[2,32,256]{2,0,1:T(2,128)S(1)}, u32[]{:S(2)}, u32[]{:S(2)}) collective-permute-start(f32[2,32,256]{2,0,1:T(2,128)S(1)} %pad_maximum_fusion.4), channel_id=1, source_target_pairs={{0,1},{1,2},{2,3},{3,4},{4,5},{5,6},{6,7},{8,9},{9,10},{10,11},{11... | collective-permute-start | bytes 196616 | tf_op jit(solution)/shard_map/ppermute | solution.py:20
  31.5 4.3 %collective-permute-start.3 = (f32[2,32,256]{2,1,0:T(8,128)S(1)}, f32[2,32,256]{2,1,0:T(8,128)S(1)}, u32[]{:S(2)}, u32[]{:S(2)}) collective-permute-start(f32[2,32,256]{2,1,0:T(8,128)S(1)} %pad_maximum_fusion.5), channel_id=1, source_target_pairs={{0,8},{8,16},{16,24},{24,32},{32,40},{40,48},{48,56},{56,64},{64,7... | collective-permute-start | bytes 196616 | tf_op jit(solution)/shard_map/ppermute | solution.py:20
  35.9 1.1 fusion.8
  37.1 1.5 fusion.14
  39.8 1.3 collective-permute-start.4
  41.2 1.9 %collective-permute-start.5 = (f32[2,32,256]{2,0,1:T(2,128)S(1)}, f32[2,32,256]{2,0,1:T(2,128)S(1)}, u32[]{:S(2)}, u32[]{:S(2)}) collective-permute-start(f32[2,32,256]{2,0,1:T(2,128)S(1)} %pad_maximum_fusion.7), channel_id=1, source_target_pairs={{1,0},{2,1},{3,2},{4,3},{5,4},{6,5},{7,6},{9,8},{10,9},{11,10},{12... | collective-permute-start | bytes 196616 | tf_op jit(solution)/shard_map/ppermute | solution.py:20
  43.1 2.9 %collective-permute-done.4 = f32[2,32,256]{2,1,0:T(8,128)S(1)} collective-permute-done((f32[2,32,256]{2,1,0:T(8,128)S(1)}, f32[2,32,256]{2,1,0:T(8,128)S(1)}, u32[]{:S(2)}, u32[]{:S(2)}) %collective-permute-start.4) | collective-permute-done | bytes 65568 | tf_op jit(solution)/shard_map/ppermute | solution.py:20
  46.1 0.7 collective-permute-done.5
  46.9 1.9 %fusion.23 = (f32[32,32,256]{2,1,0:T(8,128)S(1)}, f32[32,32,256]{2,1,0:T(8,128)S(1)}, f32[32,32,256]{2,1,0:T(8,128)S(1)}) fusion(f32[32,32,256]{2,1,0:T(8,128)S(1)} %get-tuple-element.31, f32[32,32,256]{2,1,0:T(8,128)S(1)} %get-tuple-element.28, f32[32,1,256]{2,1,0:T(1,128)S(1)} %get-tuple-element.50, f32[32,31,256]{2,1,0:T(8,128)S(1)} %slice.344, ...), kind=kLoop, calls=%fused_computation.47 | loop fusion | flops 4980736 | bytes 15720448 | tf_op jit(solution)/shard_map/sub | solution.py:92
  49.0 4.3 %collective-permute-start.7 = (f32[2,32,256]{2,1,0:T(8,128)S(1)}, f32[2,32,256]{2,1,0:T(8,128)S(1)}, u32[]{:S(2)}, u32[]{:S(2)}) collective-permute-start(f32[2,32,256]{2,1,0:T(8,128)S(1)} %pad_maximum_fusion.9), channel_id=1, source_target_pairs={{0,8},{8,16},{16,24},{24,32},{32,40},{40,48},{48,56},{56,64},{64,7... | collective-permute-start | bytes 196616 | tf_op jit(solution)/shard_map/ppermute | solution.py:20
  53.5 2.5 %collective-permute-start.6 = (f32[2,32,256]{2,0,1:T(2,128)S(1)}, f32[2,32,256]{2,0,1:T(2,128)S(1)}, u32[]{:S(2)}, u32[]{:S(2)}) collective-permute-start(f32[2,32,256]{2,0,1:T(2,128)S(1)} %pad_maximum_fusion.8), channel_id=1, source_target_pairs={{0,1},{1,2},{2,3},{3,4},{4,5},{5,6},{6,7},{8,9},{9,10},{10,11},{11... | collective-permute-start | bytes 196616 | tf_op jit(solution)/shard_map/ppermute | solution.py:20
  56.0 1.3 collective-permute-done.6
  57.4 3.6 %add_multiply_fusion = (f32[32,32,256]{2,1,0:T(8,128)}, f32[32,32,256]{2,1,0:T(8,128)}, f32[32,32,256]{2,1,0:T(8,128)}, f32[32,32,256]{2,1,0:T(8,128)}) fusion(f32[32,32,256]{2,1,0:T(8,128)S(1)} %get-tuple-element.28, f32[32,32,256]{2,1,0:T(8,128)S(1)} %get-tuple-element.27, f32[32,32,256]{2,1,0:T(8,128)S(1)} %get-tuple-element.24, ...), kind=kLoop, calls=%fused_computation.78 | loop fusion | flops 9175040 | bytes 19914752 | tf_op jit(solution)/shard_map/mul | solution.py:113
  61.0 2.8 %gather_fusion = f32[128,8,256]{2,1,0:T(8,128)} fusion(f32[128,8,256]{2,1,0:T(8,128)} %bitcast.120, s32[1024]{0:T(1024)S(1)} %pad_clamp_fusion.3), kind=kCustom, calls=%fused_computation | custom fusion | bytes 2097664 | tf_op jit(solution)/shard_map/gather | solution.py:121
  63.9 15.1 %all-to-all-start = ((f32[128,8,256]{2,1,0:T(8,128)}), f32[128,8,256]{2,1,0:T(8,128)}, u32[]{:S(2)}, u32[]{:S(2)}) async-start(f32[128,8,256]{2,1,0:T(8,128)} %gather_fusion), calls=%async_computation | async-start | bytes 2097152 | tf_op jit(solution)/shard_map/all_to_all | solution.py:122
  79.0 10.0 %select_reduce_fusion.1 = (f32[128,8,256]{2,1,0:T(8,128)}, f32[128,8,256]{2,1,0:T(8,128)}, f32[128,8,256]{2,1,0:T(8,128)}, f32[128,8,256]{2,1,0:T(8,128)}) fusion(f32[16]{0:T(128)S(1)} %get-tuple-element.65, s32[128,8,256]{2,1,0:T(8,128)} %param.18, f32[16]{0:T(128)S(1)} %get-tuple-element.64, f32[16]{0:T(128)S(1)} %get-tuple-element.63, ...), kind=kLoop, calls=%fused_computation.7 | loop fusion | flops 36700160 | bytes 5243136 | tf_op jit(solution)/shard_map/reduce_sum | solution.py:44
  89.0 8.9 %all-to-all-done = f32[128,8,256]{2,1,0:T(8,128)} async-done(((f32[128,8,256]{2,1,0:T(8,128)}), f32[128,8,256]{2,1,0:T(8,128)}, u32[]{:S(2)}, u32[]{:S(2)}) %all-to-all-start) | async-done | bytes 1048608 | tf_op jit(solution)/shard_map/all_to_all | solution.py:122
  97.9 2.8 %gather_fusion.1 = f32[128,8,256]{2,1,0:T(8,128)} fusion(f32[128,8,256]{2,1,0:T(8,128)} %all-to-all-done, s32[1024]{0:T(1024)S(1)} %pad_clamp_fusion.2), kind=kCustom, calls=%fused_computation.1 | custom fusion | bytes 2097664 | tf_op jit(solution)/shard_map/gather | solution.py:123
  100.7 4.7 %multiply_subtract_fusion = (f32[128,8,256]{2,1,0:T(8,128)}, f32[128,8,256]{2,1,0:T(8,128)S(1)}) fusion(f32[128,8,256]{2,1,0:T(8,128)} %param.17, f32[128,8,256]{2,1,0:T(8,128)} %gather_fusion.1, f32[128,8,256]{2,1,0:T(8,128)} %param.16, f32[128,8,255]{2,1,0:T(8,128)} %get-tuple-element.40, f32[128,8,1]{2,1,0:T(8,128)} %get-tuple-element.42, ...), kind=kLoop, calls=%fused_computation.73 | loop fusion | flops 4194304 | bytes 7340032 | tf_op jit(solution)/shard_map/sub | solution.py:63
  105.4 1.7 %multiply_add_fusion = (f32[128,8,256]{2,1,0:T(8,128)}, f32[128,8,256]{2,1,0:T(8,128)}) fusion(f32[128,8,256]{2,1,0:T(8,128)S(1)} %copy-done.10, f32[128,8,256]{2,1,0:T(8,128)S(1)} %copy-done.9, f32[128,8,256]{2,1,0:T(8,128)S(1)} %copy-done.11, f32[128,8,256]{2,1,0:T(8,128)S(1)} %get-tuple-element.15), kind=kLoop, calls=%fused_computation.74 | loop fusion | flops 2621440 | bytes 6291456 | tf_op jit(solution)/shard_map/add | solution.py:65
  107.2 2.9 %gather_fusion.4 = f32[128,8,256]{2,1,0:T(8,128)} fusion(f32[128,8,256]{2,1,0:T(8,128)} %get-tuple-element.18, s32[1024]{0:T(1024)S(1)} %pad_clamp_fusion.1), kind=kCustom, calls=%fused_computation.4 | custom fusion | bytes 2097664 | tf_op jit(solution)/shard_map/gather | solution.py:131
  110.0 5.6 %all-to-all-start.2 = ((f32[128,8,256]{2,1,0:T(8,128)}), f32[128,8,256]{2,1,0:T(8,128)}, u32[]{:S(2)}, u32[]{:S(2)}) async-start(f32[128,8,256]{2,1,0:T(8,128)} %gather_fusion.4), calls=%async_computation.2 | async-start | bytes 2097152 | tf_op jit(solution)/shard_map/all_to_all | solution.py:134
  115.7 3.0 %multiply_add_fusion.1 = f32[128,8,256]{2,1,0:T(8,128)} fusion(f32[128,8,256]{2,1,0:T(8,128)} %get-tuple-element.19, f32[128,8,256]{2,1,0:T(8,128)} %get-tuple-element.12, f32[128,8,256]{2,1,0:T(8,128)} %get-tuple-element.13), kind=kLoop, calls=%fused_computation.75 | loop fusion | flops 1048576 | bytes 4194304 | tf_op jit(solution)/shard_map/add | solution.py:64
  118.7 2.8 %gather_fusion.2 = f32[128,8,256]{2,1,0:T(8,128)} fusion(f32[128,8,256]{2,1,0:T(8,128)} %multiply_add_fusion.1, s32[1024]{0:T(1024)S(1)} %pad_clamp_fusion.1), kind=kCustom, calls=%fused_computation.2 | custom fusion | bytes 2097664 | tf_op jit(solution)/shard_map/gather | solution.py:130
  121.5 13.2 %all-to-all-done.2 = f32[128,8,256]{2,1,0:T(8,128)} async-done(((f32[128,8,256]{2,1,0:T(8,128)}), f32[128,8,256]{2,1,0:T(8,128)}, u32[]{:S(2)}, u32[]{:S(2)}) %all-to-all-start.2) | async-done | bytes 1048608 | tf_op jit(solution)/shard_map/all_to_all | solution.py:134
  134.7 5.6 %all-to-all-start.1 = ((f32[128,8,256]{2,1,0:T(8,128)}), f32[128,8,256]{2,1,0:T(8,128)}, u32[]{:S(2)}, u32[]{:S(2)}) async-start(f32[128,8,256]{2,1,0:T(8,128)} %gather_fusion.2), calls=%async_computation.1 | async-start | bytes 2097152 | tf_op jit(solution)/shard_map/all_to_all | solution.py:133
  140.4 1.9 %pad_maximum_fusion.1 = f32[3,32,32,256]{3,2,1,0:T(8,128)} fusion(f32[1,32,32,256]{3,2,1,0:T(8,128)S(1)} %bitcast.115, f32[1,32,32,256]{3,2,1,0:T(8,128)S(1)} %bitcast.119, f32[1,32,32,256]{3,2,1,0:T(8,128)S(1)} %bitcast.113), kind=kLoop, calls=%fused_computation.12 | loop fusion | flops 1572864 | bytes 6291456 | tf_op jit(solution)/shard_map/stack | solution.py:142
  142.3 0.5 copy-done.7
  142.8 0.6 copy-done.8
  143.4 2.0 %pad_maximum_fusion = f32[3,32,32,256]{3,2,1,0:T(8,128)} fusion(f32[1,32,32,256]{3,2,1,0:T(8,128)S(1)} %bitcast.125, f32[1,32,32,256]{3,2,1,0:T(8,128)S(1)} %bitcast.124, f32[1,32,32,256]{3,2,1,0:T(8,128)S(1)} %bitcast.123), kind=kLoop, calls=%fused_computation.11 | loop fusion | flops 1572864 | bytes 6291456 | tf_op jit(solution)/shard_map/stack | solution.py:141
  145.4 1.9 %gather_fusion.5 = f32[128,8,256]{2,1,0:T(8,128)S(1)} fusion(f32[128,8,256]{2,1,0:T(8,128)} %all-to-all-done.2, s32[1024]{0:T(1024)S(1)} %pad_clamp_fusion), kind=kCustom, calls=%fused_computation.5 | custom fusion | bytes 2097664 | tf_op jit(solution)/shard_map/gather | solution.py:137
  147.3 2.6 %bitcast_select_fusion = (f32[32,32,256]{2,1,0:T(8,128)}, pred[32,32,256]{2,1,0:T(8,128)(4,1)S(1)}) fusion(f32[32,32,256]{2,1,0:T(8,128)S(1)} %copy-done.3, s32[32,32,256]{2,1,0:T(8,128)} %param.15, f32[32,32,256]{2,1,0:T(8,128)S(1)} %bitcast.121), kind=kLoop, calls=%fused_computation.71 | loop fusion | flops 524288 | bytes 4456448 | tf_op jit(solution)/shard_map/jit(_where)/select_n | solution.py:140
  149.9 9.5 %all-to-all-done.1 = f32[128,8,256]{2,1,0:T(8,128)} async-done(((f32[128,8,256]{2,1,0:T(8,128)}), f32[128,8,256]{2,1,0:T(8,128)}, u32[]{:S(2)}, u32[]{:S(2)}) %all-to-all-start.1) | async-done | bytes 1048608 | tf_op jit(solution)/shard_map/all_to_all | solution.py:133
  159.4 1.9 %gather_fusion.3 = f32[128,8,256]{2,1,0:T(8,128)S(1)} fusion(f32[128,8,256]{2,1,0:T(8,128)} %all-to-all-done.1, s32[1024]{0:T(1024)S(1)} %pad_clamp_fusion), kind=kCustom, calls=%fused_computation.3 | custom fusion | bytes 2097664 | tf_op jit(solution)/shard_map/gather | solution.py:136
  161.3 1.2 bitcast_select_fusion.1
  (84 shorter events, 2.5 us)
Async XLA Ops:
  0.6 5.9 %copy-start = (f32[3,32,32,256]{3,2,1,0:T(8,128)S(1)}, f32[3,32,32,256]{3,2,1,0:T(8,128)}, u32[]{:S(2)}) copy-start(f32[3,32,32,256]{3,2,1,0:T(8,128)} %param.11) | copy-start | bytes 9437188
  3.1 19.0 %collective-permute-start.1 = (f32[2,32,256]{2,0,1:T(2,128)S(1)}, f32[2,32,256]{2,0,1:T(2,128)S(1)}, u32[]{:S(2)}, u32[]{:S(2)}) collective-permute-start(f32[2,32,256]{2,0,1:T(2,128)S(1)} %pad_maximum_fusion.3), channel_id=1, source_target_pairs={{1,0},{2,1},{3,2},{4,3},{5,4},{6,5},{7,6},{9,8},{10,9},{11,10},{12... | collective-permute-start | bytes 196616 | tf_op jit(solution)/shard_map/ppermute | solution.py:20
  6.5 15.7 %collective-permute-start = (f32[2,32,256]{2,1,0:T(8,128)S(1)}, f32[2,32,256]{2,1,0:T(8,128)S(1)}, u32[]{:S(2)}, u32[]{:S(2)}) collective-permute-start(f32[2,32,256]{2,1,0:T(8,128)S(1)} %pad_maximum_fusion.2), channel_id=1, source_target_pairs={{8,0},{16,8},{24,16},{32,24},{40,32},{48,40},{56,48},{64,56},{72,6... | collective-permute-start | bytes 196616 | tf_op jit(solution)/shard_map/ppermute | solution.py:20
  10.2 2.5 %copy-start.1 = (f32[128,8,256]{2,1,0:T(8,128)S(1)}, f32[128,8,256]{2,1,0:T(8,128)}, u32[]{:S(2)}) copy-start(f32[128,8,256]{2,1,0:T(8,128)} %param.16) | copy-start | bytes 3145732
  14.4 2.5 %copy-start.14 = (s32[1,128]{1,0:T(1,128)S(1)}, s32[1,128]{1,0:T(1,128)}, u32[]{:S(2)}) copy-start(s32[1,128]{1,0:T(1,128)} %param.20) | copy-start | bytes 1540
  14.4 5.1 %copy-start.13 = (s32[1,128]{1,0:T(1,128)S(1)}, s32[1,128]{1,0:T(1,128)}, u32[]{:S(2)}) copy-start(s32[1,128]{1,0:T(1,128)} %param.21) | copy-start | bytes 1540
  14.4 7.7 %copy-start.12 = (f32[4,16]{1,0:T(4,128)S(1)}, f32[4,16]{1,0:T(4,128)}, u32[]{:S(2)}) copy-start(f32[4,16]{1,0:T(4,128)} %param.19) | copy-start | bytes 772
  27.5 8.4 %copy-start.2 = (f32[32,32,256]{2,1,0:T(8,128)S(1)}, f32[32,32,256]{2,1,0:T(8,128)}, u32[]{:S(2)}) copy-start(f32[32,32,256]{2,1,0:T(8,128)} %param.14) | copy-start | bytes 3145732
  27.5 8.4 %copy-start.4 = (f32[32,32,256]{2,1,0:T(8,128)S(1)}, f32[32,32,256]{2,1,0:T(8,128)}, u32[]{:S(2)}) copy-start(f32[32,32,256]{2,1,0:T(8,128)} %param.13) | copy-start | bytes 3145732
  27.9 8.0 %collective-permute-start.2 = (f32[2,32,256]{2,0,1:T(2,128)S(1)}, f32[2,32,256]{2,0,1:T(2,128)S(1)}, u32[]{:S(2)}, u32[]{:S(2)}) collective-permute-start(f32[2,32,256]{2,0,1:T(2,128)S(1)} %pad_maximum_fusion.4), channel_id=1, source_target_pairs={{0,1},{1,2},{2,3},{3,4},{4,5},{5,6},{6,7},{8,9},{9,10},{10,11},{11... | collective-permute-start | bytes 196616 | tf_op jit(solution)/shard_map/ppermute | solution.py:20
  31.5 5.6 %collective-permute-start.3 = (f32[2,32,256]{2,1,0:T(8,128)S(1)}, f32[2,32,256]{2,1,0:T(8,128)S(1)}, u32[]{:S(2)}, u32[]{:S(2)}) collective-permute-start(f32[2,32,256]{2,1,0:T(8,128)S(1)} %pad_maximum_fusion.5), channel_id=1, source_target_pairs={{0,8},{8,16},{16,24},{24,32},{32,40},{40,48},{48,56},{56,64},{64,7... | collective-permute-start | bytes 196616 | tf_op jit(solution)/shard_map/ppermute | solution.py:20
  39.8 6.2 %collective-permute-start.4 = (f32[2,32,256]{2,1,0:T(8,128)S(1)}, f32[2,32,256]{2,1,0:T(8,128)S(1)}, u32[]{:S(2)}, u32[]{:S(2)}) collective-permute-start(f32[2,32,256]{2,1,0:T(8,128)S(1)} %pad_maximum_fusion.6), channel_id=1, source_target_pairs={{8,0},{16,8},{24,16},{32,24},{40,32},{48,40},{56,48},{64,56},{72,6... | collective-permute-start | bytes 196616 | tf_op jit(solution)/shard_map/ppermute | solution.py:20
  41.2 5.6 %collective-permute-start.5 = (f32[2,32,256]{2,0,1:T(2,128)S(1)}, f32[2,32,256]{2,0,1:T(2,128)S(1)}, u32[]{:S(2)}, u32[]{:S(2)}) collective-permute-start(f32[2,32,256]{2,0,1:T(2,128)S(1)} %pad_maximum_fusion.7), channel_id=1, source_target_pairs={{1,0},{2,1},{3,2},{4,3},{5,4},{6,5},{7,6},{9,8},{10,9},{11,10},{12... | collective-permute-start | bytes 196616 | tf_op jit(solution)/shard_map/ppermute | solution.py:20
  49.0 7.0 %collective-permute-start.7 = (f32[2,32,256]{2,1,0:T(8,128)S(1)}, f32[2,32,256]{2,1,0:T(8,128)S(1)}, u32[]{:S(2)}, u32[]{:S(2)}) collective-permute-start(f32[2,32,256]{2,1,0:T(8,128)S(1)} %pad_maximum_fusion.9), channel_id=1, source_target_pairs={{0,8},{8,16},{16,24},{24,32},{32,40},{40,48},{48,56},{56,64},{64,7... | collective-permute-start | bytes 196616 | tf_op jit(solution)/shard_map/ppermute | solution.py:20
  53.5 3.9 %collective-permute-start.6 = (f32[2,32,256]{2,0,1:T(2,128)S(1)}, f32[2,32,256]{2,0,1:T(2,128)S(1)}, u32[]{:S(2)}, u32[]{:S(2)}) collective-permute-start(f32[2,32,256]{2,0,1:T(2,128)S(1)} %pad_maximum_fusion.8), channel_id=1, source_target_pairs={{0,1},{1,2},{2,3},{3,4},{4,5},{5,6},{6,7},{8,9},{9,10},{10,11},{11... | collective-permute-start | bytes 196616 | tf_op jit(solution)/shard_map/ppermute | solution.py:20
  63.9 34.0 %all-to-all-start = ((f32[128,8,256]{2,1,0:T(8,128)}), f32[128,8,256]{2,1,0:T(8,128)}, u32[]{:S(2)}, u32[]{:S(2)}) async-start(f32[128,8,256]{2,1,0:T(8,128)} %gather_fusion), calls=%async_computation | async-start | bytes 2097152 | tf_op jit(solution)/shard_map/all_to_all | solution.py:122
  100.7 4.7 %copy-start.9 = (f32[128,8,256]{2,1,0:T(8,128)S(1)}, f32[128,8,256]{2,1,0:T(8,128)}, u32[]{:S(2)}) copy-start(f32[128,8,256]{2,1,0:T(8,128)} %get-tuple-element.10) | copy-start | bytes 3145732
  100.7 4.7 %copy-start.10 = (f32[128,8,256]{2,1,0:T(8,128)S(1)}, f32[128,8,256]{2,1,0:T(8,128)}, u32[]{:S(2)}) copy-start(f32[128,8,256]{2,1,0:T(8,128)} %get-tuple-element.11) | copy-start | bytes 3145732
  100.7 4.7 %copy-start.11 = (f32[128,8,256]{2,1,0:T(8,128)S(1)}, f32[128,8,256]{2,1,0:T(8,128)}, u32[]{:S(2)}) copy-start(f32[128,8,256]{2,1,0:T(8,128)} %param.17) | copy-start | bytes 3145732
  110.0 24.7 %all-to-all-start.2 = ((f32[128,8,256]{2,1,0:T(8,128)}), f32[128,8,256]{2,1,0:T(8,128)}, u32[]{:S(2)}, u32[]{:S(2)}) async-start(f32[128,8,256]{2,1,0:T(8,128)} %gather_fusion.4), calls=%async_computation.2 | async-start | bytes 2097152 | tf_op jit(solution)/shard_map/all_to_all | solution.py:134
  134.7 24.7 %all-to-all-start.1 = ((f32[128,8,256]{2,1,0:T(8,128)}), f32[128,8,256]{2,1,0:T(8,128)}, u32[]{:S(2)}, u32[]{:S(2)}) async-start(f32[128,8,256]{2,1,0:T(8,128)} %gather_fusion.2), calls=%async_computation.1 | async-start | bytes 2097152 | tf_op jit(solution)/shard_map/all_to_all | solution.py:133
  140.4 1.9 %copy-start.6 = (f32[32,32,256]{2,1,0:T(8,128)S(1)}, f32[32,32,256]{2,1,0:T(8,128)}, u32[]{:S(2)}) copy-start(f32[32,32,256]{2,1,0:T(8,128)} %get-tuple-element.21) | copy-start | bytes 3145732
  140.4 2.4 %copy-start.7 = (f32[32,32,256]{2,1,0:T(8,128)S(1)}, f32[32,32,256]{2,1,0:T(8,128)}, u32[]{:S(2)}) copy-start(f32[32,32,256]{2,1,0:T(8,128)} %get-tuple-element.22) | copy-start | bytes 3145732
  140.4 3.0 %copy-start.8 = (f32[32,32,256]{2,1,0:T(8,128)S(1)}, f32[32,32,256]{2,1,0:T(8,128)}, u32[]{:S(2)}) copy-start(f32[32,32,256]{2,1,0:T(8,128)} %get-tuple-element.23) | copy-start | bytes 3145732
  143.4 3.9 %copy-start.3 = (f32[32,32,256]{2,1,0:T(8,128)S(1)}, f32[32,32,256]{2,1,0:T(8,128)}, u32[]{:S(2)}) copy-start(f32[32,32,256]{2,1,0:T(8,128)} %param.14) | copy-start | bytes 3145732
  147.3 14.0 %copy-start.5 = (f32[32,32,256]{2,1,0:T(8,128)S(1)}, f32[32,32,256]{2,1,0:T(8,128)}, u32[]{:S(2)}) copy-start(f32[32,32,256]{2,1,0:T(8,128)} %param.13) | copy-start | bytes 3145732
where the time goes:
time: 163 us; the launch traced here: 162 us
  starting transfers between devices  49 us (30%)
  other arithmetic  46 us (28%)
  waiting for transfers between devices  36.7 us (23%)
  local copies, waits for them, and re-layouts  29.5 us (18%)
    ppermute x8, starting transfers between devices, passed_along(): return lax.ppermute(value, axis, pairs)  22.6 us
    all_to_all x1, starting transfers between devices, local(): lax.all_to_all(outgoing, ('gx', 'gy'), split_axis=0, concat_axis=0, tiled...  15.1 us
    all_to_all x1, waiting for transfers between devices, local(): lax.all_to_all(cond_rows, ('gx', 'gy'), split_axis=0, concat_axis=0, tile...  13.2 us
    reduce_sum x1, other arithmetic, lookup(): jnp.sum(jnp.where(matches, dielectric_lookup_lines[column][:, None, None,...  10 us
    all_to_all x1, waiting for transfers between devices, local(): lax.all_to_all(perm_rows, ('gx', 'gy'), split_axis=0, concat_axis=0, tile...  9.53 us
    all_to_all x1, waiting for transfers between devices, local(): lax.all_to_all(outgoing, ('gx', 'gy'), split_axis=0, concat_axis=0, tiled...  8.88 us
    slice x11, local copies, waits for them, and re-layouts, forward_diff(): lax.slice_in_dim(values, 1, extent, axis=along)  7.32 us
    all_to_all x1, starting transfers between devices, local(): lax.all_to_all(cond_rows, ('gx', 'gy'), split_axis=0, concat_axis=0, tile...  5.64 us
  transfers between devices with their start and end apart: 11, of which 7 were waited for; matrix products, arithmetic and copies ran while one was open for 25% of the time, Pallas kernels for 0%

commit v1 on v0

v1 whole, which is shorter than its diff:
```python
import functools

import jax
import jax.numpy as jnp
from jax import lax
from jax.experimental import pallas as pl
from jax.experimental.pallas import tpu as pltpu
from jax.sharding import PartitionSpec as P

DT = 0.5
MIB = 1 << 20


def passed_along(value, axis, by):
    count = lax.axis_size(axis)
    pairs = [(i, i + by) for i in range(count) if 0 <= i + by < count]
    return lax.ppermute(value, axis, pairs)


def vmem_spec():
    return pl.BlockSpec(memory_space=pltpu.VMEM)


def smem_spec():
    return pl.BlockSpec(memory_space=pltpu.SMEM)


def f32(*shape):
    return jax.ShapeDtypeStruct(shape, jnp.float32)


def dense(count):
    return [vmem_spec()] * count


def limit(mib):
    return pltpu.CompilerParams(vmem_limit_bytes=mib * MIB)


def cost(ops, nbytes):
    return pl.CostEstimate(flops=ops, bytes_accessed=nbytes, transcendentals=0)


def halo_kernel(layer_ref, e_ref, sx_ref, sy_ref):
    sx_ref[0] = layer_ref[1, 0]
    sx_ref[1] = layer_ref[2, 0]
    for x in range(e_ref.shape[1]):
        sy_ref[0, x : x + 1, :] = e_ref[0, x, 0:1, :]
        sy_ref[1, x : x + 1, :] = e_ref[2, x, 0:1, :]


def first_halo(efield):
    _, nx, ny, nz = efield.shape
    return pl.pallas_call(
        halo_kernel,
        grid=(1,),
        in_specs=[
            pl.BlockSpec((3, 1, ny, nz), lambda i: (0, 0, 0, 0)),
            pl.BlockSpec((3, nx, 8, nz), lambda i: (0, 0, 0, 0)),
        ],
        out_specs=[vmem_spec(), vmem_spec()],
        out_shape=[f32(2, ny, nz), f32(2, nx, nz)],
        compiler_params=limit(4),
        name="halo",
    )(efield, efield)


def patch_last(value, row):
    ny, nz = value.shape
    at = lax.broadcasted_iota(jnp.int32, (8, nz), 0) == 7
    return jnp.concatenate([value[: ny - 8], jnp.where(at, row, value[ny - 8 :])], axis=0)


def patch_first(value, row):
    nz = value.shape[1]
    at = lax.broadcasted_iota(jnp.int32, (8, nz), 0) == 0
    return jnp.concatenate([jnp.where(at, row, value[:8]), value[8:]], axis=0)


def fwd_z(f):
    ny, nz = f.shape
    lane = lax.broadcasted_iota(jnp.int32, f.shape, 1)
    return jnp.where(lane == nz - 1, 0.0, pltpu.roll(f, nz - 1, 1)) - f


def bwd_z(f):
    lane = lax.broadcasted_iota(jnp.int32, f.shape, 1)
    return f - jnp.where(lane == 0, 0.0, pltpu.roll(f, 1, 1))


def fwd_y(f):
    ny = f.shape[0]
    return patch_last(pltpu.roll(f, ny - 1, 0), 0.0) - f


def bwd_y(f):
    return f - patch_first(pltpu.roll(f, 1, 0), 0.0)


def e_slab(x, first, e_ref, layer_ref, rows_ref):
    ex, ey, ez = e_ref[0, x], e_ref[1, x], e_ref[2, x]
    if rows_ref is not None:
        ex = patch_first(ex, rows_ref[0, pl.ds(x, 1), :])
        if first:
            ey, ez = layer_ref[0], layer_ref[1]
        else:
            ez = patch_first(ez, rows_ref[1, pl.ds(x, 1), :])
    return ex, ey, ez


def h_slab(x, last, h_ref, layer_ref, rows_ref):
    hx, hy, hz = h_ref[0, x], h_ref[1, x], h_ref[2, x]
    if rows_ref is not None:
        hx = patch_last(hx, rows_ref[0, pl.ds(x, 1), :])
        if last:
            hy, hz = layer_ref[0], layer_ref[1]
        else:
            hz = patch_last(hz, rows_ref[1, pl.ds(x, 1), :])
    return hx, hy, hz


def h_kernel(fixed, *refs):
    if fixed:
        e_ref, el_ref, er_ref, h_ref, hl_ref, hr_ref, out_ref, layer_ref, rows_ref = refs
    else:
        e_ref, h_ref, out_ref, layer_ref, rows_ref = refs
        el_ref = er_ref = hl_ref = hr_ref = None
    nx, ny, nz = e_ref.shape[1:]

    def slab(x, first, last):
        ex, ey, ez = e_slab(x, first, e_ref, el_ref, er_ref)
        hx, hy, hz = h_slab(x, last, h_ref, hl_ref, hr_ref)
        if last:
            ey_step, ez_step = -ey, -ez
        else:
            _, ey_next, ez_next = e_slab(x + 1, False, e_ref, el_ref, er_ref)
            ey_step, ez_step = ey_next - ey, ez_next - ez
        hx = hx - DT * (fwd_y(ez) - fwd_z(ey))
        hy = hy - DT * (fwd_z(ex) - ez_step)
        hz = hz - DT * (ey_step - fwd_y(ex))
        out_ref[0, x] = hx
        out_ref[1, x] = hy
        out_ref[2, x] = hz
        rows_ref[0, pl.ds(x, 1), :] = hx[ny - 1 : ny]
        rows_ref[1, pl.ds(x, 1), :] = hz[ny - 1 : ny]
        if last:
            layer_ref[0] = hy
            layer_ref[1] = hz

    slab(0, True, False)
    lax.fori_loop(1, nx - 1, lambda x, c: (slab(x, False, False), c)[1], 0)
    slab(nx - 1, False, True)


def h_update(efield, e_fix, hfield, h_fix):
    _, nx, ny, nz = efield.shape
    args = [efield, *e_fix, hfield, *h_fix]
    return pl.pallas_call(
        functools.partial(h_kernel, bool(e_fix)),
        in_specs=dense(len(args)),
        out_specs=dense(3),
        out_shape=[f32(3, nx, ny, nz), f32(2, ny, nz), f32(2, nx, nz)],
        compiler_params=limit(16),
        cost_estimate=cost(40 * nx * ny * nz, 9 * MIB),
        name="hstep",
    )(*args)


def h_border_kernel(layer_ref, rows_ref, gx_ref, gy_ref, layer_out, rows_out):
    ny, nx = layer_ref.shape[1], rows_ref.shape[1]
    layer_out[0] = layer_ref[0] + DT * gx_ref[1]
    layer_out[1] = patch_last(
        layer_ref[1] - DT * gx_ref[0],
        layer_ref[1, ny - 1 : ny] - DT * gx_ref[0, ny - 1 : ny] + DT * gy_ref[0, nx - 1 : nx],
    )
    rows_out[0] = rows_ref[0] - DT * gy_ref[1]
    rows_out[1] = patch_last(
        rows_ref[1] + DT * gy_ref[0],
        rows_ref[1, nx - 1 : nx] - DT * gx_ref[0, ny - 1 : ny] + DT * gy_ref[0, nx - 1 : nx],
    )


def h_border(layer, rows, gx, gy):
    return pl.pallas_call(
        h_border_kernel,
        in_specs=dense(4),
        out_specs=dense(2),
        out_shape=[f32(*layer.shape), f32(*rows.shape)],
        compiler_params=limit(2),
        name="hborder",
    )(layer, rows, gx, gy)


def e_kernel(fixed, final, *refs):
    refs = list(refs)
    e_ref = refs.pop(0)
    el_ref, er_ref = (refs.pop(0), refs.pop(0)) if fixed else (None, None)
    h_ref, hl_ref, hr_ref, eps_ref, sig_ref, out_ref, layer_ref, rows_ref = refs[:8]
    nx, ny, nz = e_ref.shape[1:]

    def slab(x, first, last):
        hx, hy, hz = h_slab(x, last, h_ref, hl_ref, hr_ref)
        if first:
            hy_step, hz_step = hy, hz
        else:
            _, hy_prev, hz_prev = h_slab(x - 1, False, h_ref, hl_ref, hr_ref)
            hy_step, hz_step = hy - hy_prev, hz - hz_prev
        sig = sig_ref[x]
        quarter = 0.25 * sig
        eps = eps_ref[x]
        inv = 1.0 / (eps + quarter)
        scale_e = (eps - quarter) * inv
        scale_c = DT * inv
        ex0, ey0, ez0 = e_slab(x, first, e_ref, el_ref, er_ref)
        ex = scale_e * ex0 + scale_c * (bwd_y(hz) - bwd_z(hy))
        ey = scale_e * ey0 + scale_c * (bwd_z(hx) - hz_step)
        ez = scale_e * ez0 + scale_c * (hy_step - bwd_y(hx))
        out_ref[0, x] = ex
        out_ref[1, x] = ey
        out_ref[2, x] = ez
        at = pl.ds(x, 1)
        rows_ref[0, at, :] = ex[0:1]
        rows_ref[1, at, :] = ez[0:1]
        rows_ref[2, at, :] = scale_c[0:1]
        if first:
            layer_ref[0] = ey
            layer_ref[1] = ez
            layer_ref[2] = scale_c
        if final:
            before = ex0 * ex0 + ey0 * ey0 + ez0 * ez0
            half = 0.5 * sig
            refs[8][x] = half * (before + (ex * ex + ey * ey + ez * ez))
            rows_ref[3, at, :] = ey[0:1]
            rows_ref[4, at, :] = before[0:1]
            rows_ref[5, at, :] = half[0:1]
            if first:
                layer_ref[3] = ex
                layer_ref[4] = before
                layer_ref[5] = half

    slab(0, True, False)
    lax.fori_loop(1, nx - 1, lambda x, c: (slab(x, False, False), c)[1], 0)
    slab(nx - 1, False, True)


def e_update(efield, e_fix, hfield, h_fix, eps, sig, final):
    _, nx, ny, nz = efield.shape
    args = [efield, *e_fix, hfield, *h_fix, eps, sig]
    kept = 6 if final else 3
    outs = [f32(3, nx, ny, nz), f32(kept, ny, nz), f32(kept, nx, nz)]
    if final:
        outs.append(f32(nx, ny, nz))
    return pl.pallas_call(
        functools.partial(e_kernel, bool(e_fix), final),
        in_specs=dense(len(args)),
        out_specs=dense(len(outs)),
        out_shape=outs,
        compiler_params=limit(20),
        cost_estimate=cost(60 * nx * ny * nz, 11 * MIB),
        name="estep",
    )(*args)


def e_border_values(layer_ref, rows_ref, gx_ref, gy_ref):
    ey_layer = layer_ref[0] + layer_ref[2] * gx_ref[1]
    ez_layer = layer_ref[1] - layer_ref[2] * gx_ref[0]
    ez_layer = patch_first(ez_layer, ez_layer[0:1] + layer_ref[2, 0:1] * gy_ref[0, 0:1])
    ex_rows = rows_ref[0] - rows_ref[2] * gy_ref[1]
    ez_rows = patch_first(rows_ref[1] + rows_ref[2] * gy_ref[0], ez_layer[0:1])
    return ey_layer, ez_layer, ex_rows, ez_rows


def e_border_kernel(layer_ref, rows_ref, gx_ref, gy_ref, layer_out, rows_out):
    layer_out[0], layer_out[1], rows_out[0], rows_out[1] = e_border_values(
        layer_ref, rows_ref, gx_ref, gy_ref
    )


def e_border(layer, rows, gx, gy):
    return pl.pallas_call(
        e_border_kernel,
        in_specs=dense(4),
        out_specs=dense(2),
        out_shape=[f32(*gx.shape), f32(*gy.shape)],
        compiler_params=limit(2),
        name="eborder",
    )(layer, rows, gx, gy)


def power_kernel(dest, p_ref, layer_ref, rows_ref, gx_ref, gy_ref, out_ref, layer_out, rows_out, scratch):
    nx, ny, nz = p_ref.shape
    parts = ny // 8
    ey_layer, ez_layer, ex_rows, ez_rows = e_border_values(layer_ref, rows_ref, gx_ref, gy_ref)
    layer_out[0], layer_out[1], rows_out[0], rows_out[1] = ey_layer, ez_layer, ex_rows, ez_rows
    ex_layer = patch_first(layer_ref[3], ex_rows[0:1])
    squares = ex_layer * ex_layer + ey_layer * ey_layer + ez_layer * ez_layer
    layer_power = layer_ref[5] * (layer_ref[4] + squares)
    ey_rows = rows_ref[3]
    squares = ex_rows * ex_rows + ey_rows * ey_rows + ez_rows * ez_rows
    scratch[...] = rows_ref[5] * (rows_ref[4] + squares)
    top = lax.broadcasted_iota(jnp.int32, (8, nz), 0) == 0

    for part in range(parts):
        out_ref[dest[0, part]] = layer_power[part * 8 : part * 8 + 8]

    def body(x, carry):
        row = scratch[pl.ds(x, 1), :]
        out_ref[dest[0, x * parts]] = jnp.where(top, row, p_ref[x, 0:8, :])
        for part in range(1, parts):
            out_ref[dest[0, x * parts + part]] = p_ref[x, part * 8 : part * 8 + 8, :]
        return carry

    lax.fori_loop(1, nx, body, 0, unroll=2)


def power_border(dest, power, layer, rows, gx, gy):
    nx, ny, nz = power.shape
    return pl.pallas_call(
        power_kernel,
        in_specs=[smem_spec()] + dense(5),
        out_specs=dense(3),
        out_shape=[f32(nx * ny // 8, 8, nz), f32(*gx.shape), f32(*gy.shape)],
        scratch_shapes=[pltpu.VMEM((nx, nz), jnp.float32)],
        compiler_params=limit(8),
        cost_estimate=cost(4 * nx * ny * nz, 2 * MIB),
        name="power",
    )(dest, power, layer, rows, gx, gy)


def flush_kernel(e_ref, el_ref, er_ref, h_ref, hl_ref, hr_ref, e_out, h_out):
    nx = e_ref.shape[1]

    def slab(x, first, last):
        e_out[0, x], e_out[1, x], e_out[2, x] = e_slab(x, first, e_ref, el_ref, er_ref)
        h_out[0, x], h_out[1, x], h_out[2, x] = h_slab(x, last, h_ref, hl_ref, hr_ref)

    slab(0, True, False)
    lax.fori_loop(1, nx - 1, lambda x, c: (slab(x, False, False), c)[1], 0)
    slab(nx - 1, False, True)


def flush(efield, e_fix, hfield, h_fix):
    return pl.pallas_call(
        flush_kernel,
        in_specs=dense(6),
        out_specs=dense(2),
        out_shape=[f32(*efield.shape), f32(*hfield.shape)],
        compiler_params=limit(16),
        cost_estimate=cost(efield.size, 12 * MIB),
        name="flush",
    )(efield, *e_fix, hfield, *h_fix)


def lookup_kernel(lines, choice_ref, out_ref):
    levels = lines.shape[1]

    def body(j, carry):
        choice = choice_ref[j]
        factors = [jnp.full(choice.shape, lines[c, 0], jnp.float32) for c in range(4)]
        for level in range(1, levels):
            match = choice == level
            for c in range(4):
                factors[c] = jnp.where(match, lines[c, level], factors[c])
        out_ref[0, j] = 1.0 + factors[0]
        out_ref[1, j] = 4.0 * factors[1]
        out_ref[2, j] = 0.1 * factors[2]
        out_ref[3, j] = 0.3 * factors[3]
        return carry

    lax.fori_loop(0, choice_ref.shape[0], body, 0, unroll=2)


def lookup(lines, choice):
    n, width, nz = choice.shape
    return pl.pallas_call(
        lookup_kernel,
        in_specs=[smem_spec(), vmem_spec()],
        out_specs=vmem_spec(),
        out_shape=f32(4, n, width, nz),
        compiler_params=limit(10),
        cost_estimate=cost(80 * n * width * nz, 5 * MIB),
        name="lookup",
    )(lines, choice)


def thermal_kernel(arrive, p_ref, t_ref, w_ref, f_ref, send_out, t_out, w_out):
    n, width, nz = p_ref.shape
    lane = lax.broadcasted_iota(jnp.int32, (width, nz), 1)

    def body(s, carry):
        slot = arrive[0, s]
        state = t_ref[slot]
        above = jnp.where(lane == nz - 1, state, pltpu.roll(state, nz - 1, 1))
        below = jnp.where(lane == 0, state, pltpu.roll(state, 1, 1))
        heated = state + 0.2 * ((above - state) + (below - state)) + 0.5 * p_ref[s]
        wet = w_ref[slot]
        gone = wet * (1.0 - jnp.exp(-2.0 * jnp.maximum(heated - 1.0, 0.0)))
        left = wet - gone
        w_out[slot] = left
        t_out[slot] = heated - 0.8 * gone
        send_out[s, 0:width, :] = f_ref[0, slot] + f_ref[1, slot] * left
        send_out[s, width : 2 * width, :] = f_ref[2, slot] + f_ref[3, slot] * left
        return carry

    lax.fori_loop(0, n, body, 0, unroll=4)


def thermal(arrive, power, state, wetness, factors):
    n, width, nz = power.shape
    return pl.pallas_call(
        thermal_kernel,
        in_specs=[smem_spec()] + dense(4),
        out_specs=dense(3),
        out_shape=[f32(n, 2 * width, nz), f32(n, width, nz), f32(n, width, nz)],
        compiler_params=limit(20),
        cost_estimate=cost(40 * n * width * nz, 11 * MIB),
        name="thermal",
    )(arrive, power, state, wetness, factors)


def select_kernel(dest, recv_ref, eps_ref, sig_ref, lab_ref, eps_out, sig_out):
    nx, ny, nz = eps_out.shape
    parts = ny // 8

    def body(x, carry):
        for part in range(parts):
            row = dest[0, x * parts + part]
            rows = slice(part * 8, part * 8 + 8)
            product = lab_ref[x, rows, :] == 2
            eps_out[x, rows, :] = jnp.where(product, recv_ref[row, 0:8, :], eps_ref[x, rows, :])
            sig_out[x, rows, :] = jnp.where(product, recv_ref[row, 8:16, :], sig_ref[x, rows, :])
        return carry

    lax.fori_loop(0, nx, body, 0, unroll=2)


def select(dest, recv, eps, sig, label):
    nx, ny, nz = eps.shape
    return pl.pallas_call(
        select_kernel,
        in_specs=[smem_spec()] + dense(4),
        out_specs=dense(2),
        out_shape=[f32(nx, ny, nz), f32(nx, ny, nz)],
        compiler_params=limit(12),
        cost_estimate=cost(4 * nx * ny * nz, 7 * MIB),
        name="select",
    )(dest, recv, eps, sig, label)


def exchange(value):
    return lax.all_to_all(value, ("gx", "gy"), split_axis=0, concat_axis=0, tiled=True)


def borders(layer, rows, by):
    return passed_along(layer, "gx", by), passed_along(rows, "gy", by)


def local(
    efield_vector,
    hfield_vector,
    dielectric_grid,
    sigma_grid,
    substance_label,
    thermal_state,
    wetness_share,
    dielectric_line_choice,
    dielectric_lookup_lines,
    dispatch_keeper_map,
    arrival_position_map,
):
    efield, hfield = efield_vector, hfield_vector
    e_fix, h_fix = (), ()
    layer, rows = first_halo(efield)
    for step in range(2):
        gx, gy = borders(layer, rows, -1)
        hfield, layer, rows = h_update(efield, e_fix, hfield, h_fix)
        h_fix = h_border(layer, rows, gx, gy)
        gx, gy = borders(*h_fix, 1)
        final = step == 1
        efield, layer, rows, *power = e_update(
            efield, e_fix, hfield, h_fix, dielectric_grid, sigma_grid, final
        )
        if final:
            power, *e_fix = power_border(dispatch_keeper_map, power[0], layer, rows, gx, gy)
        else:
            e_fix = layer, rows = e_border(layer, rows, gx, gy)
    arrived = exchange(power)
    factors = lookup(dielectric_lookup_lines, dielectric_line_choice)
    final_efield, final_hfield = flush(efield, e_fix, hfield, h_fix)
    outgoing, warmth, moisture = thermal(
        arrival_position_map, arrived, thermal_state, wetness_share, factors
    )
    returned = exchange(outgoing)
    dielectric_result, sigma_result = select(
        dispatch_keeper_map, returned, dielectric_grid, sigma_grid, substance_label
    )
    return final_efield, final_hfield, dielectric_result, sigma_result, warmth, moisture


def solution(mesh):
    in_specs = (
        P(None, "gx", "gy", None),
        P(None, "gx", "gy", None),
        P("gx", "gy", None),
        P("gx", "gy", None),
        P("gx", "gy", None),
        P(("gx", "gy"), None, None),
        P(("gx", "gy"), None, None),
        P(("gx", "gy"), None, None),
        P(),
        P(("gx", "gy"), None),
        P(("gx", "gy"), None),
    )
    out_specs = (
        P(None, "gx", "gy", None),
        P(None, "gx", "gy", None),
        P("gx", "gy", None),
        P("gx", "gy", None),
        P(("gx", "gy"), None, None),
        P(("gx", "gy"), None, None),
    )
    return jax.shard_map(local, mesh=mesh, in_specs=in_specs, out_specs=out_specs, check_vma=False)
```

time: 163 us -> 131 us (0.80)
  other arithmetic: 46 us -> 0 us
  Pallas kernels: 0 us -> 30.2 us
  local copies, waits for them, and re-layouts: 29.5 us -> 19.2 us
  starting transfers between devices: 49 us -> 42.7 us
    pallas_call x0 -> x13, Pallas kernels: none -> 30.2 us  [the longest x2 6.19 us: e_update(): pl.pallas_call(functools.partial(e_kernel, bool(e_fix), final), in_specs=...]
    unnamed x30 -> x40, local copies, waits for them, and re-layouts: 1.12 us -> 19.2 us
    gather x6 -> x0, local copies, waits for them, and re-layouts: 15.1 us -> none  [the longest x1 2.86 us: local(): cond_rows = sigma_refreshed[slots_here]]
    sub x3 -> x0, other arithmetic: 11.8 us -> none  [the longest x1 5.23 us: local(): mag_y - TIME_STEP * (forward_diff(elec_x, zero_z, 2) - forward_diff(elec_...]
    slice x28 -> x0, local copies, waits for them, and re-layouts: 10.5 us -> none  [the longest x11 7.32 us: forward_diff(): lax.slice_in_dim(values, 1, extent, axis=along)]
    reduce_sum x1 -> x0, other arithmetic: 10 us -> none  [lookup(): jnp.sum(jnp.where(matches, dielectric_lookup_lines[column][:, None, None,...]
    add x4 -> x0, other arithmetic: 7.3 us -> none  [the longest x1 3.03 us: thermal_wetness_advance(): 1.0 + lookup_factors[0] + 4.0 * lookup_factors[1] * wetness_refreshed]
    all_to_all x3 -> x2, starting transfers between devices: 26.4 us -> 19.8 us  [exchange(): lax.all_to_all(value, ('gx', 'gy'), split_axis=0, concat_axis=0, tiled=True)]
  transfers between devices with their start and end apart: 11 -> 10, of which waited for: 7 -> 4; matrix products, arithmetic and copies ran while one was open for 25% -> 0% of each run, Pallas kernels for 0% -> 15%
where the time goes in v1:
time: 131 us
  starting transfers between devices  42.7 us (33%)
  waiting for transfers between devices  37.4 us (29%)
  Pallas kernels  30.2 us (23%)
  local copies, waits for them, and re-layouts  19.2 us (15%)
    all_to_all x2, waiting for transfers between devices, exchange(): lax.all_to_all(value, ('gx', 'gy'), split_axis=0, concat_axis=0, tiled=True)  36.1 us
    ppermute x8, starting transfers between devices, passed_along(): return lax.ppermute(value, axis, pairs)  22.9 us
    all_to_all x2, starting transfers between devices, exchange(): lax.all_to_all(value, ('gx', 'gy'), split_axis=0, concat_axis=0, tiled=True)  19.8 us
    unnamed x40, local copies, waits for them, and re-layouts  19.2 us
    pallas_call x2, Pallas kernels, e_update(): pl.pallas_call(functools.partial(e_kernel, bool(e_fix), final), in_specs=...  6.19 us
    pallas_call x1, Pallas kernels, thermal(): pl.pallas_call(thermal_kernel, in_specs=[smem_spec()] + dense(4), out_spe...  6 us
    pallas_call x2, Pallas kernels, h_update(): pl.pallas_call(functools.partial(h_kernel, bool(e_fix)), in_specs=dense(l...  5.79 us
    pallas_call x1, Pallas kernels, lookup(): pl.pallas_call(lookup_kernel, in_specs=[smem_spec(), vmem_spec()], out_sp...  4.81 us
  transfers between devices with their start and end apart: 10, of which 4 were waited for; matrix products, arithmetic and copies ran while one was open for 0% of the time, Pallas kernels for 15%

profile of v1, /device:TPU:1, one launch (start us, length us, event | category | flops | bytes accessed | tf_op | source)
XLA Modules:
  0.0 130.5 jit_solution(14263561389758964351)
XLA Ops:
  0.6 1.9 %copy-done = f32[3,32,32,256]{3,2,1,0:T(8,128)S(1)} copy-done((f32[3,32,32,256]{3,2,1,0:T(8,128)S(1)}, f32[3,32,32,256]{3,2,1,0:T(8,128)}, u32[]{:S(2)}) %copy-start) | copy-done | bytes 3145752
  2.5 0.1 halo.1
  2.6 1.6 %collective-permute-start = (f32[2,32,256]{2,1,0:T(8,128)S(1)}, f32[2,32,256]{2,1,0:T(8,128)S(1)}, u32[]{:S(2)}, u32[]{:S(2)}) collective-permute-start(f32[2,32,256]{2,1,0:T(8,128)S(1)} %get-tuple-element.40), channel_id=1, source_target_pairs={{8,0},{16,8},{24,16},{32,24},{40,32},{48,40},{56,48},{64,56},{72,6... | collective-permute-start | bytes 196616 | tf_op jit(solution)/shard_map/ppermute | solution.py:17
  4.2 0.0 copy-start.4
  4.2 0.0 copy-start.6
  4.2 3.5 %collective-permute-start.1 = (f32[2,32,256]{2,1,0:T(8,128)S(1)}, f32[2,32,256]{2,1,0:T(8,128)S(1)}, u32[]{:S(2)}, u32[]{:S(2)}) collective-permute-start(f32[2,32,256]{2,1,0:T(8,128)S(1)} %get-tuple-element.41), channel_id=1, source_target_pairs={{1,0},{2,1},{3,2},{4,3},{5,4},{6,5},{7,6},{9,8},{10,9},{11,10},{12... | collective-permute-start | bytes 196616 | tf_op jit(solution)/shard_map/ppermute | solution.py:17
  7.7 2.9 %hstep.2 = (f32[3,32,32,256]{3,2,1,0:T(8,128)S(1)}, f32[2,32,256]{2,1,0:T(8,128)S(1)}, f32[2,32,256]{2,1,0:T(8,128)S(1)}) custom-call(f32[3,32,32,256]{3,2,1,0:T(8,128)S(1)} %copy-done.1, f32[3,32,32,256]{3,2,1,0:T(8,128)S(1)} %copy-done.8), custom_call_target="tpu_custom_call" | custom-call | flops 10485760 | bytes 9437184 | tf_op jit(solution)/shard_map/hstep/pallas_call | solution.py:158
  10.6 0.0 collective-permute-done.gx_ref
  10.6 0.6 collective-permute-done.1.gy_ref
  11.2 4.3 %collective-permute-start.2 = (f32[2,32,256]{2,1,0:T(8,128)S(1)}, f32[2,32,256]{2,1,0:T(8,128)S(1)}, u32[]{:S(2)}, u32[]{:S(2)}) collective-permute-start(f32[2,32,256]{2,1,0:T(8,128)S(1)} %get-tuple-element.42.refs_2_.refs_4_), channel_id=1, source_target_pairs={{0,8},{8,16},{16,24},{24,32},{32,40},{40,48},{48,56},{56,64},{64,7... | collective-permute-start | bytes 196616 | tf_op jit(solution)/shard_map/ppermute | solution.py:17
  15.5 3.2 %collective-permute-start.3 = (f32[2,32,256]{2,1,0:T(8,128)S(1)}, f32[2,32,256]{2,1,0:T(8,128)S(1)}, u32[]{:S(2)}, u32[]{:S(2)}) collective-permute-start(f32[2,32,256]{2,1,0:T(8,128)S(1)} %get-tuple-element.43.refs_3_.refs_5_), channel_id=1, source_target_pairs={{0,1},{1,2},{2,3},{3,4},{4,5},{5,6},{6,7},{8,9},{9,10},{10,11},{11... | collective-permute-start | bytes 196616 | tf_op jit(solution)/shard_map/ppermute | solution.py:17
  18.7 2.9 %estep.2 = (f32[3,32,32,256]{3,2,1,0:T(8,128)S(1)}, f32[3,32,256]{2,1,0:T(8,128)S(1)}, f32[3,32,256]{2,1,0:T(8,128)S(1)}) custom-call(f32[3,32,32,256]{3,2,1,0:T(8,128)S(1)} %copy-done.1, f32[3,32,32,256]{3,2,1,0:T(8,128)S(1)} %get-tuple-element.37.refs_1_.refs_3_, f32[2,32,256]{2,1,0:T(8,128)S(1)} %get-tuple-element.42.refs_2_.refs_4_, ...), custom_call_target="tpu_custom_call" | custom-call | flops 15728640 | bytes 11534336 | tf_op jit(solution)/shard_map/estep/pallas_call | solution.py:253
  21.7 0.0 collective-permute-done.2.gx_ref
  21.7 1.3 collective-permute-start.4
  23.0 1.9 %collective-permute-start.5 = (f32[2,32,256]{2,1,0:T(8,128)S(1)}, f32[2,32,256]{2,1,0:T(8,128)S(1)}, u32[]{:S(2)}, u32[]{:S(2)}) collective-permute-start(f32[2,32,256]{2,1,0:T(8,128)S(1)} %get-tuple-element.48.refs_2_), channel_id=1, source_target_pairs={{1,0},{2,1},{3,2},{4,3},{5,4},{6,5},{7,6},{9,8},{10,9},{11,10},{12... | collective-permute-start | bytes 196616 | tf_op jit(solution)/shard_map/ppermute | solution.py:17
  24.9 2.9 %hstep.3 = (f32[3,32,32,256]{3,2,1,0:T(8,128)S(1)}, f32[2,32,256]{2,1,0:T(8,128)S(1)}, f32[2,32,256]{2,1,0:T(8,128)S(1)}) custom-call(f32[3,32,32,256]{3,2,1,0:T(8,128)S(1)} %get-tuple-element.44.refs_0_, f32[2,32,256]{2,1,0:T(8,128)S(1)} %get-tuple-element.47.refs_1_, f32[2,32,256]{2,1,0:T(8,128)S(1)} %get-tuple-element.48.refs_2_, ...), custom_call_target="tpu_custom_call" | custom-call | flops 10485760 | bytes 9437184 | tf_op jit(solution)/shard_map/hstep/pallas_call | solution.py:158
  27.9 0.0 collective-permute-done.4.gx_ref
  27.9 0.7 collective-permute-done.5.gy_ref
  28.6 4.0 %collective-permute-start.6 = (f32[2,32,256]{2,1,0:T(8,128)S(1)}, f32[2,32,256]{2,1,0:T(8,128)S(1)}, u32[]{:S(2)}, u32[]{:S(2)}) collective-permute-start(f32[2,32,256]{2,1,0:T(8,128)S(1)} %get-tuple-element.52.refs_4_.hl_ref), channel_id=1, source_target_pairs={{0,8},{8,16},{16,24},{24,32},{32,40},{40,48},{48,56},{56,64},{64,7... | collective-permute-start | bytes 196616 | tf_op jit(solution)/shard_map/ppermute | solution.py:17
  32.6 3.2 %collective-permute-start.7 = (f32[2,32,256]{2,1,0:T(8,128)S(1)}, f32[2,32,256]{2,1,0:T(8,128)S(1)}, u32[]{:S(2)}, u32[]{:S(2)}) collective-permute-start(f32[2,32,256]{2,1,0:T(8,128)S(1)} %get-tuple-element.53.refs_5_.hr_ref), channel_id=1, source_target_pairs={{0,1},{1,2},{2,3},{3,4},{4,5},{5,6},{6,7},{8,9},{9,10},{10,11},{11... | collective-permute-start | bytes 196616 | tf_op jit(solution)/shard_map/ppermute | solution.py:17
  35.8 0.0 copy-start.18
  35.9 3.3 %estep.3 = (f32[3,32,32,256]{3,2,1,0:T(8,128)S(1)}, f32[6,32,256]{2,1,0:T(8,128)S(1)}, f32[6,32,256]{2,1,0:T(8,128)S(1)}, f32[32,32,256]{2,1,0:T(8,128)S(1)}) custom-call(f32[3,32,32,256]{3,2,1,0:T(8,128)S(1)} %get-tuple-element.44.refs_0_, f32[2,32,256]{2,1,0:T(8,128)S(1)} %get-tuple-element.47.refs_1_, f32[2,32,256]{2,1,0:T(8,128)S(1)} %get-tuple-element.48.refs_2_, ...), custom_call_target="tpu_custom_call" | custom-call | flops 15728640 | bytes 11534336 | tf_op jit(solution)/shard_map/estep/pallas_call | solution.py:253
  39.1 0.0 copy-start.9
  39.1 1.7 %copy-done.9 = f32[3,32,32,256]{3,2,1,0:T(8,128)} copy-done((f32[3,32,32,256]{3,2,1,0:T(8,128)}, f32[3,32,32,256]{3,2,1,0:T(8,128)S(1)}, u32[]{:S(2)}) %copy-start.9) | copy-done | bytes 3145752
  40.8 0.0 collective-permute-done.6.gx_ref
  40.8 0.8 power.1
  41.6 0.0 copy-start.13
  41.6 1.0 copy-done.13
  42.6 14.2 %all-to-all-start = ((f32[128,8,256]{2,1,0:T(8,128)}), f32[128,8,256]{2,1,0:T(8,128)}, u32[]{:S(2)}, u32[]{:S(2)}) async-start(f32[128,8,256]{2,1,0:T(8,128)} %copy-done.13), calls=%async_computation | async-start | bytes 2097152 | tf_op jit(solution)/shard_map/all_to_all | solution.py:451
  56.8 0.0 copy-start.12
  56.8 1.2 copy-done.12
  58.0 4.8 %lookup.1.f_ref = f32[4,128,8,256]{3,2,1,0:T(8,128)S(1)} custom-call(f32[4,16]{1,0:T(4,128)S(1)} %copy-done.17, s32[128,8,256]{2,1,0:T(8,128)S(1)} %copy-done.12), custom_call_target="tpu_custom_call" | custom-call | flops 20971520 | bytes 5242880 | tf_op jit(solution)/shard_map/lookup/pallas_call | solution.py:375
  62.8 2.0 %copy-done.2 = f32[4,128,8,256]{3,2,1,0:T(8,128)} copy-done((f32[4,128,8,256]{3,2,1,0:T(8,128)}, f32[4,128,8,256]{3,2,1,0:T(8,128)S(1)}, u32[]{:S(2)}) %copy-start.2) | copy-done | bytes 4194328
  64.8 10.9 %all-to-all-done.p_ref = f32[128,8,256]{2,1,0:T(8,128)} async-done(((f32[128,8,256]{2,1,0:T(8,128)}), f32[128,8,256]{2,1,0:T(8,128)}, u32[]{:S(2)}, u32[]{:S(2)}) %all-to-all-start) | async-done | bytes 1048608 | tf_op jit(solution)/shard_map/all_to_all | solution.py:451
  75.7 2.2 %copy-done.3 = f32[4,128,8,256]{3,2,1,0:T(8,128)S(1)} copy-done((f32[4,128,8,256]{3,2,1,0:T(8,128)S(1)}, f32[4,128,8,256]{3,2,1,0:T(8,128)}, u32[]{:S(2)}) %copy-start.3) | copy-done | bytes 4194328
  77.9 1.2 copy-done.15
  79.1 1.2 copy-done.16
  80.3 6.0 %thermal.1 = (f32[128,16,256]{2,1,0:T(8,128)S(1)}, f32[128,8,256]{2,1,0:T(8,128)}, f32[128,8,256]{2,1,0:T(8,128)}) custom-call(s32[1,128]{1,0:T(1,128)S(1)} %copy-done.19, f32[128,8,256]{2,1,0:T(8,128)} %all-to-all-done.p_ref, f32[128,8,256]{2,1,0:T(8,128)S(1)} %copy-done.15, f32[128,8,256]{2,1,0:T(8,128)S(1)} %copy-done.16, f32[4,128,8,256]{3,2,1,0:T(8,128)S(1)} %copy-done.3), custom_call_target="tpu_custom_call" | custom-call | flops 10485760 | bytes 11534336 | tf_op jit(solution)/shard_map/thermal/pallas_call | solution.py:410
  86.3 1.3 %copy-done.11 = f32[128,16,256]{2,1,0:T(8,128)} copy-done((f32[128,16,256]{2,1,0:T(8,128)}, f32[128,16,256]{2,1,0:T(8,128)S(1)}, u32[]{:S(2)}) %copy-start.11) | copy-done | bytes 2097176
  87.7 5.7 %all-to-all-start.1 = ((f32[128,16,256]{2,1,0:T(8,128)}), f32[128,16,256]{2,1,0:T(8,128)}, u32[]{:S(2)}, u32[]{:S(2)}) async-start(f32[128,16,256]{2,1,0:T(8,128)} %copy-done.11), calls=%async_computation.1 | async-start | bytes 4194304 | tf_op jit(solution)/shard_map/all_to_all | solution.py:451
  93.3 0.0 copy-start.10
  93.3 1.9 %copy-done.10 = f32[3,32,32,256]{3,2,1,0:T(8,128)S(1)} copy-done((f32[3,32,32,256]{3,2,1,0:T(8,128)S(1)}, f32[3,32,32,256]{3,2,1,0:T(8,128)}, u32[]{:S(2)}) %copy-start.10) | copy-done | bytes 3145752
  95.2 3.2 %flush.1 = (f32[3,32,32,256]{3,2,1,0:T(8,128)}, f32[3,32,32,256]{3,2,1,0:T(8,128)}) custom-call(f32[3,32,32,256]{3,2,1,0:T(8,128)S(1)} %copy-done.10, f32[2,32,256]{2,1,0:T(8,128)S(1)} %get-tuple-element.58.el_ref, f32[2,32,256]{2,1,0:T(8,128)S(1)} %get-tuple-element.59.er_ref, f32[3,32,32,256]{3,2,1,0:T(8,128)S(1)} %get-tuple-element.49.refs_3_.h_ref, ...), custom_call_target="tpu_custom_call" | custom-call | flops 786432 | bytes 12582912 | tf_op jit(solution)/shard_map/flush/pallas_call | solution.py:343
  98.4 25.2 %all-to-all-done.1.recv_ref = f32[128,16,256]{2,1,0:T(8,128)} async-done(((f32[128,16,256]{2,1,0:T(8,128)}), f32[128,16,256]{2,1,0:T(8,128)}, u32[]{:S(2)}, u32[]{:S(2)}) %all-to-all-start.1) | async-done | bytes 2097184 | tf_op jit(solution)/shard_map/all_to_all | solution.py:451
  123.6 1.2 copy-done.5
  124.9 1.2 copy-done.7
  126.1 1.2 copy-done.14
  127.3 3.2 %select.1 = (f32[32,32,256]{2,1,0:T(8,128)}, f32[32,32,256]{2,1,0:T(8,128)}) custom-call(s32[1,128]{1,0:T(1,128)S(1)} %copy-done.18, f32[128,16,256]{2,1,0:T(8,128)} %all-to-all-done.1.recv_ref, f32[32,32,256]{2,1,0:T(8,128)S(1)} %copy-done.5, f32[32,32,256]{2,1,0:T(8,128)S(1)} %copy-done.7, s32[32,32,256]{2,1,0:T(8,128)S(1)} %copy-done.14), custom_call_target="tpu_custom_call" | custom-call | flops 1048576 | bytes 7340032 | tf_op jit(solution)/shard_map/select/pallas_call | solution.py:439
  (25 shorter events, 0.1 us)
Async XLA Ops:
  0.6 1.9 %copy-start = (f32[3,32,32,256]{3,2,1,0:T(8,128)S(1)}, f32[3,32,32,256]{3,2,1,0:T(8,128)}, u32[]{:S(2)}) copy-start(f32[3,32,32,256]{3,2,1,0:T(8,128)} %refs_0_.3) | copy-start | bytes 9437188
  2.5 5.1 %copy-start.1 = (f32[3,32,32,256]{3,2,1,0:T(8,128)S(1)}, f32[3,32,32,256]{3,2,1,0:T(8,128)}, u32[]{:S(2)}) copy-start(f32[3,32,32,256]{3,2,1,0:T(8,128)} %refs_0_.3) | copy-start | bytes 9437188
  2.5 5.2 %copy-start.8 = (f32[3,32,32,256]{3,2,1,0:T(8,128)S(1)}, f32[3,32,32,256]{3,2,1,0:T(8,128)}, u32[]{:S(2)}) copy-start(f32[3,32,32,256]{3,2,1,0:T(8,128)} %refs_1_.1) | copy-start | bytes 9437188
  2.6 8.0 %collective-permute-start = (f32[2,32,256]{2,1,0:T(8,128)S(1)}, f32[2,32,256]{2,1,0:T(8,128)S(1)}, u32[]{:S(2)}, u32[]{:S(2)}) collective-permute-start(f32[2,32,256]{2,1,0:T(8,128)S(1)} %get-tuple-element.40), channel_id=1, source_target_pairs={{8,0},{16,8},{24,16},{32,24},{40,32},{48,40},{56,48},{64,56},{72,6... | collective-permute-start | bytes 196616 | tf_op jit(solution)/shard_map/ppermute | solution.py:17
  4.2 14.5 %copy-start.4 = (f32[32,32,256]{2,1,0:T(8,128)S(1)}, f32[32,32,256]{2,1,0:T(8,128)}, u32[]{:S(2)}) copy-start(f32[32,32,256]{2,1,0:T(8,128)} %eps_ref.1) | copy-start | bytes 3145732
  4.2 14.5 %copy-start.6 = (f32[32,32,256]{2,1,0:T(8,128)S(1)}, f32[32,32,256]{2,1,0:T(8,128)}, u32[]{:S(2)}) copy-start(f32[32,32,256]{2,1,0:T(8,128)} %sig_ref.1) | copy-start | bytes 3145732
  4.2 7.0 %collective-permute-start.1 = (f32[2,32,256]{2,1,0:T(8,128)S(1)}, f32[2,32,256]{2,1,0:T(8,128)S(1)}, u32[]{:S(2)}, u32[]{:S(2)}) collective-permute-start(f32[2,32,256]{2,1,0:T(8,128)S(1)} %get-tuple-element.41), channel_id=1, source_target_pairs={{1,0},{2,1},{3,2},{4,3},{5,4},{6,5},{7,6},{9,8},{10,9},{11,10},{12... | collective-permute-start | bytes 196616 | tf_op jit(solution)/shard_map/ppermute | solution.py:17
  11.2 10.4 %collective-permute-start.2 = (f32[2,32,256]{2,1,0:T(8,128)S(1)}, f32[2,32,256]{2,1,0:T(8,128)S(1)}, u32[]{:S(2)}, u32[]{:S(2)}) collective-permute-start(f32[2,32,256]{2,1,0:T(8,128)S(1)} %get-tuple-element.42.refs_2_.refs_4_), channel_id=1, source_target_pairs={{0,8},{8,16},{16,24},{24,32},{32,40},{40,48},{48,56},{56,64},{64,7... | collective-permute-start | bytes 196616 | tf_op jit(solution)/shard_map/ppermute | solution.py:17
  15.5 6.2 %collective-permute-start.3 = (f32[2,32,256]{2,1,0:T(8,128)S(1)}, f32[2,32,256]{2,1,0:T(8,128)S(1)}, u32[]{:S(2)}, u32[]{:S(2)}) collective-permute-start(f32[2,32,256]{2,1,0:T(8,128)S(1)} %get-tuple-element.43.refs_3_.refs_5_), channel_id=1, source_target_pairs={{0,1},{1,2},{2,3},{3,4},{4,5},{5,6},{6,7},{8,9},{9,10},{10,11},{11... | collective-permute-start | bytes 196616 | tf_op jit(solution)/shard_map/ppermute | solution.py:17
  21.7 6.2 %collective-permute-start.4 = (f32[2,32,256]{2,1,0:T(8,128)S(1)}, f32[2,32,256]{2,1,0:T(8,128)S(1)}, u32[]{:S(2)}, u32[]{:S(2)}) collective-permute-start(f32[2,32,256]{2,1,0:T(8,128)S(1)} %get-tuple-element.47.refs_1_), channel_id=1, source_target_pairs={{8,0},{16,8},{24,16},{32,24},{40,32},{48,40},{56,48},{64,56},{72,6... | collective-permute-start | bytes 196616 | tf_op jit(solution)/shard_map/ppermute | solution.py:17
  23.0 5.6 %collective-permute-start.5 = (f32[2,32,256]{2,1,0:T(8,128)S(1)}, f32[2,32,256]{2,1,0:T(8,128)S(1)}, u32[]{:S(2)}, u32[]{:S(2)}) collective-permute-start(f32[2,32,256]{2,1,0:T(8,128)S(1)} %get-tuple-element.48.refs_2_), channel_id=1, source_target_pairs={{1,0},{2,1},{3,2},{4,3},{5,4},{6,5},{7,6},{9,8},{10,9},{11,10},{12... | collective-permute-start | bytes 196616 | tf_op jit(solution)/shard_map/ppermute | solution.py:17
  28.6 12.2 %collective-permute-start.6 = (f32[2,32,256]{2,1,0:T(8,128)S(1)}, f32[2,32,256]{2,1,0:T(8,128)S(1)}, u32[]{:S(2)}, u32[]{:S(2)}) collective-permute-start(f32[2,32,256]{2,1,0:T(8,128)S(1)} %get-tuple-element.52.refs_4_.hl_ref), channel_id=1, source_target_pairs={{0,8},{8,16},{16,24},{24,32},{32,40},{40,48},{48,56},{56,64},{64,7... | collective-permute-start | bytes 196616 | tf_op jit(solution)/shard_map/ppermute | solution.py:17
  32.6 8.2 %collective-permute-start.7 = (f32[2,32,256]{2,1,0:T(8,128)S(1)}, f32[2,32,256]{2,1,0:T(8,128)S(1)}, u32[]{:S(2)}, u32[]{:S(2)}) collective-permute-start(f32[2,32,256]{2,1,0:T(8,128)S(1)} %get-tuple-element.53.refs_5_.hr_ref), channel_id=1, source_target_pairs={{0,1},{1,2},{2,3},{3,4},{4,5},{5,6},{6,7},{8,9},{9,10},{10,11},{11... | collective-permute-start | bytes 196616 | tf_op jit(solution)/shard_map/ppermute | solution.py:17
  35.8 5.0 %copy-start.18 = (s32[1,128]{1,0:T(1,128)S(1)}, s32[1,128]{1,0:T(1,128)}, u32[]{:S(2)}) copy-start(s32[1,128]{1,0:T(1,128)} %dest.3) | copy-start | bytes 1540
  39.1 1.7 %copy-start.9 = (f32[3,32,32,256]{3,2,1,0:T(8,128)}, f32[3,32,32,256]{3,2,1,0:T(8,128)S(1)}, u32[]{:S(2)}) copy-start(f32[3,32,32,256]{3,2,1,0:T(8,128)S(1)} %get-tuple-element.54.e_ref) | copy-start | bytes 9437188
  40.8 16.0 %copy-start.17 = (f32[4,16]{1,0:T(4,128)S(1)}, f32[4,16]{1,0:T(4,128)}, u32[]{:S(2)}) copy-start(f32[4,16]{1,0:T(4,128)} %lines.1) | copy-start | bytes 772
  41.6 1.0 copy-start.13
  42.6 33.1 %all-to-all-start = ((f32[128,8,256]{2,1,0:T(8,128)}), f32[128,8,256]{2,1,0:T(8,128)}, u32[]{:S(2)}, u32[]{:S(2)}) async-start(f32[128,8,256]{2,1,0:T(8,128)} %copy-done.13), calls=%async_computation | async-start | bytes 2097152 | tf_op jit(solution)/shard_map/all_to_all | solution.py:451
  56.8 1.2 copy-start.12
  58.0 17.7 %copy-start.19 = (s32[1,128]{1,0:T(1,128)S(1)}, s32[1,128]{1,0:T(1,128)}, u32[]{:S(2)}) copy-start(s32[1,128]{1,0:T(1,128)} %arrive.1) | copy-start | bytes 1540
  62.8 2.0 %copy-start.2 = (f32[4,128,8,256]{3,2,1,0:T(8,128)}, f32[4,128,8,256]{3,2,1,0:T(8,128)S(1)}, u32[]{:S(2)}) copy-start(f32[4,128,8,256]{3,2,1,0:T(8,128)S(1)} %lookup.1.f_ref) | copy-start | bytes 12582916
  75.7 2.2 %copy-start.3 = (f32[4,128,8,256]{3,2,1,0:T(8,128)S(1)}, f32[4,128,8,256]{3,2,1,0:T(8,128)}, u32[]{:S(2)}) copy-start(f32[4,128,8,256]{3,2,1,0:T(8,128)} %copy-done.2) | copy-start | bytes 12582916
  77.9 1.2 copy-start.15
  79.1 1.2 copy-start.16
  86.3 1.3 %copy-start.11 = (f32[128,16,256]{2,1,0:T(8,128)}, f32[128,16,256]{2,1,0:T(8,128)S(1)}, u32[]{:S(2)}) copy-start(f32[128,16,256]{2,1,0:T(8,128)S(1)} %get-tuple-element.63) | copy-start | bytes 6291460
  87.7 36.0 %all-to-all-start.1 = ((f32[128,16,256]{2,1,0:T(8,128)}), f32[128,16,256]{2,1,0:T(8,128)}, u32[]{:S(2)}, u32[]{:S(2)}) async-start(f32[128,16,256]{2,1,0:T(8,128)} %copy-done.11), calls=%async_computation.1 | async-start | bytes 4194304 | tf_op jit(solution)/shard_map/all_to_all | solution.py:451
  93.3 1.9 %copy-start.10 = (f32[3,32,32,256]{3,2,1,0:T(8,128)S(1)}, f32[3,32,32,256]{3,2,1,0:T(8,128)}, u32[]{:S(2)}) copy-start(f32[3,32,32,256]{3,2,1,0:T(8,128)} %copy-done.9) | copy-start | bytes 9437188
  123.6 1.2 copy-start.5
  124.9 1.2 copy-start.7
  126.1 1.2 copy-start.14

commit v2 on v1

--- a/solution.py
+++ b/solution.py
@@ -9,6 +9,9 @@
 
 DT = 0.5
 MIB = 1 << 20
+GROUP = 10
+FAR = 5
+THERMAL_MIB = 62
 
 
 def passed_along(value, axis, by):
@@ -35,6 +38,32 @@
 
 def limit(mib):
     return pltpu.CompilerParams(vmem_limit_bytes=mib * MIB)
+
+
+def hbm_spec():
+    return pl.BlockSpec(memory_space=pltpu.HBM)
+
+
+def part_of(ref, axis, chunk, chunks):
+    size = ref.shape[axis] // chunks
+    where = [slice(None)] * axis + [pl.ds(chunk * size, size)]
+    return ref.at[tuple(where)]
+
+
+def copies(sources, targets, sem, chunks, axis=0):
+    return [
+        [
+            pltpu.make_async_copy(
+                part_of(source, axis, chunk, chunks), part_of(target, axis, chunk, chunks), sem.at[k, chunk]
+            )
+            for k, (source, target) in enumerate(zip(sources, targets))
+        ]
+        for chunk in range(chunks)
+    ]
+
+
+def hbm(*shape):
+    return pltpu.HBM(shape, jnp.float32)
 
 
 def cost(ops, nbytes):
@@ -119,9 +148,28 @@
     return hx, hy, hz
 
 
+def parts_of_copy(source, target, sem):
+    return [pltpu.make_async_copy(source.at[k], target.at[k], sem.at[k]) for k in range(source.shape[0])]
+
+
+def walk(slab, nx):
+    groups = (nx - 2) // GROUP
+    slab(0, True, False)
+
+    def body(g, carry):
+        for k in range(GROUP):
+            slab(1 + g * GROUP + k, False, False)
+        return carry
+
+    lax.fori_loop(0, groups, body, 0)
+    for x in range(1 + groups * GROUP, nx - 1):
+        slab(x, False, False)
+    slab(nx - 1, False, True)
+
+
 def h_kernel(fixed, *refs):
     if fixed:
-        e_ref, el_ref, er_ref, h_ref, hl_ref, hr_ref, out_ref, layer_ref, rows_ref = refs
+        e_ref, el_ref, er_ref, h_ref, hl_ref, hr_ref, out_ref, layer_ref, rows_ref, out_hbm, sem = refs
     else:
         e_ref, h_ref, out_ref, layer_ref, rows_ref = refs
         el_ref = er_ref = hl_ref = hr_ref = None
@@ -147,19 +195,25 @@
             layer_ref[0] = hy
             layer_ref[1] = hz
 
-    slab(0, True, False)
-    lax.fori_loop(1, nx - 1, lambda x, c: (slab(x, False, False), c)[1], 0)
-    slab(nx - 1, False, True)
+    walk(slab, nx)
+    if fixed:
+        moves = parts_of_copy(out_ref, out_hbm, sem)
+        for move in moves:
+            move.start()
+        for move in moves:
+            move.wait()
 
 
 def h_update(efield, e_fix, hfield, h_fix):
     _, nx, ny, nz = efield.shape
     args = [efield, *e_fix, hfield, *h_fix]
+    outs = [f32(3, nx, ny, nz), f32(2, ny, nz), f32(2, nx, nz)]
     return pl.pallas_call(
         functools.partial(h_kernel, bool(e_fix)),
         in_specs=dense(len(args)),
-        out_specs=dense(3),
-        out_shape=[f32(3, nx, ny, nz), f32(2, ny, nz), f32(2, nx, nz)],
+        out_specs=dense(3) + [hbm_spec()] * bool(e_fix),
+        out_shape=outs + [hbm(3, nx, ny, nz)] * bool(e_fix),
+        scratch_shapes=[pltpu.SemaphoreType.DMA((3,))] * bool(e_fix),
         compiler_params=limit(16),
         cost_estimate=cost(40 * nx * ny * nz, 9 * MIB),
         name="hstep",
@@ -238,9 +292,7 @@
                 layer_ref[4] = before
                 layer_ref[5] = half
 
-    slab(0, True, False)
-    lax.fori_loop(1, nx - 1, lambda x, c: (slab(x, False, False), c)[1], 0)
-    slab(nx - 1, False, True)
+    walk(slab, nx)
 
 
 def e_update(efield, e_fix, hfield, h_fix, eps, sig, final):
@@ -255,7 +307,7 @@
         in_specs=dense(len(args)),
         out_specs=dense(len(outs)),
         out_shape=outs,
-        compiler_params=limit(20),
+        compiler_params=limit(16),
         cost_estimate=cost(60 * nx * ny * nz, 11 * MIB),
         name="estep",
     )(*args)
@@ -287,7 +339,10 @@
     )(layer, rows, gx, gy)
 
 
-def power_kernel(dest, p_ref, layer_ref, rows_ref, gx_ref, gy_ref, out_ref, layer_out, rows_out, scratch):
+def power_kernel(dest, e_ref, p_ref, layer_ref, rows_ref, gx_ref, gy_ref, out_hbm, layer_out, rows_out, e_hbm, scratch, out_ref, sem, e_sem):
+    moves = parts_of_copy(e_ref, e_hbm, e_sem)
+    for move in moves:
+        move.start()
     nx, ny, nz = p_ref.shape
     parts = ny // 8
     ey_layer, ez_layer, ex_rows, ez_rows = e_border_values(layer_ref, rows_ref, gx_ref, gy_ref)
@@ -311,20 +366,29 @@
         return carry
 
     lax.fori_loop(1, nx, body, 0, unroll=2)
-
-
-def power_border(dest, power, layer, rows, gx, gy):
+    moves.append(pltpu.make_async_copy(out_ref, out_hbm, sem))
+    moves[-1].start()
+    for move in moves:
+        move.wait()
+
+
+def power_border(dest, efield, power, layer, rows, gx, gy):
     nx, ny, nz = power.shape
     return pl.pallas_call(
         power_kernel,
-        in_specs=[smem_spec()] + dense(5),
-        out_specs=dense(3),
-        out_shape=[f32(nx * ny // 8, 8, nz), f32(*gx.shape), f32(*gy.shape)],
-        scratch_shapes=[pltpu.VMEM((nx, nz), jnp.float32)],
+        in_specs=[smem_spec()] + dense(6),
+        out_specs=[hbm_spec()] + dense(2) + [hbm_spec()],
+        out_shape=[hbm(nx * ny // 8, 8, nz), f32(*gx.shape), f32(*gy.shape), hbm(*efield.shape)],
+        scratch_shapes=[
+            pltpu.VMEM((nx, nz), jnp.float32),
+            pltpu.VMEM((nx * ny // 8, 8, nz), jnp.float32),
+            pltpu.SemaphoreType.DMA(()),
+            pltpu.SemaphoreType.DMA((3,)),
+        ],
         compiler_params=limit(8),
-        cost_estimate=cost(4 * nx * ny * nz, 2 * MIB),
+        cost_estimate=cost(4 * nx * ny * nz, 8 * MIB),
         name="power",
-    )(dest, power, layer, rows, gx, gy)
+    )(dest, efield, power, layer, rows, gx, gy)
 
 
 def flush_kernel(e_ref, el_ref, er_ref, h_ref, hl_ref, hr_ref, e_out, h_out):
@@ -351,39 +415,112 @@
     )(efield, *e_fix, hfield, *h_fix)
 
 
-def lookup_kernel(lines, choice_ref, out_ref):
+def pack_kernel(arrive, lines, t_ref, w_ref, c_ref, *out_refs):
+    rows = out_refs[0].shape[0]
+    width, nz = t_ref.shape[1:]
     levels = lines.shape[1]
-
-    def body(j, carry):
-        choice = choice_ref[j]
+    step = pl.program_id(0)
+    lane = lax.broadcasted_iota(jnp.int32, (width, nz), 1)
+
+    def body(r, carry):
+        slot = arrive[0, step * rows + r]
+        state = t_ref[slot]
+        choice = c_ref[slot]
+        above = jnp.where(lane == nz - 1, state, pltpu.roll(state, nz - 1, 1))
+        below = jnp.where(lane == 0, state, pltpu.roll(state, 1, 1))
         factors = [jnp.full(choice.shape, lines[c, 0], jnp.float32) for c in range(4)]
         for level in range(1, levels):
             match = choice == level
             for c in range(4):
                 factors[c] = jnp.where(match, lines[c, level], factors[c])
-        out_ref[0, j] = 1.0 + factors[0]
-        out_ref[1, j] = 4.0 * factors[1]
-        out_ref[2, j] = 0.1 * factors[2]
-        out_ref[3, j] = 0.3 * factors[3]
+        wet = w_ref[slot]
+        values = [
+            state + 0.2 * ((above - state) + (below - state)),
+            1.0 + factors[0],
+            4.0 * factors[1] * wet,
+            0.1 * factors[2],
+            0.3 * factors[3] * wet,
+        ]
+        for k, value in enumerate(values):
+            target, at = (out_refs[0], k) if k < FAR else (out_refs[1], k - FAR)
+            target[r, at * width : (at + 1) * width, :] = value
         return carry
 
-    lax.fori_loop(0, choice_ref.shape[0], body, 0, unroll=2)
-
-
-def lookup(lines, choice):
-    n, width, nz = choice.shape
-    return pl.pallas_call(
-        lookup_kernel,
-        in_specs=[smem_spec(), vmem_spec()],
-        out_specs=vmem_spec(),
-        out_shape=f32(4, n, width, nz),
-        compiler_params=limit(10),
-        cost_estimate=cost(80 * n * width * nz, 5 * MIB),
-        name="lookup",
-    )(lines, choice)
-
-
-def thermal_kernel(arrive, p_ref, t_ref, w_ref, f_ref, send_out, t_out, w_out):
+    lax.fori_loop(0, rows, body, 0, unroll=2)
+
+
+def pack(arrive, lines, state, wetness, choice):
+    n, width, nz = state.shape
+    steps = 4
+    return pl.pallas_call(
+        pack_kernel,
+        grid=(steps,),
+        in_specs=[smem_spec(), smem_spec()] + dense(3),
+        out_specs=[
+            pl.BlockSpec((n // steps, count * width, nz), lambda i: (i, 0, 0))
+            for count in (FAR, 5 - FAR)
+            if count
+        ],
+        out_shape=[hbm(n, FAR * width, nz)] + [f32(n, (5 - FAR) * width, nz)] * (FAR < 5),
+        compiler_params=limit(6),
+        cost_estimate=cost(80 * n * width * nz, 9 * MIB),
+        name="pack",
+    )(arrive, lines, state, wetness, choice)
+
+
+def thermal_kernel(p_hbm, far_hbm, *refs):
+    near_refs, (send_hbm, p_ref, far_ref, send_ref, in_sem, out_sem) = refs[:-6], refs[-6:]
+    n, width, nz = p_ref.shape
+    chunks = in_sem.shape[1]
+    size = n // chunks
+    loads = copies([p_hbm, far_hbm], [p_ref, far_ref], in_sem, chunks)
+    stores = copies([send_ref], [send_hbm], out_sem, chunks)
+    for group in loads:
+        for move in group:
+            move.start()
+
+    def body(s, carry):
+        kept = [far_ref[s, k * width : (k + 1) * width, :] for k in range(FAR)]
+        kept += [near_refs[0][s, k * width : (k + 1) * width, :] for k in range(5 - FAR)]
+        heated = kept[0] + 0.5 * p_ref[s]
+        share = jnp.exp(-2.0 * jnp.maximum(heated - 1.0, 0.0))
+        send_ref[s, 0:width, :] = kept[1] + kept[2] * share
+        send_ref[s, width : 2 * width, :] = kept[3] + kept[4] * share
+        return carry
+
+    for chunk in range(chunks):
+        for move in loads[chunk]:
+            move.wait()
+        lax.fori_loop(chunk * size, (chunk + 1) * size, body, 0, unroll=4)
+        for move in stores[chunk]:
+            move.start()
+    for group in stores:
+        for move in group:
+            move.wait()
+
+
+def thermal(power, far, *near):
+    n, width, nz = power.shape
+    chunks = 8
+    return pl.pallas_call(
+        thermal_kernel,
+        in_specs=[hbm_spec(), hbm_spec()] + dense(len(near)),
+        out_specs=hbm_spec(),
+        out_shape=hbm(n, 2 * width, nz),
+        scratch_shapes=[
+            pltpu.VMEM((n, width, nz), jnp.float32),
+            pltpu.VMEM(far.shape, jnp.float32),
+            pltpu.VMEM((n, 2 * width, nz), jnp.float32),
+            pltpu.SemaphoreType.DMA((2, chunks)),
+            pltpu.SemaphoreType.DMA((1, chunks)),
+        ],
+        compiler_params=limit(THERMAL_MIB),
+        cost_estimate=cost(40 * n * width * nz, 8 * MIB),
+        name="thermal",
+    )(power, far, *near)
+
+
+def heat_kernel(arrive, p_ref, t_ref, w_ref, t_out, w_out):
     n, width, nz = p_ref.shape
     lane = lax.broadcasted_iota(jnp.int32, (width, nz), 1)
 
@@ -395,56 +532,103 @@
         heated = state + 0.2 * ((above - state) + (below - state)) + 0.5 * p_ref[s]
         wet = w_ref[slot]
         gone = wet * (1.0 - jnp.exp(-2.0 * jnp.maximum(heated - 1.0, 0.0)))
-        left = wet - gone
-        w_out[slot] = left
+        w_out[slot] = wet - gone
         t_out[slot] = heated - 0.8 * gone
-        send_out[s, 0:width, :] = f_ref[0, slot] + f_ref[1, slot] * left
-        send_out[s, width : 2 * width, :] = f_ref[2, slot] + f_ref[3, slot] * left
         return carry
 
     lax.fori_loop(0, n, body, 0, unroll=4)
 
 
-def thermal(arrive, power, state, wetness, factors):
+def heat(arrive, power, state, wetness):
     n, width, nz = power.shape
     return pl.pallas_call(
-        thermal_kernel,
-        in_specs=[smem_spec()] + dense(4),
-        out_specs=dense(3),
-        out_shape=[f32(n, 2 * width, nz), f32(n, width, nz), f32(n, width, nz)],
-        compiler_params=limit(20),
-        cost_estimate=cost(40 * n * width * nz, 11 * MIB),
-        name="thermal",
-    )(arrive, power, state, wetness, factors)
-
-
-def select_kernel(dest, recv_ref, eps_ref, sig_ref, lab_ref, eps_out, sig_out):
-    nx, ny, nz = eps_out.shape
+        heat_kernel,
+        in_specs=[smem_spec()] + dense(3),
+        out_specs=dense(2),
+        out_shape=[f32(n, width, nz)] * 2,
+        compiler_params=limit(8),
+        cost_estimate=cost(40 * n * width * nz, 5 * MIB),
+        name="heat",
+    )(arrive, power, state, wetness)
+
+
+def near_kernel(eps_ref, sig_ref, lab_ref, out_ref):
+    out_ref[0] = jnp.where(lab_ref[...] == 2, -1.0, eps_ref[...])
+    out_ref[1] = sig_ref[...]
+
+
+def near(eps, sig, label):
+    nx, ny, nz = eps.shape
+    steps = 4
+    cells = pl.BlockSpec((nx // steps, ny, nz), lambda i: (i, 0, 0))
+    return pl.pallas_call(
+        near_kernel,
+        grid=(steps,),
+        in_specs=[cells] * 3,
+        out_specs=pl.BlockSpec((2, nx // steps, ny, nz), lambda i: (0, i, 0, 0)),
+        out_shape=f32(2, nx, ny, nz),
+        compiler_params=limit(4),
+        cost_estimate=cost(2 * nx * ny * nz, 5 * MIB),
+        name="near",
+    )(eps, sig, label)
+
+
+def select_kernel(dest, recv_hbm, kept, eps_out, sig_out, recv, eps_new, sig_new, recv_sem, out_sem):
+    nx, ny, nz = eps_new.shape
     parts = ny // 8
+    chunks = out_sem.shape[1]
+    size = nx // chunks
+    group = size * parts
+    stores = copies([eps_new, sig_new], [eps_out, sig_out], out_sem, chunks)
+
+    for chunk in range(chunks):
+
+        def fetch(k, carry, chunk=chunk):
+            pltpu.make_async_copy(recv_hbm.at[dest[0, k]], recv.at[k], recv_sem.at[chunk]).start()
+            return carry
+
+        lax.fori_loop(chunk * group, (chunk + 1) * group, fetch, 0, unroll=8)
 
     def body(x, carry):
         for part in range(parts):
-            row = dest[0, x * parts + part]
             rows = slice(part * 8, part * 8 + 8)
-            product = lab_ref[x, rows, :] == 2
-            eps_out[x, rows, :] = jnp.where(product, recv_ref[row, 0:8, :], eps_ref[x, rows, :])
-            sig_out[x, rows, :] = jnp.where(product, recv_ref[row, 8:16, :], sig_ref[x, rows, :])
+            eps = kept[0, x, rows, :]
+            product = eps < 0.0
+            eps_new[x, rows, :] = jnp.where(product, recv[x * parts + part, 0:8, :], eps)
+            sig_new[x, rows, :] = jnp.where(product, recv[x * parts + part, 8:16, :], kept[1, x, rows, :])
         return carry
 
-    lax.fori_loop(0, nx, body, 0, unroll=2)
-
-
-def select(dest, recv, eps, sig, label):
-    nx, ny, nz = eps.shape
+    for chunk in range(chunks):
+        block = pl.ds(chunk * group, group)
+        pltpu.make_async_copy(recv_hbm.at[block], recv.at[block], recv_sem.at[chunk]).wait()
+        lax.fori_loop(chunk * size, (chunk + 1) * size, body, 0, unroll=2)
+        for move in stores[chunk]:
+            move.start()
+    for moves in stores:
+        for move in moves:
+            move.wait()
+
+
+def select(dest, recv, kept):
+    nx, ny, nz = kept.shape[1:]
+    chunks = 8
+    cells = pltpu.VMEM((nx, ny, nz), jnp.float32)
     return pl.pallas_call(
         select_kernel,
-        in_specs=[smem_spec()] + dense(4),
-        out_specs=dense(2),
-        out_shape=[f32(nx, ny, nz), f32(nx, ny, nz)],
-        compiler_params=limit(12),
+        in_specs=[smem_spec(), hbm_spec(), vmem_spec()],
+        out_specs=[hbm_spec()] * 2,
+        out_shape=[hbm(nx, ny, nz), hbm(nx, ny, nz)],
+        scratch_shapes=[
+            pltpu.VMEM(recv.shape, jnp.float32),
+            cells,
+            cells,
+            pltpu.SemaphoreType.DMA((chunks,)),
+            pltpu.SemaphoreType.DMA((2, chunks)),
+        ],
+        compiler_params=limit(8),
         cost_estimate=cost(4 * nx * ny * nz, 7 * MIB),
         name="select",
-    )(dest, recv, eps, sig, label)
+    )(dest, recv, kept)
 
 
 def exchange(value):
@@ -473,7 +657,7 @@
     layer, rows = first_halo(efield)
     for step in range(2):
         gx, gy = borders(layer, rows, -1)
-        hfield, layer, rows = h_update(efield, e_fix, hfield, h_fix)
+        hfield, layer, rows, *h_kept = h_update(efield, e_fix, hfield, h_fix)
         h_fix = h_border(layer, rows, gx, gy)
         gx, gy = borders(*h_fix, 1)
         final = step == 1
@@ -481,18 +665,26 @@
             efield, e_fix, hfield, h_fix, dielectric_grid, sigma_grid, final
         )
         if final:
-            power, *e_fix = power_border(dispatch_keeper_map, power[0], layer, rows, gx, gy)
+            power, *e_fix, e_kept = power_border(
+                dispatch_keeper_map, efield, power[0], layer, rows, gx, gy
+            )
         else:
             e_fix = layer, rows = e_border(layer, rows, gx, gy)
     arrived = exchange(power)
-    factors = lookup(dielectric_lookup_lines, dielectric_line_choice)
+    blocks = lax.optimization_barrier(
+        (power, thermal_state, wetness_share, dielectric_line_choice)
+    )
+    packed = pack(arrival_position_map, dielectric_lookup_lines, *blocks[1:])
+    outgoing = thermal(arrived, *packed)
+    returned = exchange(outgoing)
+    outgoing, arrived, efield, hfield, label = lax.optimization_barrier(
+        (outgoing, arrived, e_kept, h_kept[0], substance_label)
+    )
+    kept = near(dielectric_grid, sigma_grid, label)
     final_efield, final_hfield = flush(efield, e_fix, hfield, h_fix)
-    outgoing, warmth, moisture = thermal(
-        arrival_position_map, arrived, thermal_state, wetness_share, factors
-    )
-    returned = exchange(outgoing)
+    warmth, moisture = heat(arrival_position_map, arrived, thermal_state, wetness_share)
     dielectric_result, sigma_result = select(
-        dispatch_keeper_map, returned, dielectric_grid, sigma_grid, substance_label
+        dispatch_keeper_map, returned, kept
     )
     return final_efield, final_hfield, dielectric_result, sigma_result, warmth, moisture
 

time: 131 us -> 116 us (0.89)
  local copies, waits for them, and re-layouts: 19.2 us -> 8.98 us
  waiting for transfers between devices: 37.4 us -> 28 us
  Pallas kernels: 30.2 us -> 34.9 us
    all_to_all x2, waiting for transfers between devices: 36.1 us -> 24.4 us  [exchange(): lax.all_to_all(value, ('gx', 'gy'), split_axis=0, concat_axis=0, tiled=True)]
    unnamed x40 -> x38, local copies, waits for them, and re-layouts: 19.2 us -> 8.98 us
    pallas_call x4 -> x6, Pallas kernels: 14.9 us -> 24.4 us  [the longest x1 8.03 us: pack(): pl.pallas_call(pack_kernel, grid=(steps,), in_specs=[smem_spec(), smem_sp...]
    pallas_call x2, Pallas kernels: 6.19 us -> 3.35 us  [e_update(): pl.pallas_call(functools.partial(e_kernel, bool(e_fix), final), in_specs=...]
    ppermute x8, waiting for transfers between devices: 1.37 us -> 3.59 us  [passed_along(): return lax.ppermute(value, axis, pairs)]
    pallas_call x2, Pallas kernels: 5.79 us -> 3.79 us  [h_update(): pl.pallas_call(functools.partial(h_kernel, bool(e_fix)), in_specs=dense(l...]
  transfers between devices with their start and end apart: 10 -> 10, of which waited for: 4 -> 4; matrix products, arithmetic and copies ran while one was open for 0% -> 0% of each run, Pallas kernels for 15% -> 21%
where the time goes in v2:
time: 116 us
  starting transfers between devices  42.7 us (37%)
  Pallas kernels  34.9 us (30%)
  waiting for transfers between devices  28 us (24%)
  local copies, waits for them, and re-layouts  8.98 us (8%)
    all_to_all x2, waiting for transfers between devices, exchange(): lax.all_to_all(value, ('gx', 'gy'), split_axis=0, concat_axis=0, tiled=True)  24.4 us
    ppermute x8, starting transfers between devices, passed_along(): return lax.ppermute(value, axis, pairs)  22.5 us
    all_to_all x2, starting transfers between devices, exchange(): lax.all_to_all(value, ('gx', 'gy'), split_axis=0, concat_axis=0, tiled=True)  20.2 us
    unnamed x38, local copies, waits for them, and re-layouts  8.98 us
    pallas_call x1, Pallas kernels, pack(): pl.pallas_call(pack_kernel, grid=(steps,), in_specs=[smem_spec(), smem_sp...  8.03 us
    pallas_call x1, Pallas kernels, heat(): pl.pallas_call(heat_kernel, in_specs=[smem_spec()] + dense(3), out_specs=...  6.08 us
    pallas_call x1, Pallas kernels, thermal(): pl.pallas_call(thermal_kernel, in_specs=[hbm_spec(), hbm_spec()] + dense(...  4.28 us
    pallas_call x2, Pallas kernels, h_update(): pl.pallas_call(functools.partial(h_kernel, bool(e_fix)), in_specs=dense(l...  3.79 us
  transfers between devices with their start and end apart: 10, of which 4 were waited for; matrix products, arithmetic and copies ran while one was open for 0% of the time, Pallas kernels for 21%

profile of v2, /device:TPU:1, one launch (start us, length us, event | category | flops | bytes accessed | tf_op | source)
XLA Modules:
  0.0 115.5 jit_solution(8513379533881506392)
XLA Ops:
  0.6 1.9 %copy-done = f32[3,32,32,256]{3,2,1,0:T(8,128)S(1)} copy-done((f32[3,32,32,256]{3,2,1,0:T(8,128)S(1)}, f32[3,32,32,256]{3,2,1,0:T(8,128)}, u32[]{:S(2)}) %copy-start) | copy-done | bytes 3145752
  2.5 0.1 halo.1
  2.6 1.6 %collective-permute-start = (f32[2,32,256]{2,1,0:T(8,128)S(1)}, f32[2,32,256]{2,1,0:T(8,128)S(1)}, u32[]{:S(2)}, u32[]{:S(2)}) collective-permute-start(f32[2,32,256]{2,1,0:T(8,128)S(1)} %get-tuple-element.48), channel_id=1, source_target_pairs={{8,0},{16,8},{24,16},{32,24},{40,32},{48,40},{56,48},{64,56},{72,6... | collective-permute-start | bytes 196616 | tf_op jit(solution)/shard_map/ppermute | solution.py:20
  4.2 0.0 copy-start.2
  4.2 0.0 copy-start.3
  4.2 3.5 %collective-permute-start.1 = (f32[2,32,256]{2,1,0:T(8,128)S(1)}, f32[2,32,256]{2,1,0:T(8,128)S(1)}, u32[]{:S(2)}, u32[]{:S(2)}) collective-permute-start(f32[2,32,256]{2,1,0:T(8,128)S(1)} %get-tuple-element.49), channel_id=1, source_target_pairs={{1,0},{2,1},{3,2},{4,3},{5,4},{6,5},{7,6},{9,8},{10,9},{11,10},{12... | collective-permute-start | bytes 196616 | tf_op jit(solution)/shard_map/ppermute | solution.py:20
  7.7 1.0 hstep.2
  8.7 0.0 collective-permute-done.gx_ref
  8.7 2.5 %collective-permute-done.1.gy_ref = f32[2,32,256]{2,1,0:T(8,128)S(1)} collective-permute-done((f32[2,32,256]{2,1,0:T(8,128)S(1)}, f32[2,32,256]{2,1,0:T(8,128)S(1)}, u32[]{:S(2)}, u32[]{:S(2)}) %collective-permute-start.1) | collective-permute-done | bytes 65568 | tf_op jit(solution)/shard_map/ppermute | solution.py:20
  11.2 4.3 %collective-permute-start.2 = (f32[2,32,256]{2,1,0:T(8,128)S(1)}, f32[2,32,256]{2,1,0:T(8,128)S(1)}, u32[]{:S(2)}, u32[]{:S(2)}) collective-permute-start(f32[2,32,256]{2,1,0:T(8,128)S(1)} %get-tuple-element.50.refs_2_.refs_4_), channel_id=1, source_target_pairs={{0,8},{8,16},{16,24},{24,32},{32,40},{40,48},{48,56},{56,64},{64,7... | collective-permute-start | bytes 196616 | tf_op jit(solution)/shard_map/ppermute | solution.py:20
  15.5 2.1 %collective-permute-start.3 = (f32[2,32,256]{2,1,0:T(8,128)S(1)}, f32[2,32,256]{2,1,0:T(8,128)S(1)}, u32[]{:S(2)}, u32[]{:S(2)}) collective-permute-start(f32[2,32,256]{2,1,0:T(8,128)S(1)} %get-tuple-element.51.refs_3_.refs_5_), channel_id=1, source_target_pairs={{0,1},{1,2},{2,3},{3,4},{4,5},{5,6},{6,7},{8,9},{9,10},{10,11},{11... | collective-permute-start | bytes 196616 | tf_op jit(solution)/shard_map/ppermute | solution.py:20
  17.7 1.4 %estep.2 = (f32[3,32,32,256]{3,2,1,0:T(8,128)S(1)}, f32[3,32,256]{2,1,0:T(8,128)S(1)}, f32[3,32,256]{2,1,0:T(8,128)S(1)}) custom-call(f32[3,32,32,256]{3,2,1,0:T(8,128)S(1)} %copy-done.1, f32[3,32,32,256]{3,2,1,0:T(8,128)S(1)} %get-tuple-element.45.refs_1_.refs_3_, f32[2,32,256]{2,1,0:T(8,128)S(1)} %get-tuple-element.50.refs_2_.refs_4_, ...), custom_call_target="tpu_custom_call" | custom-call | flops 15728640 | bytes 11534336 | tf_op jit(solution)/shard_map/estep/pallas_call | solution.py:305
  19.1 0.0 collective-permute-done.2.gx_ref
  19.1 0.0 collective-permute-done.3.gy_ref
  19.2 1.3 %collective-permute-start.4 = (f32[2,32,256]{2,1,0:T(8,128)S(1)}, f32[2,32,256]{2,1,0:T(8,128)S(1)}, u32[]{:S(2)}, u32[]{:S(2)}) collective-permute-start(f32[2,32,256]{2,1,0:T(8,128)S(1)} %get-tuple-element.55.refs_1_), channel_id=1, source_target_pairs={{8,0},{16,8},{24,16},{32,24},{40,32},{48,40},{56,48},{64,56},{72,6... | collective-permute-start | bytes 196616 | tf_op jit(solution)/shard_map/ppermute | solution.py:20
  20.5 2.2 %collective-permute-start.5 = (f32[2,32,256]{2,1,0:T(8,128)S(1)}, f32[2,32,256]{2,1,0:T(8,128)S(1)}, u32[]{:S(2)}, u32[]{:S(2)}) collective-permute-start(f32[2,32,256]{2,1,0:T(8,128)S(1)} %get-tuple-element.56.refs_2_), channel_id=1, source_target_pairs={{1,0},{2,1},{3,2},{4,3},{5,4},{6,5},{7,6},{9,8},{10,9},{11,10},{12... | collective-permute-start | bytes 196616 | tf_op jit(solution)/shard_map/ppermute | solution.py:20
  22.6 2.8 %hstep.3 = (f32[3,32,32,256]{3,2,1,0:T(8,128)S(1)}, f32[2,32,256]{2,1,0:T(8,128)S(1)}, f32[2,32,256]{2,1,0:T(8,128)S(1)}, f32[3,32,32,256]{3,2,1,0:T(8,128)}) custom-call(f32[3,32,32,256]{3,2,1,0:T(8,128)S(1)} %get-tuple-element.52.refs_0_, f32[2,32,256]{2,1,0:T(8,128)S(1)} %get-tuple-element.55.refs_1_, f32[2,32,256]{2,1,0:T(8,128)S(1)} %get-tuple-element.56.refs_2_, ...), custom_call_target="tpu_custom_call" | custom-call | flops 10485760 | bytes 9437184 | tf_op jit(solution)/shard_map/hstep/pallas_call | solution.py:211
  25.4 0.0 collective-permute-done.4.gx_ref
  25.4 1.1 collective-permute-done.5.gy_ref
  26.5 4.3 %collective-permute-start.6 = (f32[2,32,256]{2,1,0:T(8,128)S(1)}, f32[2,32,256]{2,1,0:T(8,128)S(1)}, u32[]{:S(2)}, u32[]{:S(2)}) collective-permute-start(f32[2,32,256]{2,1,0:T(8,128)S(1)} %get-tuple-element.60.refs_4_.hl_ref), channel_id=1, source_target_pairs={{0,8},{8,16},{16,24},{24,32},{32,40},{40,48},{48,56},{56,64},{64,7... | collective-permute-start | bytes 196616 | tf_op jit(solution)/shard_map/ppermute | solution.py:20
  30.8 3.3 %collective-permute-start.7 = (f32[2,32,256]{2,1,0:T(8,128)S(1)}, f32[2,32,256]{2,1,0:T(8,128)S(1)}, u32[]{:S(2)}, u32[]{:S(2)}) collective-permute-start(f32[2,32,256]{2,1,0:T(8,128)S(1)} %get-tuple-element.61.refs_5_.hr_ref), channel_id=1, source_target_pairs={{0,1},{1,2},{2,3},{3,4},{4,5},{5,6},{6,7},{8,9},{9,10},{10,11},{11... | collective-permute-start | bytes 196616 | tf_op jit(solution)/shard_map/ppermute | solution.py:20
  34.2 0.0 copy-start.17
  34.2 1.9 %estep.3 = (f32[3,32,32,256]{3,2,1,0:T(8,128)S(1)}, f32[6,32,256]{2,1,0:T(8,128)S(1)}, f32[6,32,256]{2,1,0:T(8,128)S(1)}, f32[32,32,256]{2,1,0:T(8,128)S(1)}) custom-call(f32[3,32,32,256]{3,2,1,0:T(8,128)S(1)} %get-tuple-element.52.refs_0_, f32[2,32,256]{2,1,0:T(8,128)S(1)} %get-tuple-element.55.refs_1_, f32[2,32,256]{2,1,0:T(8,128)S(1)} %get-tuple-element.56.refs_2_, ...), custom_call_target="tpu_custom_call" | custom-call | flops 15728640 | bytes 11534336 | tf_op jit(solution)/shard_map/estep/pallas_call | solution.py:305
  36.1 0.0 collective-permute-done.6.gx_ref
  36.1 0.0 collective-permute-done.7.gy_ref
  36.1 0.0 copy-start.7
  36.2 0.0 copy-start.16
  36.2 0.0 copy-start.18
  36.2 2.6 %power.1 = (f32[128,8,256]{2,1,0:T(8,128)}, f32[2,32,256]{2,1,0:T(8,128)S(1)}, f32[2,32,256]{2,1,0:T(8,128)S(1)}, f32[3,32,32,256]{3,2,1,0:T(8,128)}) custom-call(s32[1,128]{1,0:T(1,128)S(1)} %copy-done.17, f32[3,32,32,256]{3,2,1,0:T(8,128)S(1)} %get-tuple-element.62.e_ref, f32[32,32,256]{2,1,0:T(8,128)S(1)} %get-tuple-element.63.p_ref, ...), custom_call_target="tpu_custom_call" | custom-call | flops 1048576 | bytes 8388608 | tf_op jit(solution)/shard_map/power/pallas_call | solution.py:377
  38.8 14.4 %all-to-all-start = ((f32[128,8,256]{2,1,0:T(8,128)}), f32[128,8,256]{2,1,0:T(8,128)}, u32[]{:S(2)}, u32[]{:S(2)}) async-start(f32[128,8,256]{2,1,0:T(8,128)} %get-tuple-element.66), calls=%async_computation | async-start | bytes 2097152 | tf_op jit(solution)/shard_map/all_to_all | solution.py:635
  53.2 0.0 copy-start.9
  53.2 1.2 %copy-done.9 = f32[128,8,256]{2,1,0:T(8,128)S(1)} copy-done((f32[128,8,256]{2,1,0:T(8,128)S(1)}, f32[128,8,256]{2,1,0:T(8,128)}, u32[]{:S(2)}) %copy-start.9) | copy-done | bytes 1048600
  54.4 1.2 %copy-done.14 = s32[128,8,256]{2,1,0:T(8,128)S(1)} copy-done((s32[128,8,256]{2,1,0:T(8,128)S(1)}, s32[128,8,256]{2,1,0:T(8,128)}, u32[]{:S(2)}) %copy-start.14) | copy-done | bytes 1048600
  55.6 8.0 %pack.1.far_hbm = f32[128,40,256]{2,1,0:T(8,128)} custom-call(s32[1,128]{1,0:T(1,128)S(1)} %copy-done.18, f32[4,16]{1,0:T(4,128)S(1)} %copy-done.16, f32[128,8,256]{2,1,0:T(8,128)S(1)} %copy-done.7, f32[128,8,256]{2,1,0:T(8,128)S(1)} %copy-done.9, s32[128,8,256]{2,1,0:T(8,128)S(1)} %copy-done.14), custom_call_target="tpu_custom_call" | custom-call | flops 20971520 | bytes 9437184 | tf_op jit(solution)/shard_map/pack/pallas_call | solution.py:455
  63.7 8.4 %all-to-all-done.p_hbm.p_ref = f32[128,8,256]{2,1,0:T(8,128)} async-done(((f32[128,8,256]{2,1,0:T(8,128)}), f32[128,8,256]{2,1,0:T(8,128)}, u32[]{:S(2)}, u32[]{:S(2)}) %all-to-all-start) | async-done | bytes 1048608 | tf_op jit(solution)/shard_map/all_to_all | solution.py:635
  72.1 4.3 %thermal.1 = f32[128,16,256]{2,1,0:T(8,128)} custom-call(f32[128,8,256]{2,1,0:T(8,128)} %all-to-all-done.p_hbm.p_ref, f32[128,40,256]{2,1,0:T(8,128)} %pack.1.far_hbm), custom_call_target="tpu_custom_call" | custom-call | flops 10485760 | bytes 8388608 | tf_op jit(solution)/shard_map/thermal/pallas_call | solution.py:505
  76.4 0.0 copy-start.4
  76.4 5.8 %all-to-all-start.1 = ((f32[128,16,256]{2,1,0:T(8,128)}), f32[128,16,256]{2,1,0:T(8,128)}, u32[]{:S(2)}, u32[]{:S(2)}) async-start(f32[128,16,256]{2,1,0:T(8,128)} %thermal.1), calls=%async_computation.1 | async-start | bytes 4194304 | tf_op jit(solution)/shard_map/all_to_all | solution.py:635
  82.2 0.0 copy-start.12
  82.2 0.0 copy-start.15
  82.2 1.4 %copy-done.15 = s32[32,32,256]{2,1,0:T(8,128)S(1)} copy-done((s32[32,32,256]{2,1,0:T(8,128)S(1)}, s32[32,32,256]{2,1,0:T(8,128)}, u32[]{:S(2)}) %copy-start.15) | copy-done | bytes 1048600
  83.6 0.4 near.1.kept
  84.0 1.3 %copy-done.5 = f32[2,32,32,256]{3,2,1,0:T(8,128)} copy-done((f32[2,32,32,256]{3,2,1,0:T(8,128)}, f32[2,32,32,256]{3,2,1,0:T(8,128)S(1)}, u32[]{:S(2)}) %copy-start.5) | copy-done | bytes 2097176
  85.3 1.9 %copy-done.13 = f32[3,32,32,256]{3,2,1,0:T(8,128)S(1)} copy-done((f32[3,32,32,256]{3,2,1,0:T(8,128)S(1)}, f32[3,32,32,256]{3,2,1,0:T(8,128)}, u32[]{:S(2)}) %copy-start.13) | copy-done | bytes 3145752
  87.2 3.2 %flush.1 = (f32[3,32,32,256]{3,2,1,0:T(8,128)}, f32[3,32,32,256]{3,2,1,0:T(8,128)}) custom-call(f32[3,32,32,256]{3,2,1,0:T(8,128)S(1)} %copy-done.13, f32[2,32,256]{2,1,0:T(8,128)S(1)} %get-tuple-element.73.el_ref, f32[2,32,256]{2,1,0:T(8,128)S(1)} %get-tuple-element.74.er_ref, f32[3,32,32,256]{3,2,1,0:T(8,128)S(1)} %copy-done.12, ...), custom_call_target="tpu_custom_call" | custom-call | flops 786432 | bytes 12582912 | tf_op jit(solution)/shard_map/flush/pallas_call | solution.py:407
  90.4 6.1 %heat.1 = (f32[128,8,256]{2,1,0:T(8,128)}, f32[128,8,256]{2,1,0:T(8,128)}) custom-call(s32[1,128]{1,0:T(1,128)S(1)} %copy-done.18, f32[128,8,256]{2,1,0:T(8,128)} %all-to-all-done.p_hbm.p_ref, f32[128,8,256]{2,1,0:T(8,128)S(1)} %copy-done.8, f32[128,8,256]{2,1,0:T(8,128)S(1)} %copy-done.10), custom_call_target="tpu_custom_call" | custom-call | flops 10485760 | bytes 5242880 | tf_op jit(solution)/shard_map/heat/pallas_call | solution.py:544
  96.5 16.0 %all-to-all-done.1.recv_hbm = f32[128,16,256]{2,1,0:T(8,128)} async-done(((f32[128,16,256]{2,1,0:T(8,128)}), f32[128,16,256]{2,1,0:T(8,128)}, u32[]{:S(2)}, u32[]{:S(2)}) %all-to-all-start.1) | async-done | bytes 2097184 | tf_op jit(solution)/shard_map/all_to_all | solution.py:635
  112.5 3.0 %select.1 = (f32[32,32,256]{2,1,0:T(8,128)}, f32[32,32,256]{2,1,0:T(8,128)}) custom-call(s32[1,128]{1,0:T(1,128)S(1)} %copy-done.17, f32[128,16,256]{2,1,0:T(8,128)} %all-to-all-done.1.recv_hbm, f32[2,32,32,256]{3,2,1,0:T(8,128)S(1)} %copy-done.6), custom_call_target="tpu_custom_call" | custom-call | flops 1048576 | bytes 7340032 | tf_op jit(solution)/shard_map/select/pallas_call | solution.py:616
  (25 shorter events, 0.1 us)
Async XLA Ops:
  0.6 1.9 %copy-start = (f32[3,32,32,256]{3,2,1,0:T(8,128)S(1)}, f32[3,32,32,256]{3,2,1,0:T(8,128)}, u32[]{:S(2)}) copy-start(f32[3,32,32,256]{3,2,1,0:T(8,128)} %refs_0_.3) | copy-start | bytes 9437188
  2.5 5.1 %copy-start.1 = (f32[3,32,32,256]{3,2,1,0:T(8,128)S(1)}, f32[3,32,32,256]{3,2,1,0:T(8,128)}, u32[]{:S(2)}) copy-start(f32[3,32,32,256]{3,2,1,0:T(8,128)} %refs_0_.3) | copy-start | bytes 9437188
  2.5 5.2 %copy-start.11 = (f32[3,32,32,256]{3,2,1,0:T(8,128)S(1)}, f32[3,32,32,256]{3,2,1,0:T(8,128)}, u32[]{:S(2)}) copy-start(f32[3,32,32,256]{3,2,1,0:T(8,128)} %refs_1_.1) | copy-start | bytes 9437188
  2.6 6.1 %collective-permute-start = (f32[2,32,256]{2,1,0:T(8,128)S(1)}, f32[2,32,256]{2,1,0:T(8,128)S(1)}, u32[]{:S(2)}, u32[]{:S(2)}) collective-permute-start(f32[2,32,256]{2,1,0:T(8,128)S(1)} %get-tuple-element.48), channel_id=1, source_target_pairs={{8,0},{16,8},{24,16},{32,24},{40,32},{48,40},{56,48},{64,56},{72,6... | collective-permute-start | bytes 196616 | tf_op jit(solution)/shard_map/ppermute | solution.py:20
  4.2 13.5 %copy-start.2 = (f32[32,32,256]{2,1,0:T(8,128)S(1)}, f32[32,32,256]{2,1,0:T(8,128)}, u32[]{:S(2)}) copy-start(f32[32,32,256]{2,1,0:T(8,128)} %eps_ref.1) | copy-start | bytes 3145732
  4.2 13.5 %copy-start.3 = (f32[32,32,256]{2,1,0:T(8,128)S(1)}, f32[32,32,256]{2,1,0:T(8,128)}, u32[]{:S(2)}) copy-start(f32[32,32,256]{2,1,0:T(8,128)} %sig_ref.1) | copy-start | bytes 3145732
  4.2 7.0 %collective-permute-start.1 = (f32[2,32,256]{2,1,0:T(8,128)S(1)}, f32[2,32,256]{2,1,0:T(8,128)S(1)}, u32[]{:S(2)}, u32[]{:S(2)}) collective-permute-start(f32[2,32,256]{2,1,0:T(8,128)S(1)} %get-tuple-element.49), channel_id=1, source_target_pairs={{1,0},{2,1},{3,2},{4,3},{5,4},{6,5},{7,6},{9,8},{10,9},{11,10},{12... | collective-permute-start | bytes 196616 | tf_op jit(solution)/shard_map/ppermute | solution.py:20
  11.2 7.9 %collective-permute-start.2 = (f32[2,32,256]{2,1,0:T(8,128)S(1)}, f32[2,32,256]{2,1,0:T(8,128)S(1)}, u32[]{:S(2)}, u32[]{:S(2)}) collective-permute-start(f32[2,32,256]{2,1,0:T(8,128)S(1)} %get-tuple-element.50.refs_2_.refs_4_), channel_id=1, source_target_pairs={{0,8},{8,16},{16,24},{24,32},{32,40},{40,48},{48,56},{56,64},{64,7... | collective-permute-start | bytes 196616 | tf_op jit(solution)/shard_map/ppermute | solution.py:20
  15.5 3.6 %collective-permute-start.3 = (f32[2,32,256]{2,1,0:T(8,128)S(1)}, f32[2,32,256]{2,1,0:T(8,128)S(1)}, u32[]{:S(2)}, u32[]{:S(2)}) collective-permute-start(f32[2,32,256]{2,1,0:T(8,128)S(1)} %get-tuple-element.51.refs_3_.refs_5_), channel_id=1, source_target_pairs={{0,1},{1,2},{2,3},{3,4},{4,5},{5,6},{6,7},{8,9},{9,10},{10,11},{11... | collective-permute-start | bytes 196616 | tf_op jit(solution)/shard_map/ppermute | solution.py:20
  19.2 6.3 %collective-permute-start.4 = (f32[2,32,256]{2,1,0:T(8,128)S(1)}, f32[2,32,256]{2,1,0:T(8,128)S(1)}, u32[]{:S(2)}, u32[]{:S(2)}) collective-permute-start(f32[2,32,256]{2,1,0:T(8,128)S(1)} %get-tuple-element.55.refs_1_), channel_id=1, source_target_pairs={{8,0},{16,8},{24,16},{32,24},{40,32},{48,40},{56,48},{64,56},{72,6... | collective-permute-start | bytes 196616 | tf_op jit(solution)/shard_map/ppermute | solution.py:20
  20.5 6.1 %collective-permute-start.5 = (f32[2,32,256]{2,1,0:T(8,128)S(1)}, f32[2,32,256]{2,1,0:T(8,128)S(1)}, u32[]{:S(2)}, u32[]{:S(2)}) collective-permute-start(f32[2,32,256]{2,1,0:T(8,128)S(1)} %get-tuple-element.56.refs_2_), channel_id=1, source_target_pairs={{1,0},{2,1},{3,2},{4,3},{5,4},{6,5},{7,6},{9,8},{10,9},{11,10},{12... | collective-permute-start | bytes 196616 | tf_op jit(solution)/shard_map/ppermute | solution.py:20
  26.5 9.6 %collective-permute-start.6 = (f32[2,32,256]{2,1,0:T(8,128)S(1)}, f32[2,32,256]{2,1,0:T(8,128)S(1)}, u32[]{:S(2)}, u32[]{:S(2)}) collective-permute-start(f32[2,32,256]{2,1,0:T(8,128)S(1)} %get-tuple-element.60.refs_4_.hl_ref), channel_id=1, source_target_pairs={{0,8},{8,16},{16,24},{24,32},{32,40},{40,48},{48,56},{56,64},{64,7... | collective-permute-start | bytes 196616 | tf_op jit(solution)/shard_map/ppermute | solution.py:20
  30.8 5.3 %collective-permute-start.7 = (f32[2,32,256]{2,1,0:T(8,128)S(1)}, f32[2,32,256]{2,1,0:T(8,128)S(1)}, u32[]{:S(2)}, u32[]{:S(2)}) collective-permute-start(f32[2,32,256]{2,1,0:T(8,128)S(1)} %get-tuple-element.61.refs_5_.hr_ref), channel_id=1, source_target_pairs={{0,1},{1,2},{2,3},{3,4},{4,5},{5,6},{6,7},{8,9},{9,10},{10,11},{11... | collective-permute-start | bytes 196616 | tf_op jit(solution)/shard_map/ppermute | solution.py:20
  34.2 2.0 %copy-start.17 = (s32[1,128]{1,0:T(1,128)S(1)}, s32[1,128]{1,0:T(1,128)}, u32[]{:S(2)}) copy-start(s32[1,128]{1,0:T(1,128)} %dest.3) | copy-start | bytes 1540
  36.1 17.0 %copy-start.7 = (f32[128,8,256]{2,1,0:T(8,128)S(1)}, f32[128,8,256]{2,1,0:T(8,128)}, u32[]{:S(2)}) copy-start(f32[128,8,256]{2,1,0:T(8,128)} %t_ref.2) | copy-start | bytes 3145732
  36.2 17.0 %copy-start.16 = (f32[4,16]{1,0:T(4,128)S(1)}, f32[4,16]{1,0:T(4,128)}, u32[]{:S(2)}) copy-start(f32[4,16]{1,0:T(4,128)} %lines.1) | copy-start | bytes 772
  36.2 17.0 %copy-start.18 = (s32[1,128]{1,0:T(1,128)S(1)}, s32[1,128]{1,0:T(1,128)}, u32[]{:S(2)}) copy-start(s32[1,128]{1,0:T(1,128)} %arrive.3) | copy-start | bytes 1540
  38.8 33.3 %all-to-all-start = ((f32[128,8,256]{2,1,0:T(8,128)}), f32[128,8,256]{2,1,0:T(8,128)}, u32[]{:S(2)}, u32[]{:S(2)}) async-start(f32[128,8,256]{2,1,0:T(8,128)} %get-tuple-element.66), calls=%async_computation | async-start | bytes 2097152 | tf_op jit(solution)/shard_map/all_to_all | solution.py:635
  53.2 1.2 %copy-start.9 = (f32[128,8,256]{2,1,0:T(8,128)S(1)}, f32[128,8,256]{2,1,0:T(8,128)}, u32[]{:S(2)}) copy-start(f32[128,8,256]{2,1,0:T(8,128)} %w_ref.2) | copy-start | bytes 3145732
  54.4 1.2 %copy-start.14 = (s32[128,8,256]{2,1,0:T(8,128)S(1)}, s32[128,8,256]{2,1,0:T(8,128)}, u32[]{:S(2)}) copy-start(s32[128,8,256]{2,1,0:T(8,128)} %c_ref) | copy-start | bytes 3145732
  76.4 5.9 %copy-start.4 = (f32[32,32,256]{2,1,0:T(8,128)S(1)}, f32[32,32,256]{2,1,0:T(8,128)}, u32[]{:S(2)}) copy-start(f32[32,32,256]{2,1,0:T(8,128)} %sig_ref.1) | copy-start | bytes 3145732
  76.4 36.1 %all-to-all-start.1 = ((f32[128,16,256]{2,1,0:T(8,128)}), f32[128,16,256]{2,1,0:T(8,128)}, u32[]{:S(2)}, u32[]{:S(2)}) async-start(f32[128,16,256]{2,1,0:T(8,128)} %thermal.1), calls=%async_computation.1 | async-start | bytes 4194304 | tf_op jit(solution)/shard_map/all_to_all | solution.py:635
  82.2 3.1 %copy-start.12 = (f32[3,32,32,256]{3,2,1,0:T(8,128)S(1)}, f32[3,32,32,256]{3,2,1,0:T(8,128)}, u32[]{:S(2)}) copy-start(f32[3,32,32,256]{3,2,1,0:T(8,128)} %get-tuple-element.75.h_ref) | copy-start | bytes 9437188
  82.2 1.4 %copy-start.15 = (s32[32,32,256]{2,1,0:T(8,128)S(1)}, s32[32,32,256]{2,1,0:T(8,128)}, u32[]{:S(2)}) copy-start(s32[32,32,256]{2,1,0:T(8,128)} %lab_ref) | copy-start | bytes 3145732
  84.0 1.3 %copy-start.5 = (f32[2,32,32,256]{3,2,1,0:T(8,128)}, f32[2,32,32,256]{3,2,1,0:T(8,128)S(1)}, u32[]{:S(2)}) copy-start(f32[2,32,32,256]{3,2,1,0:T(8,128)S(1)} %near.1.kept) | copy-start | bytes 6291460
  85.3 1.9 %copy-start.13 = (f32[3,32,32,256]{3,2,1,0:T(8,128)S(1)}, f32[3,32,32,256]{3,2,1,0:T(8,128)}, u32[]{:S(2)}) copy-start(f32[3,32,32,256]{3,2,1,0:T(8,128)} %get-tuple-element.72.e_ref) | copy-start | bytes 9437188
  87.2 3.2 %copy-start.8 = (f32[128,8,256]{2,1,0:T(8,128)S(1)}, f32[128,8,256]{2,1,0:T(8,128)}, u32[]{:S(2)}) copy-start(f32[128,8,256]{2,1,0:T(8,128)} %t_ref.2) | copy-start | bytes 3145732
  87.2 3.2 %copy-start.10 = (f32[128,8,256]{2,1,0:T(8,128)S(1)}, f32[128,8,256]{2,1,0:T(8,128)}, u32[]{:S(2)}) copy-start(f32[128,8,256]{2,1,0:T(8,128)} %w_ref.2) | copy-start | bytes 3145732
  90.4 22.1 %copy-start.6 = (f32[2,32,32,256]{3,2,1,0:T(8,128)S(1)}, f32[2,32,32,256]{3,2,1,0:T(8,128)}, u32[]{:S(2)}) copy-start(f32[2,32,32,256]{3,2,1,0:T(8,128)} %copy-done.5) | copy-start | bytes 6291460

commit v3 on v2

--- a/solution.py
+++ b/solution.py
@@ -10,6 +10,7 @@
 DT = 0.5
 MIB = 1 << 20
 GROUP = 10
+HALF = 5
 FAR = 5
 THERMAL_MIB = 62
 
@@ -148,23 +149,48 @@
     return hx, hy, hz
 
 
-def parts_of_copy(source, target, sem):
-    return [pltpu.make_async_copy(source.at[k], target.at[k], sem.at[k]) for k in range(source.shape[0])]
-
-
-def walk(slab, nx):
+def walk(slab, nx, move=None):
     groups = (nx - 2) // GROUP
+    pieces = GROUP // HALF
+
+    def send(*where):
+        if move is not None:
+            move(*where).start()
+
     slab(0, True, False)
+    send(0, 1, 0)
 
     def body(g, carry):
-        for k in range(GROUP):
-            slab(1 + g * GROUP + k, False, False)
+        for piece in range(pieces):
+            first = 1 + g * GROUP + piece * HALF
+            for k in range(HALF):
+                slab(first + k, False, False)
+            send(first, HALF, 1 + g * pieces + piece)
         return carry
 
     lax.fori_loop(0, groups, body, 0)
     for x in range(1 + groups * GROUP, nx - 1):
         slab(x, False, False)
     slab(nx - 1, False, True)
+    rest = 1 + groups * GROUP
+    send(rest, nx - rest, 1 + groups * pieces)
+    if move is not None:
+        move(0, 1, 0).wait()
+        for k in range(groups * pieces):
+            move(1 + k * HALF, HALF, 1 + k).wait()
+        move(rest, nx - rest, 1 + groups * pieces).wait()
+
+
+def carry_off(source, target, sem):
+    def move(start, size, index):
+        where = (slice(None), pl.ds(start, size))
+        return pltpu.make_async_copy(source.at[where], target.at[where], sem.at[index])
+
+    return move
+
+
+def copy_count(nx):
+    return 2 + (nx - 2) // GROUP * (GROUP // HALF)
 
 
 def h_kernel(fixed, *refs):
@@ -195,13 +221,7 @@
             layer_ref[0] = hy
             layer_ref[1] = hz
 
-    walk(slab, nx)
-    if fixed:
-        moves = parts_of_copy(out_ref, out_hbm, sem)
-        for move in moves:
-            move.start()
-        for move in moves:
-            move.wait()
+    walk(slab, nx, carry_off(out_ref, out_hbm, sem) if fixed else None)
 
 
 def h_update(efield, e_fix, hfield, h_fix):
@@ -213,7 +233,7 @@
         in_specs=dense(len(args)),
         out_specs=dense(3) + [hbm_spec()] * bool(e_fix),
         out_shape=outs + [hbm(3, nx, ny, nz)] * bool(e_fix),
-        scratch_shapes=[pltpu.SemaphoreType.DMA((3,))] * bool(e_fix),
+        scratch_shapes=[pltpu.SemaphoreType.DMA((copy_count(nx),))] * bool(e_fix),
         compiler_params=limit(16),
         cost_estimate=cost(40 * nx * ny * nz, 9 * MIB),
         name="hstep",
@@ -247,10 +267,16 @@
 
 def e_kernel(fixed, final, *refs):
     refs = list(refs)
+    if final:
+        *refs, keep_ref, sem = refs
     e_ref = refs.pop(0)
     el_ref, er_ref = (refs.pop(0), refs.pop(0)) if fixed else (None, None)
     h_ref, hl_ref, hr_ref, eps_ref, sig_ref, out_ref, layer_ref, rows_ref = refs[:8]
     nx, ny, nz = e_ref.shape[1:]
+    move = None
+    if final:
+        move = carry_off(keep_ref, out_ref, sem)
+        out_ref = keep_ref
 
     def slab(x, first, last):
         hx, hy, hz = h_slab(x, last, h_ref, hl_ref, hr_ref)
@@ -292,7 +318,7 @@
                 layer_ref[4] = before
                 layer_ref[5] = half
 
-    walk(slab, nx)
+    walk(slab, nx, move)
 
 
 def e_update(efield, e_fix, hfield, h_fix, eps, sig, final):
@@ -300,13 +326,19 @@
     args = [efield, *e_fix, hfield, *h_fix, eps, sig]
     kept = 6 if final else 3
     outs = [f32(3, nx, ny, nz), f32(kept, ny, nz), f32(kept, nx, nz)]
+    specs = dense(3)
+    scratch = []
     if final:
+        outs[0] = hbm(3, nx, ny, nz)
         outs.append(f32(nx, ny, nz))
+        specs = [hbm_spec(), vmem_spec(), vmem_spec(), vmem_spec()]
+        scratch = [pltpu.VMEM((3, nx, ny, nz), jnp.float32), pltpu.SemaphoreType.DMA((copy_count(nx),))]
     return pl.pallas_call(
         functools.partial(e_kernel, bool(e_fix), final),
         in_specs=dense(len(args)),
-        out_specs=dense(len(outs)),
+        out_specs=specs,
         out_shape=outs,
+        scratch_shapes=scratch,
         compiler_params=limit(16),
         cost_estimate=cost(60 * nx * ny * nz, 11 * MIB),
         name="estep",
@@ -339,10 +371,7 @@
     )(layer, rows, gx, gy)
 
 
-def power_kernel(dest, e_ref, p_ref, layer_ref, rows_ref, gx_ref, gy_ref, out_hbm, layer_out, rows_out, e_hbm, scratch, out_ref, sem, e_sem):
-    moves = parts_of_copy(e_ref, e_hbm, e_sem)
-    for move in moves:
-        move.start()
+def power_kernel(dest, p_ref, layer_ref, rows_ref, gx_ref, gy_ref, out_hbm, layer_out, rows_out, scratch, out_ref, sem):
     nx, ny, nz = p_ref.shape
     parts = ny // 8
     ey_layer, ez_layer, ex_rows, ez_rows = e_border_values(layer_ref, rows_ref, gx_ref, gy_ref)
@@ -366,29 +395,27 @@
         return carry
 
     lax.fori_loop(1, nx, body, 0, unroll=2)
-    moves.append(pltpu.make_async_copy(out_ref, out_hbm, sem))
-    moves[-1].start()
-    for move in moves:
-        move.wait()
-
-
-def power_border(dest, efield, power, layer, rows, gx, gy):
+    move = pltpu.make_async_copy(out_ref, out_hbm, sem)
+    move.start()
+    move.wait()
+
+
+def power_border(dest, power, layer, rows, gx, gy):
     nx, ny, nz = power.shape
     return pl.pallas_call(
         power_kernel,
-        in_specs=[smem_spec()] + dense(6),
-        out_specs=[hbm_spec()] + dense(2) + [hbm_spec()],
-        out_shape=[hbm(nx * ny // 8, 8, nz), f32(*gx.shape), f32(*gy.shape), hbm(*efield.shape)],
+        in_specs=[smem_spec()] + dense(5),
+        out_specs=[hbm_spec()] + dense(2),
+        out_shape=[hbm(nx * ny // 8, 8, nz), f32(*gx.shape), f32(*gy.shape)],
         scratch_shapes=[
             pltpu.VMEM((nx, nz), jnp.float32),
             pltpu.VMEM((nx * ny // 8, 8, nz), jnp.float32),
             pltpu.SemaphoreType.DMA(()),
-            pltpu.SemaphoreType.DMA((3,)),
         ],
         compiler_params=limit(8),
-        cost_estimate=cost(4 * nx * ny * nz, 8 * MIB),
+        cost_estimate=cost(4 * nx * ny * nz, 2 * MIB),
         name="power",
-    )(dest, efield, power, layer, rows, gx, gy)
+    )(dest, power, layer, rows, gx, gy)
 
 
 def flush_kernel(e_ref, el_ref, er_ref, h_ref, hl_ref, hr_ref, e_out, h_out):
@@ -665,9 +692,7 @@
             efield, e_fix, hfield, h_fix, dielectric_grid, sigma_grid, final
         )
         if final:
-            power, *e_fix, e_kept = power_border(
-                dispatch_keeper_map, efield, power[0], layer, rows, gx, gy
-            )
+            power, *e_fix = power_border(dispatch_keeper_map, power[0], layer, rows, gx, gy)
         else:
             e_fix = layer, rows = e_border(layer, rows, gx, gy)
     arrived = exchange(power)
@@ -678,7 +703,7 @@
     outgoing = thermal(arrived, *packed)
     returned = exchange(outgoing)
     outgoing, arrived, efield, hfield, label = lax.optimization_barrier(
-        (outgoing, arrived, e_kept, h_kept[0], substance_label)
+        (outgoing, arrived, efield, h_kept[0], substance_label)
     )
     kept = near(dielectric_grid, sigma_grid, label)
     final_efield, final_hfield = flush(efield, e_fix, hfield, h_fix)

time: 116 us -> 115 us (level)
  starting transfers between devices: 42.7 us -> 41.5 us
    all_to_all x2, starting transfers between devices: 20.2 us -> 19 us  [exchange(): lax.all_to_all(value, ('gx', 'gy'), split_axis=0, concat_axis=0, tiled=True)]
  transfers between devices with their start and end apart: 10 -> 10, of which waited for: 4 -> 4; matrix products, arithmetic and copies ran while one was open for 0% -> 0% of each run, Pallas kernels for 21% -> 22%
where the time goes in v3:
time: 115 us; the launch traced here: 114 us
  starting transfers between devices  41.5 us (36%)
  Pallas kernels  34 us (30%)
  waiting for transfers between devices  28.8 us (25%)
  local copies, waits for them, and re-layouts  8.98 us (8%)
    all_to_all x2, waiting for transfers between devices, exchange(): lax.all_to_all(value, ('gx', 'gy'), split_axis=0, concat_axis=0, tiled=True)  24.4 us
    ppermute x8, starting transfers between devices, passed_along(): return lax.ppermute(value, axis, pairs)  22.5 us
    all_to_all x2, starting transfers between devices, exchange(): lax.all_to_all(value, ('gx', 'gy'), split_axis=0, concat_axis=0, tiled=True)  19 us
    unnamed x38, local copies, waits for them, and re-layouts  8.98 us
    pallas_call x1, Pallas kernels, pack(): pl.pallas_call(pack_kernel, grid=(steps,), in_specs=[smem_spec(), smem_sp...  8.03 us
    pallas_call x1, Pallas kernels, heat(): pl.pallas_call(heat_kernel, in_specs=[smem_spec()] + dense(3), out_specs=...  6.08 us
    ppermute x8, waiting for transfers between devices, passed_along(): return lax.ppermute(value, axis, pairs)  4.4 us
    pallas_call x1, Pallas kernels, thermal(): pl.pallas_call(thermal_kernel, in_specs=[hbm_spec(), hbm_spec()] + dense(...  4.28 us
  transfers between devices with their start and end apart: 10, of which 4 were waited for; matrix products, arithmetic and copies ran while one was open for 0% of the time, Pallas kernels for 22%

profile of v3, /device:TPU:1, one launch (start us, length us, event | category | flops | bytes accessed | tf_op | source)
XLA Modules:
  0.0 114.3 jit_solution(9849733742861366568)
XLA Ops:
  0.6 1.9 %copy-done = f32[3,32,32,256]{3,2,1,0:T(8,128)S(1)} copy-done((f32[3,32,32,256]{3,2,1,0:T(8,128)S(1)}, f32[3,32,32,256]{3,2,1,0:T(8,128)}, u32[]{:S(2)}) %copy-start) | copy-done | bytes 3145752
  2.5 0.1 halo.1
  2.6 1.6 %collective-permute-start = (f32[2,32,256]{2,1,0:T(8,128)S(1)}, f32[2,32,256]{2,1,0:T(8,128)S(1)}, u32[]{:S(2)}, u32[]{:S(2)}) collective-permute-start(f32[2,32,256]{2,1,0:T(8,128)S(1)} %get-tuple-element.47), channel_id=1, source_target_pairs={{8,0},{16,8},{24,16},{32,24},{40,32},{48,40},{56,48},{64,56},{72,6... | collective-permute-start | bytes 196616 | tf_op jit(solution)/shard_map/ppermute | solution.py:21
  4.2 0.0 copy-start.2
  4.2 0.0 copy-start.3
  4.2 3.5 %collective-permute-start.1 = (f32[2,32,256]{2,1,0:T(8,128)S(1)}, f32[2,32,256]{2,1,0:T(8,128)S(1)}, u32[]{:S(2)}, u32[]{:S(2)}) collective-permute-start(f32[2,32,256]{2,1,0:T(8,128)S(1)} %get-tuple-element.48), channel_id=1, source_target_pairs={{1,0},{2,1},{3,2},{4,3},{5,4},{6,5},{7,6},{9,8},{10,9},{11,10},{12... | collective-permute-start | bytes 196616 | tf_op jit(solution)/shard_map/ppermute | solution.py:21
  7.7 1.0 hstep.2
  8.7 0.0 collective-permute-done.gx_ref
  8.7 2.5 %collective-permute-done.1.gy_ref = f32[2,32,256]{2,1,0:T(8,128)S(1)} collective-permute-done((f32[2,32,256]{2,1,0:T(8,128)S(1)}, f32[2,32,256]{2,1,0:T(8,128)S(1)}, u32[]{:S(2)}, u32[]{:S(2)}) %collective-permute-start.1) | collective-permute-done | bytes 65568 | tf_op jit(solution)/shard_map/ppermute | solution.py:21
  11.2 4.3 %collective-permute-start.2 = (f32[2,32,256]{2,1,0:T(8,128)S(1)}, f32[2,32,256]{2,1,0:T(8,128)S(1)}, u32[]{:S(2)}, u32[]{:S(2)}) collective-permute-start(f32[2,32,256]{2,1,0:T(8,128)S(1)} %get-tuple-element.49.refs_2_.refs_4_), channel_id=1, source_target_pairs={{0,8},{8,16},{16,24},{24,32},{32,40},{40,48},{48,56},{56,64},{64,7... | collective-permute-start | bytes 196616 | tf_op jit(solution)/shard_map/ppermute | solution.py:21
  15.5 2.1 %collective-permute-start.3 = (f32[2,32,256]{2,1,0:T(8,128)S(1)}, f32[2,32,256]{2,1,0:T(8,128)S(1)}, u32[]{:S(2)}, u32[]{:S(2)}) collective-permute-start(f32[2,32,256]{2,1,0:T(8,128)S(1)} %get-tuple-element.50.refs_3_.refs_5_), channel_id=1, source_target_pairs={{0,1},{1,2},{2,3},{3,4},{4,5},{5,6},{6,7},{8,9},{9,10},{10,11},{11... | collective-permute-start | bytes 196616 | tf_op jit(solution)/shard_map/ppermute | solution.py:21
  17.7 1.4 %estep.2 = (f32[3,32,32,256]{3,2,1,0:T(8,128)S(1)}, f32[3,32,256]{2,1,0:T(8,128)S(1)}, f32[3,32,256]{2,1,0:T(8,128)S(1)}) custom-call(f32[3,32,32,256]{3,2,1,0:T(8,128)S(1)} %copy-done.1, f32[3,32,32,256]{3,2,1,0:T(8,128)S(1)} %get-tuple-element.44.refs_1_.refs_3_, f32[2,32,256]{2,1,0:T(8,128)S(1)} %get-tuple-element.49.refs_2_.refs_4_, ...), custom_call_target="tpu_custom_call" | custom-call | flops 15728640 | bytes 11534336 | tf_op jit(solution)/shard_map/estep/pallas_call | solution.py:336
  19.1 0.0 collective-permute-done.2.gx_ref
  19.1 0.0 collective-permute-done.3.gy_ref
  19.2 1.3 %collective-permute-start.4 = (f32[2,32,256]{2,1,0:T(8,128)S(1)}, f32[2,32,256]{2,1,0:T(8,128)S(1)}, u32[]{:S(2)}, u32[]{:S(2)}) collective-permute-start(f32[2,32,256]{2,1,0:T(8,128)S(1)} %get-tuple-element.54.refs_1_), channel_id=1, source_target_pairs={{8,0},{16,8},{24,16},{32,24},{40,32},{48,40},{56,48},{64,56},{72,6... | collective-permute-start | bytes 196616 | tf_op jit(solution)/shard_map/ppermute | solution.py:21
  20.5 2.2 %collective-permute-start.5 = (f32[2,32,256]{2,1,0:T(8,128)S(1)}, f32[2,32,256]{2,1,0:T(8,128)S(1)}, u32[]{:S(2)}, u32[]{:S(2)}) collective-permute-start(f32[2,32,256]{2,1,0:T(8,128)S(1)} %get-tuple-element.55.refs_2_), channel_id=1, source_target_pairs={{1,0},{2,1},{3,2},{4,3},{5,4},{6,5},{7,6},{9,8},{10,9},{11,10},{12... | collective-permute-start | bytes 196616 | tf_op jit(solution)/shard_map/ppermute | solution.py:21
  22.6 2.0 %hstep.3 = (f32[3,32,32,256]{3,2,1,0:T(8,128)S(1)}, f32[2,32,256]{2,1,0:T(8,128)S(1)}, f32[2,32,256]{2,1,0:T(8,128)S(1)}, f32[3,32,32,256]{3,2,1,0:T(8,128)}) custom-call(f32[3,32,32,256]{3,2,1,0:T(8,128)S(1)} %get-tuple-element.51.refs_0_, f32[2,32,256]{2,1,0:T(8,128)S(1)} %get-tuple-element.54.refs_1_, f32[2,32,256]{2,1,0:T(8,128)S(1)} %get-tuple-element.55.refs_2_, ...), custom_call_target="tpu_custom_call" | custom-call | flops 10485760 | bytes 9437184 | tf_op jit(solution)/shard_map/hstep/pallas_call | solution.py:231
  24.6 0.0 collective-permute-done.4.gx_ref
  24.6 1.9 %collective-permute-done.5.gy_ref = f32[2,32,256]{2,1,0:T(8,128)S(1)} collective-permute-done((f32[2,32,256]{2,1,0:T(8,128)S(1)}, f32[2,32,256]{2,1,0:T(8,128)S(1)}, u32[]{:S(2)}, u32[]{:S(2)}) %collective-permute-start.5) | collective-permute-done | bytes 65568 | tf_op jit(solution)/shard_map/ppermute | solution.py:21
  26.5 4.3 %collective-permute-start.6 = (f32[2,32,256]{2,1,0:T(8,128)S(1)}, f32[2,32,256]{2,1,0:T(8,128)S(1)}, u32[]{:S(2)}, u32[]{:S(2)}) collective-permute-start(f32[2,32,256]{2,1,0:T(8,128)S(1)} %get-tuple-element.59.refs_4_.hl_ref), channel_id=1, source_target_pairs={{0,8},{8,16},{16,24},{24,32},{32,40},{40,48},{48,56},{56,64},{64,7... | collective-permute-start | bytes 196616 | tf_op jit(solution)/shard_map/ppermute | solution.py:21
  30.8 3.3 %collective-permute-start.7 = (f32[2,32,256]{2,1,0:T(8,128)S(1)}, f32[2,32,256]{2,1,0:T(8,128)S(1)}, u32[]{:S(2)}, u32[]{:S(2)}) collective-permute-start(f32[2,32,256]{2,1,0:T(8,128)S(1)} %get-tuple-element.60.refs_5_.hr_ref), channel_id=1, source_target_pairs={{0,1},{1,2},{2,3},{3,4},{4,5},{5,6},{6,7},{8,9},{9,10},{10,11},{11... | collective-permute-start | bytes 196616 | tf_op jit(solution)/shard_map/ppermute | solution.py:21
  34.2 0.0 copy-start.17
  34.2 2.7 %estep.3 = (f32[3,32,32,256]{3,2,1,0:T(8,128)}, f32[6,32,256]{2,1,0:T(8,128)S(1)}, f32[6,32,256]{2,1,0:T(8,128)S(1)}, f32[32,32,256]{2,1,0:T(8,128)S(1)}) custom-call(f32[3,32,32,256]{3,2,1,0:T(8,128)S(1)} %get-tuple-element.51.refs_0_, f32[2,32,256]{2,1,0:T(8,128)S(1)} %get-tuple-element.54.refs_1_, f32[2,32,256]{2,1,0:T(8,128)S(1)} %get-tuple-element.55.refs_2_, ...), custom_call_target="tpu_custom_call" | custom-call | flops 15728640 | bytes 11534336 | tf_op jit(solution)/shard_map/estep/pallas_call | solution.py:336
  36.9 0.0 copy-start.7
  36.9 0.0 copy-start.16
  36.9 0.0 copy-start.18
  37.0 0.0 collective-permute-done.6.gx_ref
  37.0 0.0 collective-permute-done.7.gy_ref
  37.0 1.8 %power.1 = (f32[128,8,256]{2,1,0:T(8,128)}, f32[2,32,256]{2,1,0:T(8,128)S(1)}, f32[2,32,256]{2,1,0:T(8,128)S(1)}) custom-call(s32[1,128]{1,0:T(1,128)S(1)} %copy-done.17, f32[32,32,256]{2,1,0:T(8,128)S(1)} %get-tuple-element.61.p_ref, f32[6,32,256]{2,1,0:T(8,128)S(1)} %get-tuple-element.62.layer_ref, f32[6,32,256]{2,1,0:T(8,128)S(1)} %get-tuple-element.63.rows_ref, ...), custom_call_target="tpu_custom_call" | custom-call | flops 1048576 | bytes 2097152 | tf_op jit(solution)/shard_map/power/pallas_call | solution.py:405
  38.8 13.1 %all-to-all-start = ((f32[128,8,256]{2,1,0:T(8,128)}), f32[128,8,256]{2,1,0:T(8,128)}, u32[]{:S(2)}, u32[]{:S(2)}) async-start(f32[128,8,256]{2,1,0:T(8,128)} %get-tuple-element.64), calls=%async_computation | async-start | bytes 2097152 | tf_op jit(solution)/shard_map/all_to_all | solution.py:662
  52.0 0.0 copy-start.9
  52.0 1.2 %copy-done.9 = f32[128,8,256]{2,1,0:T(8,128)S(1)} copy-done((f32[128,8,256]{2,1,0:T(8,128)S(1)}, f32[128,8,256]{2,1,0:T(8,128)}, u32[]{:S(2)}) %copy-start.9) | copy-done | bytes 1048600
  53.2 1.2 %copy-done.14 = s32[128,8,256]{2,1,0:T(8,128)S(1)} copy-done((s32[128,8,256]{2,1,0:T(8,128)S(1)}, s32[128,8,256]{2,1,0:T(8,128)}, u32[]{:S(2)}) %copy-start.14) | copy-done | bytes 1048600
  54.4 8.0 %pack.1.far_hbm = f32[128,40,256]{2,1,0:T(8,128)} custom-call(s32[1,128]{1,0:T(1,128)S(1)} %copy-done.18, f32[4,16]{1,0:T(4,128)S(1)} %copy-done.16, f32[128,8,256]{2,1,0:T(8,128)S(1)} %copy-done.7, f32[128,8,256]{2,1,0:T(8,128)S(1)} %copy-done.9, s32[128,8,256]{2,1,0:T(8,128)S(1)} %copy-done.14), custom_call_target="tpu_custom_call" | custom-call | flops 20971520 | bytes 9437184 | tf_op jit(solution)/shard_map/pack/pallas_call | solution.py:482
  62.4 8.4 %all-to-all-done.p_hbm.p_ref = f32[128,8,256]{2,1,0:T(8,128)} async-done(((f32[128,8,256]{2,1,0:T(8,128)}), f32[128,8,256]{2,1,0:T(8,128)}, u32[]{:S(2)}, u32[]{:S(2)}) %all-to-all-start) | async-done | bytes 1048608 | tf_op jit(solution)/shard_map/all_to_all | solution.py:662
  70.8 4.3 %thermal.1 = f32[128,16,256]{2,1,0:T(8,128)} custom-call(f32[128,8,256]{2,1,0:T(8,128)} %all-to-all-done.p_hbm.p_ref, f32[128,40,256]{2,1,0:T(8,128)} %pack.1.far_hbm), custom_call_target="tpu_custom_call" | custom-call | flops 10485760 | bytes 8388608 | tf_op jit(solution)/shard_map/thermal/pallas_call | solution.py:532
  75.1 0.0 copy-start.4
  75.1 5.8 %all-to-all-start.1 = ((f32[128,16,256]{2,1,0:T(8,128)}), f32[128,16,256]{2,1,0:T(8,128)}, u32[]{:S(2)}, u32[]{:S(2)}) async-start(f32[128,16,256]{2,1,0:T(8,128)} %thermal.1), calls=%async_computation.1 | async-start | bytes 4194304 | tf_op jit(solution)/shard_map/all_to_all | solution.py:662
  81.0 0.0 copy-start.12
  81.0 0.0 copy-start.15
  81.0 1.4 %copy-done.15 = s32[32,32,256]{2,1,0:T(8,128)S(1)} copy-done((s32[32,32,256]{2,1,0:T(8,128)S(1)}, s32[32,32,256]{2,1,0:T(8,128)}, u32[]{:S(2)}) %copy-start.15) | copy-done | bytes 1048600
  82.4 0.4 near.1.kept
  82.8 1.3 %copy-done.5 = f32[2,32,32,256]{3,2,1,0:T(8,128)} copy-done((f32[2,32,32,256]{3,2,1,0:T(8,128)}, f32[2,32,32,256]{3,2,1,0:T(8,128)S(1)}, u32[]{:S(2)}) %copy-start.5) | copy-done | bytes 2097176
  84.1 1.9 %copy-done.13 = f32[3,32,32,256]{3,2,1,0:T(8,128)S(1)} copy-done((f32[3,32,32,256]{3,2,1,0:T(8,128)S(1)}, f32[3,32,32,256]{3,2,1,0:T(8,128)}, u32[]{:S(2)}) %copy-start.13) | copy-done | bytes 3145752
  86.0 3.2 %flush.1 = (f32[3,32,32,256]{3,2,1,0:T(8,128)}, f32[3,32,32,256]{3,2,1,0:T(8,128)}) custom-call(f32[3,32,32,256]{3,2,1,0:T(8,128)S(1)} %copy-done.13, f32[2,32,256]{2,1,0:T(8,128)S(1)} %get-tuple-element.71.el_ref, f32[2,32,256]{2,1,0:T(8,128)S(1)} %get-tuple-element.72.er_ref, f32[3,32,32,256]{3,2,1,0:T(8,128)S(1)} %copy-done.12, ...), custom_call_target="tpu_custom_call" | custom-call | flops 786432 | bytes 12582912 | tf_op jit(solution)/shard_map/flush/pallas_call | solution.py:434
  89.2 6.1 %heat.1 = (f32[128,8,256]{2,1,0:T(8,128)}, f32[128,8,256]{2,1,0:T(8,128)}) custom-call(s32[1,128]{1,0:T(1,128)S(1)} %copy-done.18, f32[128,8,256]{2,1,0:T(8,128)} %all-to-all-done.p_hbm.p_ref, f32[128,8,256]{2,1,0:T(8,128)S(1)} %copy-done.8, f32[128,8,256]{2,1,0:T(8,128)S(1)} %copy-done.10), custom_call_target="tpu_custom_call" | custom-call | flops 10485760 | bytes 5242880 | tf_op jit(solution)/shard_map/heat/pallas_call | solution.py:571
  95.3 16.0 %all-to-all-done.1.recv_hbm = f32[128,16,256]{2,1,0:T(8,128)} async-done(((f32[128,16,256]{2,1,0:T(8,128)}), f32[128,16,256]{2,1,0:T(8,128)}, u32[]{:S(2)}, u32[]{:S(2)}) %all-to-all-start.1) | async-done | bytes 2097184 | tf_op jit(solution)/shard_map/all_to_all | solution.py:662
  111.3 3.0 %select.1 = (f32[32,32,256]{2,1,0:T(8,128)}, f32[32,32,256]{2,1,0:T(8,128)}) custom-call(s32[1,128]{1,0:T(1,128)S(1)} %copy-done.17, f32[128,16,256]{2,1,0:T(8,128)} %all-to-all-done.1.recv_hbm, f32[2,32,32,256]{3,2,1,0:T(8,128)S(1)} %copy-done.6), custom_call_target="tpu_custom_call" | custom-call | flops 1048576 | bytes 7340032 | tf_op jit(solution)/shard_map/select/pallas_call | solution.py:643
  (25 shorter events, 0.1 us)
Async XLA Ops:
  0.6 1.9 %copy-start = (f32[3,32,32,256]{3,2,1,0:T(8,128)S(1)}, f32[3,32,32,256]{3,2,1,0:T(8,128)}, u32[]{:S(2)}) copy-start(f32[3,32,32,256]{3,2,1,0:T(8,128)} %refs_0_.3) | copy-start | bytes 9437188
  2.5 5.1 %copy-start.1 = (f32[3,32,32,256]{3,2,1,0:T(8,128)S(1)}, f32[3,32,32,256]{3,2,1,0:T(8,128)}, u32[]{:S(2)}) copy-start(f32[3,32,32,256]{3,2,1,0:T(8,128)} %refs_0_.3) | copy-start | bytes 9437188
  2.5 5.2 %copy-start.11 = (f32[3,32,32,256]{3,2,1,0:T(8,128)S(1)}, f32[3,32,32,256]{3,2,1,0:T(8,128)}, u32[]{:S(2)}) copy-start(f32[3,32,32,256]{3,2,1,0:T(8,128)} %refs_1_.1) | copy-start | bytes 9437188
  2.6 6.1 %collective-permute-start = (f32[2,32,256]{2,1,0:T(8,128)S(1)}, f32[2,32,256]{2,1,0:T(8,128)S(1)}, u32[]{:S(2)}, u32[]{:S(2)}) collective-permute-start(f32[2,32,256]{2,1,0:T(8,128)S(1)} %get-tuple-element.47), channel_id=1, source_target_pairs={{8,0},{16,8},{24,16},{32,24},{40,32},{48,40},{56,48},{64,56},{72,6... | collective-permute-start | bytes 196616 | tf_op jit(solution)/shard_map/ppermute | solution.py:21
  4.2 13.5 %copy-start.2 = (f32[32,32,256]{2,1,0:T(8,128)S(1)}, f32[32,32,256]{2,1,0:T(8,128)}, u32[]{:S(2)}) copy-start(f32[32,32,256]{2,1,0:T(8,128)} %eps_ref.1) | copy-start | bytes 3145732
  4.2 13.5 %copy-start.3 = (f32[32,32,256]{2,1,0:T(8,128)S(1)}, f32[32,32,256]{2,1,0:T(8,128)}, u32[]{:S(2)}) copy-start(f32[32,32,256]{2,1,0:T(8,128)} %sig_ref.1) | copy-start | bytes 3145732
  4.2 7.0 %collective-permute-start.1 = (f32[2,32,256]{2,1,0:T(8,128)S(1)}, f32[2,32,256]{2,1,0:T(8,128)S(1)}, u32[]{:S(2)}, u32[]{:S(2)}) collective-permute-start(f32[2,32,256]{2,1,0:T(8,128)S(1)} %get-tuple-element.48), channel_id=1, source_target_pairs={{1,0},{2,1},{3,2},{4,3},{5,4},{6,5},{7,6},{9,8},{10,9},{11,10},{12... | collective-permute-start | bytes 196616 | tf_op jit(solution)/shard_map/ppermute | solution.py:21
  11.2 7.9 %collective-permute-start.2 = (f32[2,32,256]{2,1,0:T(8,128)S(1)}, f32[2,32,256]{2,1,0:T(8,128)S(1)}, u32[]{:S(2)}, u32[]{:S(2)}) collective-permute-start(f32[2,32,256]{2,1,0:T(8,128)S(1)} %get-tuple-element.49.refs_2_.refs_4_), channel_id=1, source_target_pairs={{0,8},{8,16},{16,24},{24,32},{32,40},{40,48},{48,56},{56,64},{64,7... | collective-permute-start | bytes 196616 | tf_op jit(solution)/shard_map/ppermute | solution.py:21
  15.5 3.6 %collective-permute-start.3 = (f32[2,32,256]{2,1,0:T(8,128)S(1)}, f32[2,32,256]{2,1,0:T(8,128)S(1)}, u32[]{:S(2)}, u32[]{:S(2)}) collective-permute-start(f32[2,32,256]{2,1,0:T(8,128)S(1)} %get-tuple-element.50.refs_3_.refs_5_), channel_id=1, source_target_pairs={{0,1},{1,2},{2,3},{3,4},{4,5},{5,6},{6,7},{8,9},{9,10},{10,11},{11... | collective-permute-start | bytes 196616 | tf_op jit(solution)/shard_map/ppermute | solution.py:21
  19.2 5.5 %collective-permute-start.4 = (f32[2,32,256]{2,1,0:T(8,128)S(1)}, f32[2,32,256]{2,1,0:T(8,128)S(1)}, u32[]{:S(2)}, u32[]{:S(2)}) collective-permute-start(f32[2,32,256]{2,1,0:T(8,128)S(1)} %get-tuple-element.54.refs_1_), channel_id=1, source_target_pairs={{8,0},{16,8},{24,16},{32,24},{40,32},{48,40},{56,48},{64,56},{72,6... | collective-permute-start | bytes 196616 | tf_op jit(solution)/shard_map/ppermute | solution.py:21
  20.5 6.1 %collective-permute-start.5 = (f32[2,32,256]{2,1,0:T(8,128)S(1)}, f32[2,32,256]{2,1,0:T(8,128)S(1)}, u32[]{:S(2)}, u32[]{:S(2)}) collective-permute-start(f32[2,32,256]{2,1,0:T(8,128)S(1)} %get-tuple-element.55.refs_2_), channel_id=1, source_target_pairs={{1,0},{2,1},{3,2},{4,3},{5,4},{6,5},{7,6},{9,8},{10,9},{11,10},{12... | collective-permute-start | bytes 196616 | tf_op jit(solution)/shard_map/ppermute | solution.py:21
  26.5 10.4 %collective-permute-start.6 = (f32[2,32,256]{2,1,0:T(8,128)S(1)}, f32[2,32,256]{2,1,0:T(8,128)S(1)}, u32[]{:S(2)}, u32[]{:S(2)}) collective-permute-start(f32[2,32,256]{2,1,0:T(8,128)S(1)} %get-tuple-element.59.refs_4_.hl_ref), channel_id=1, source_target_pairs={{0,8},{8,16},{16,24},{24,32},{32,40},{40,48},{48,56},{56,64},{64,7... | collective-permute-start | bytes 196616 | tf_op jit(solution)/shard_map/ppermute | solution.py:21
  30.8 6.2 %collective-permute-start.7 = (f32[2,32,256]{2,1,0:T(8,128)S(1)}, f32[2,32,256]{2,1,0:T(8,128)S(1)}, u32[]{:S(2)}, u32[]{:S(2)}) collective-permute-start(f32[2,32,256]{2,1,0:T(8,128)S(1)} %get-tuple-element.60.refs_5_.hr_ref), channel_id=1, source_target_pairs={{0,1},{1,2},{2,3},{3,4},{4,5},{5,6},{6,7},{8,9},{9,10},{10,11},{11... | collective-permute-start | bytes 196616 | tf_op jit(solution)/shard_map/ppermute | solution.py:21
  34.2 2.8 %copy-start.17 = (s32[1,128]{1,0:T(1,128)S(1)}, s32[1,128]{1,0:T(1,128)}, u32[]{:S(2)}) copy-start(s32[1,128]{1,0:T(1,128)} %dest.3) | copy-start | bytes 1540
  36.9 15.0 %copy-start.7 = (f32[128,8,256]{2,1,0:T(8,128)S(1)}, f32[128,8,256]{2,1,0:T(8,128)}, u32[]{:S(2)}) copy-start(f32[128,8,256]{2,1,0:T(8,128)} %t_ref.2) | copy-start | bytes 3145732
  36.9 15.0 %copy-start.16 = (f32[4,16]{1,0:T(4,128)S(1)}, f32[4,16]{1,0:T(4,128)}, u32[]{:S(2)}) copy-start(f32[4,16]{1,0:T(4,128)} %lines.1) | copy-start | bytes 772
  36.9 15.0 %copy-start.18 = (s32[1,128]{1,0:T(1,128)S(1)}, s32[1,128]{1,0:T(1,128)}, u32[]{:S(2)}) copy-start(s32[1,128]{1,0:T(1,128)} %arrive.3) | copy-start | bytes 1540
  38.8 32.1 %all-to-all-start = ((f32[128,8,256]{2,1,0:T(8,128)}), f32[128,8,256]{2,1,0:T(8,128)}, u32[]{:S(2)}, u32[]{:S(2)}) async-start(f32[128,8,256]{2,1,0:T(8,128)} %get-tuple-element.64), calls=%async_computation | async-start | bytes 2097152 | tf_op jit(solution)/shard_map/all_to_all | solution.py:662
  52.0 1.2 %copy-start.9 = (f32[128,8,256]{2,1,0:T(8,128)S(1)}, f32[128,8,256]{2,1,0:T(8,128)}, u32[]{:S(2)}) copy-start(f32[128,8,256]{2,1,0:T(8,128)} %w_ref.2) | copy-start | bytes 3145732
  53.2 1.2 %copy-start.14 = (s32[128,8,256]{2,1,0:T(8,128)S(1)}, s32[128,8,256]{2,1,0:T(8,128)}, u32[]{:S(2)}) copy-start(s32[128,8,256]{2,1,0:T(8,128)} %c_ref) | copy-start | bytes 3145732
  75.1 5.9 %copy-start.4 = (f32[32,32,256]{2,1,0:T(8,128)S(1)}, f32[32,32,256]{2,1,0:T(8,128)}, u32[]{:S(2)}) copy-start(f32[32,32,256]{2,1,0:T(8,128)} %sig_ref.1) | copy-start | bytes 3145732
  75.1 36.1 %all-to-all-start.1 = ((f32[128,16,256]{2,1,0:T(8,128)}), f32[128,16,256]{2,1,0:T(8,128)}, u32[]{:S(2)}, u32[]{:S(2)}) async-start(f32[128,16,256]{2,1,0:T(8,128)} %thermal.1), calls=%async_computation.1 | async-start | bytes 4194304 | tf_op jit(solution)/shard_map/all_to_all | solution.py:662
  81.0 3.1 %copy-start.12 = (f32[3,32,32,256]{3,2,1,0:T(8,128)S(1)}, f32[3,32,32,256]{3,2,1,0:T(8,128)}, u32[]{:S(2)}) copy-start(f32[3,32,32,256]{3,2,1,0:T(8,128)} %get-tuple-element.73.h_ref) | copy-start | bytes 9437188
  81.0 1.4 %copy-start.15 = (s32[32,32,256]{2,1,0:T(8,128)S(1)}, s32[32,32,256]{2,1,0:T(8,128)}, u32[]{:S(2)}) copy-start(s32[32,32,256]{2,1,0:T(8,128)} %lab_ref) | copy-start | bytes 3145732
  82.8 1.3 %copy-start.5 = (f32[2,32,32,256]{3,2,1,0:T(8,128)}, f32[2,32,32,256]{3,2,1,0:T(8,128)S(1)}, u32[]{:S(2)}) copy-start(f32[2,32,32,256]{3,2,1,0:T(8,128)S(1)} %near.1.kept) | copy-start | bytes 6291460
  84.1 1.9 %copy-start.13 = (f32[3,32,32,256]{3,2,1,0:T(8,128)S(1)}, f32[3,32,32,256]{3,2,1,0:T(8,128)}, u32[]{:S(2)}) copy-start(f32[3,32,32,256]{3,2,1,0:T(8,128)} %get-tuple-element.70.e_ref) | copy-start | bytes 9437188
  86.0 3.2 %copy-start.8 = (f32[128,8,256]{2,1,0:T(8,128)S(1)}, f32[128,8,256]{2,1,0:T(8,128)}, u32[]{:S(2)}) copy-start(f32[128,8,256]{2,1,0:T(8,128)} %t_ref.2) | copy-start | bytes 3145732
  86.0 3.2 %copy-start.10 = (f32[128,8,256]{2,1,0:T(8,128)S(1)}, f32[128,8,256]{2,1,0:T(8,128)}, u32[]{:S(2)}) copy-start(f32[128,8,256]{2,1,0:T(8,128)} %w_ref.2) | copy-start | bytes 3145732
  89.2 22.1 %copy-start.6 = (f32[2,32,32,256]{3,2,1,0:T(8,128)S(1)}, f32[2,32,32,256]{3,2,1,0:T(8,128)}, u32[]{:S(2)}) copy-start(f32[2,32,32,256]{3,2,1,0:T(8,128)} %copy-done.5) | copy-start | bytes 6291460

commit v4 on v3

--- a/solution.py
+++ b/solution.py
@@ -394,7 +394,7 @@
             out_ref[dest[0, x * parts + part]] = p_ref[x, part * 8 : part * 8 + 8, :]
         return carry
 
-    lax.fori_loop(1, nx, body, 0, unroll=2)
+    lax.fori_loop(1, nx, body, 0, unroll=8)
     move = pltpu.make_async_copy(out_ref, out_hbm, sem)
     move.start()
     move.wait()
@@ -518,7 +518,7 @@
     for chunk in range(chunks):
         for move in loads[chunk]:
             move.wait()
-        lax.fori_loop(chunk * size, (chunk + 1) * size, body, 0, unroll=4)
+        lax.fori_loop(chunk * size, (chunk + 1) * size, body, 0, unroll=16)
         for move in stores[chunk]:
             move.start()
     for group in stores:
@@ -614,7 +614,7 @@
             pltpu.make_async_copy(recv_hbm.at[dest[0, k]], recv.at[k], recv_sem.at[chunk]).start()
             return carry
 
-        lax.fori_loop(chunk * group, (chunk + 1) * group, fetch, 0, unroll=8)
+        lax.fori_loop(chunk * group, (chunk + 1) * group, fetch, 0, unroll=16)
 
     def body(x, carry):
         for part in range(parts):
@@ -628,7 +628,7 @@
     for chunk in range(chunks):
         block = pl.ds(chunk * group, group)
         pltpu.make_async_copy(recv_hbm.at[block], recv.at[block], recv_sem.at[chunk]).wait()
-        lax.fori_loop(chunk * size, (chunk + 1) * size, body, 0, unroll=2)
+        lax.fori_loop(chunk * size, (chunk + 1) * size, body, 0, unroll=4)
         for move in stores[chunk]:
             move.start()
     for moves in stores:

time: 115 us -> 115 us (level)
  no operation moved by 1% of the time
where the time goes in v4:
time: 115 us; the launch traced here: 114 us
  starting transfers between devices  41.5 us (36%)
  Pallas kernels  34 us (30%)
  waiting for transfers between devices  28.8 us (25%)
  local copies, waits for them, and re-layouts  8.98 us (8%)
    all_to_all x2, waiting for transfers between devices, exchange(): lax.all_to_all(value, ('gx', 'gy'), split_axis=0, concat_axis=0, tiled=True)  24.4 us
    ppermute x8, starting transfers between devices, passed_along(): return lax.ppermute(value, axis, pairs)  22.5 us
    all_to_all x2, starting transfers between devices, exchange(): lax.all_to_all(value, ('gx', 'gy'), split_axis=0, concat_axis=0, tiled=True)  19 us
    unnamed x38, local copies, waits for them, and re-layouts  8.98 us
    pallas_call x1, Pallas kernels, pack(): pl.pallas_call(pack_kernel, grid=(steps,), in_specs=[smem_spec(), smem_sp...  8.03 us
    pallas_call x1, Pallas kernels, heat(): pl.pallas_call(heat_kernel, in_specs=[smem_spec()] + dense(3), out_specs=...  6.08 us
    ppermute x8, waiting for transfers between devices, passed_along(): return lax.ppermute(value, axis, pairs)  4.4 us
    pallas_call x1, Pallas kernels, thermal(): pl.pallas_call(thermal_kernel, in_specs=[hbm_spec(), hbm_spec()] + dense(...  4.26 us
  transfers between devices with their start and end apart: 10, of which 4 were waited for; matrix products, arithmetic and copies ran while one was open for 0% of the time, Pallas kernels for 22%

profile of v4, /device:TPU:1, one launch (start us, length us, event | category | flops | bytes accessed | tf_op | source)
XLA Modules:
  0.0 114.2 jit_solution(14273796502439529291)
XLA Ops:
  0.6 1.9 %copy-done = f32[3,32,32,256]{3,2,1,0:T(8,128)S(1)} copy-done((f32[3,32,32,256]{3,2,1,0:T(8,128)S(1)}, f32[3,32,32,256]{3,2,1,0:T(8,128)}, u32[]{:S(2)}) %copy-start) | copy-done | bytes 3145752
  2.5 0.1 halo.1
  2.6 1.6 %collective-permute-start = (f32[2,32,256]{2,1,0:T(8,128)S(1)}, f32[2,32,256]{2,1,0:T(8,128)S(1)}, u32[]{:S(2)}, u32[]{:S(2)}) collective-permute-start(f32[2,32,256]{2,1,0:T(8,128)S(1)} %get-tuple-element.47), channel_id=1, source_target_pairs={{8,0},{16,8},{24,16},{32,24},{40,32},{48,40},{56,48},{64,56},{72,6... | collective-permute-start | bytes 196616 | tf_op jit(solution)/shard_map/ppermute | solution.py:21
  4.2 0.0 copy-start.2
  4.2 0.0 copy-start.3
  4.2 3.5 %collective-permute-start.1 = (f32[2,32,256]{2,1,0:T(8,128)S(1)}, f32[2,32,256]{2,1,0:T(8,128)S(1)}, u32[]{:S(2)}, u32[]{:S(2)}) collective-permute-start(f32[2,32,256]{2,1,0:T(8,128)S(1)} %get-tuple-element.48), channel_id=1, source_target_pairs={{1,0},{2,1},{3,2},{4,3},{5,4},{6,5},{7,6},{9,8},{10,9},{11,10},{12... | collective-permute-start | bytes 196616 | tf_op jit(solution)/shard_map/ppermute | solution.py:21
  7.7 1.0 hstep.2
  8.7 0.0 collective-permute-done.gx_ref
  8.7 2.5 %collective-permute-done.1.gy_ref = f32[2,32,256]{2,1,0:T(8,128)S(1)} collective-permute-done((f32[2,32,256]{2,1,0:T(8,128)S(1)}, f32[2,32,256]{2,1,0:T(8,128)S(1)}, u32[]{:S(2)}, u32[]{:S(2)}) %collective-permute-start.1) | collective-permute-done | bytes 65568 | tf_op jit(solution)/shard_map/ppermute | solution.py:21
  11.2 4.3 %collective-permute-start.2 = (f32[2,32,256]{2,1,0:T(8,128)S(1)}, f32[2,32,256]{2,1,0:T(8,128)S(1)}, u32[]{:S(2)}, u32[]{:S(2)}) collective-permute-start(f32[2,32,256]{2,1,0:T(8,128)S(1)} %get-tuple-element.49.refs_2_.refs_4_), channel_id=1, source_target_pairs={{0,8},{8,16},{16,24},{24,32},{32,40},{40,48},{48,56},{56,64},{64,7... | collective-permute-start | bytes 196616 | tf_op jit(solution)/shard_map/ppermute | solution.py:21
  15.5 2.1 %collective-permute-start.3 = (f32[2,32,256]{2,1,0:T(8,128)S(1)}, f32[2,32,256]{2,1,0:T(8,128)S(1)}, u32[]{:S(2)}, u32[]{:S(2)}) collective-permute-start(f32[2,32,256]{2,1,0:T(8,128)S(1)} %get-tuple-element.50.refs_3_.refs_5_), channel_id=1, source_target_pairs={{0,1},{1,2},{2,3},{3,4},{4,5},{5,6},{6,7},{8,9},{9,10},{10,11},{11... | collective-permute-start | bytes 196616 | tf_op jit(solution)/shard_map/ppermute | solution.py:21
  17.7 1.4 %estep.2 = (f32[3,32,32,256]{3,2,1,0:T(8,128)S(1)}, f32[3,32,256]{2,1,0:T(8,128)S(1)}, f32[3,32,256]{2,1,0:T(8,128)S(1)}) custom-call(f32[3,32,32,256]{3,2,1,0:T(8,128)S(1)} %copy-done.1, f32[3,32,32,256]{3,2,1,0:T(8,128)S(1)} %get-tuple-element.44.refs_1_.refs_3_, f32[2,32,256]{2,1,0:T(8,128)S(1)} %get-tuple-element.49.refs_2_.refs_4_, ...), custom_call_target="tpu_custom_call" | custom-call | flops 15728640 | bytes 11534336 | tf_op jit(solution)/shard_map/estep/pallas_call | solution.py:336
  19.1 0.0 collective-permute-done.2.gx_ref
  19.1 0.0 collective-permute-done.3.gy_ref
  19.2 1.3 %collective-permute-start.4 = (f32[2,32,256]{2,1,0:T(8,128)S(1)}, f32[2,32,256]{2,1,0:T(8,128)S(1)}, u32[]{:S(2)}, u32[]{:S(2)}) collective-permute-start(f32[2,32,256]{2,1,0:T(8,128)S(1)} %get-tuple-element.54.refs_1_), channel_id=1, source_target_pairs={{8,0},{16,8},{24,16},{32,24},{40,32},{48,40},{56,48},{64,56},{72,6... | collective-permute-start | bytes 196616 | tf_op jit(solution)/shard_map/ppermute | solution.py:21
  20.5 2.2 %collective-permute-start.5 = (f32[2,32,256]{2,1,0:T(8,128)S(1)}, f32[2,32,256]{2,1,0:T(8,128)S(1)}, u32[]{:S(2)}, u32[]{:S(2)}) collective-permute-start(f32[2,32,256]{2,1,0:T(8,128)S(1)} %get-tuple-element.55.refs_2_), channel_id=1, source_target_pairs={{1,0},{2,1},{3,2},{4,3},{5,4},{6,5},{7,6},{9,8},{10,9},{11,10},{12... | collective-permute-start | bytes 196616 | tf_op jit(solution)/shard_map/ppermute | solution.py:21
  22.6 2.0 %hstep.3 = (f32[3,32,32,256]{3,2,1,0:T(8,128)S(1)}, f32[2,32,256]{2,1,0:T(8,128)S(1)}, f32[2,32,256]{2,1,0:T(8,128)S(1)}, f32[3,32,32,256]{3,2,1,0:T(8,128)}) custom-call(f32[3,32,32,256]{3,2,1,0:T(8,128)S(1)} %get-tuple-element.51.refs_0_, f32[2,32,256]{2,1,0:T(8,128)S(1)} %get-tuple-element.54.refs_1_, f32[2,32,256]{2,1,0:T(8,128)S(1)} %get-tuple-element.55.refs_2_, ...), custom_call_target="tpu_custom_call" | custom-call | flops 10485760 | bytes 9437184 | tf_op jit(solution)/shard_map/hstep/pallas_call | solution.py:231
  24.6 0.0 collective-permute-done.4.gx_ref
  24.6 1.9 %collective-permute-done.5.gy_ref = f32[2,32,256]{2,1,0:T(8,128)S(1)} collective-permute-done((f32[2,32,256]{2,1,0:T(8,128)S(1)}, f32[2,32,256]{2,1,0:T(8,128)S(1)}, u32[]{:S(2)}, u32[]{:S(2)}) %collective-permute-start.5) | collective-permute-done | bytes 65568 | tf_op jit(solution)/shard_map/ppermute | solution.py:21
  26.5 4.3 %collective-permute-start.6 = (f32[2,32,256]{2,1,0:T(8,128)S(1)}, f32[2,32,256]{2,1,0:T(8,128)S(1)}, u32[]{:S(2)}, u32[]{:S(2)}) collective-permute-start(f32[2,32,256]{2,1,0:T(8,128)S(1)} %get-tuple-element.59.refs_4_.hl_ref), channel_id=1, source_target_pairs={{0,8},{8,16},{16,24},{24,32},{32,40},{40,48},{48,56},{56,64},{64,7... | collective-permute-start | bytes 196616 | tf_op jit(solution)/shard_map/ppermute | solution.py:21
  30.8 3.3 %collective-permute-start.7 = (f32[2,32,256]{2,1,0:T(8,128)S(1)}, f32[2,32,256]{2,1,0:T(8,128)S(1)}, u32[]{:S(2)}, u32[]{:S(2)}) collective-permute-start(f32[2,32,256]{2,1,0:T(8,128)S(1)} %get-tuple-element.60.refs_5_.hr_ref), channel_id=1, source_target_pairs={{0,1},{1,2},{2,3},{3,4},{4,5},{5,6},{6,7},{8,9},{9,10},{10,11},{11... | collective-permute-start | bytes 196616 | tf_op jit(solution)/shard_map/ppermute | solution.py:21
  34.2 0.0 copy-start.17
  34.2 2.7 %estep.3 = (f32[3,32,32,256]{3,2,1,0:T(8,128)}, f32[6,32,256]{2,1,0:T(8,128)S(1)}, f32[6,32,256]{2,1,0:T(8,128)S(1)}, f32[32,32,256]{2,1,0:T(8,128)S(1)}) custom-call(f32[3,32,32,256]{3,2,1,0:T(8,128)S(1)} %get-tuple-element.51.refs_0_, f32[2,32,256]{2,1,0:T(8,128)S(1)} %get-tuple-element.54.refs_1_, f32[2,32,256]{2,1,0:T(8,128)S(1)} %get-tuple-element.55.refs_2_, ...), custom_call_target="tpu_custom_call" | custom-call | flops 15728640 | bytes 11534336 | tf_op jit(solution)/shard_map/estep/pallas_call | solution.py:336
  36.9 0.0 copy-start.7
  36.9 0.0 copy-start.16
  36.9 0.0 copy-start.18
  37.0 0.0 collective-permute-done.6.gx_ref
  37.0 0.0 collective-permute-done.7.gy_ref
  37.0 1.8 %power.1 = (f32[128,8,256]{2,1,0:T(8,128)}, f32[2,32,256]{2,1,0:T(8,128)S(1)}, f32[2,32,256]{2,1,0:T(8,128)S(1)}) custom-call(s32[1,128]{1,0:T(1,128)S(1)} %copy-done.17, f32[32,32,256]{2,1,0:T(8,128)S(1)} %get-tuple-element.61.p_ref, f32[6,32,256]{2,1,0:T(8,128)S(1)} %get-tuple-element.62.layer_ref, f32[6,32,256]{2,1,0:T(8,128)S(1)} %get-tuple-element.63.rows_ref, ...), custom_call_target="tpu_custom_call" | custom-call | flops 1048576 | bytes 2097152 | tf_op jit(solution)/shard_map/power/pallas_call | solution.py:405
  38.8 13.1 %all-to-all-start = ((f32[128,8,256]{2,1,0:T(8,128)}), f32[128,8,256]{2,1,0:T(8,128)}, u32[]{:S(2)}, u32[]{:S(2)}) async-start(f32[128,8,256]{2,1,0:T(8,128)} %get-tuple-element.64), calls=%async_computation | async-start | bytes 2097152 | tf_op jit(solution)/shard_map/all_to_all | solution.py:662
  52.0 0.0 copy-start.9
  52.0 1.2 %copy-done.9 = f32[128,8,256]{2,1,0:T(8,128)S(1)} copy-done((f32[128,8,256]{2,1,0:T(8,128)S(1)}, f32[128,8,256]{2,1,0:T(8,128)}, u32[]{:S(2)}) %copy-start.9) | copy-done | bytes 1048600
  53.2 1.2 %copy-done.14 = s32[128,8,256]{2,1,0:T(8,128)S(1)} copy-done((s32[128,8,256]{2,1,0:T(8,128)S(1)}, s32[128,8,256]{2,1,0:T(8,128)}, u32[]{:S(2)}) %copy-start.14) | copy-done | bytes 1048600
  54.4 8.0 %pack.1.far_hbm = f32[128,40,256]{2,1,0:T(8,128)} custom-call(s32[1,128]{1,0:T(1,128)S(1)} %copy-done.18, f32[4,16]{1,0:T(4,128)S(1)} %copy-done.16, f32[128,8,256]{2,1,0:T(8,128)S(1)} %copy-done.7, f32[128,8,256]{2,1,0:T(8,128)S(1)} %copy-done.9, s32[128,8,256]{2,1,0:T(8,128)S(1)} %copy-done.14), custom_call_target="tpu_custom_call" | custom-call | flops 20971520 | bytes 9437184 | tf_op jit(solution)/shard_map/pack/pallas_call | solution.py:482
  62.4 8.4 %all-to-all-done.p_hbm.p_ref = f32[128,8,256]{2,1,0:T(8,128)} async-done(((f32[128,8,256]{2,1,0:T(8,128)}), f32[128,8,256]{2,1,0:T(8,128)}, u32[]{:S(2)}, u32[]{:S(2)}) %all-to-all-start) | async-done | bytes 1048608 | tf_op jit(solution)/shard_map/all_to_all | solution.py:662
  70.8 4.3 %thermal.1 = f32[128,16,256]{2,1,0:T(8,128)} custom-call(f32[128,8,256]{2,1,0:T(8,128)} %all-to-all-done.p_hbm.p_ref, f32[128,40,256]{2,1,0:T(8,128)} %pack.1.far_hbm), custom_call_target="tpu_custom_call" | custom-call | flops 10485760 | bytes 8388608 | tf_op jit(solution)/shard_map/thermal/pallas_call | solution.py:532
  75.1 0.0 copy-start.4
  75.1 5.8 %all-to-all-start.1 = ((f32[128,16,256]{2,1,0:T(8,128)}), f32[128,16,256]{2,1,0:T(8,128)}, u32[]{:S(2)}, u32[]{:S(2)}) async-start(f32[128,16,256]{2,1,0:T(8,128)} %thermal.1), calls=%async_computation.1 | async-start | bytes 4194304 | tf_op jit(solution)/shard_map/all_to_all | solution.py:662
  81.0 0.0 copy-start.12
  81.0 0.0 copy-start.15
  81.0 1.4 %copy-done.15 = s32[32,32,256]{2,1,0:T(8,128)S(1)} copy-done((s32[32,32,256]{2,1,0:T(8,128)S(1)}, s32[32,32,256]{2,1,0:T(8,128)}, u32[]{:S(2)}) %copy-start.15) | copy-done | bytes 1048600
  82.4 0.4 near.1.kept
  82.7 1.3 %copy-done.5 = f32[2,32,32,256]{3,2,1,0:T(8,128)} copy-done((f32[2,32,32,256]{3,2,1,0:T(8,128)}, f32[2,32,32,256]{3,2,1,0:T(8,128)S(1)}, u32[]{:S(2)}) %copy-start.5) | copy-done | bytes 2097176
  84.1 1.9 %copy-done.13 = f32[3,32,32,256]{3,2,1,0:T(8,128)S(1)} copy-done((f32[3,32,32,256]{3,2,1,0:T(8,128)S(1)}, f32[3,32,32,256]{3,2,1,0:T(8,128)}, u32[]{:S(2)}) %copy-start.13) | copy-done | bytes 3145752
  86.0 3.2 %flush.1 = (f32[3,32,32,256]{3,2,1,0:T(8,128)}, f32[3,32,32,256]{3,2,1,0:T(8,128)}) custom-call(f32[3,32,32,256]{3,2,1,0:T(8,128)S(1)} %copy-done.13, f32[2,32,256]{2,1,0:T(8,128)S(1)} %get-tuple-element.71.el_ref, f32[2,32,256]{2,1,0:T(8,128)S(1)} %get-tuple-element.72.er_ref, f32[3,32,32,256]{3,2,1,0:T(8,128)S(1)} %copy-done.12, ...), custom_call_target="tpu_custom_call" | custom-call | flops 786432 | bytes 12582912 | tf_op jit(solution)/shard_map/flush/pallas_call | solution.py:434
  89.2 6.1 %heat.1 = (f32[128,8,256]{2,1,0:T(8,128)}, f32[128,8,256]{2,1,0:T(8,128)}) custom-call(s32[1,128]{1,0:T(1,128)S(1)} %copy-done.18, f32[128,8,256]{2,1,0:T(8,128)} %all-to-all-done.p_hbm.p_ref, f32[128,8,256]{2,1,0:T(8,128)S(1)} %copy-done.8, f32[128,8,256]{2,1,0:T(8,128)S(1)} %copy-done.10), custom_call_target="tpu_custom_call" | custom-call | flops 10485760 | bytes 5242880 | tf_op jit(solution)/shard_map/heat/pallas_call | solution.py:571
  95.3 16.0 %all-to-all-done.1.recv_hbm = f32[128,16,256]{2,1,0:T(8,128)} async-done(((f32[128,16,256]{2,1,0:T(8,128)}), f32[128,16,256]{2,1,0:T(8,128)}, u32[]{:S(2)}, u32[]{:S(2)}) %all-to-all-start.1) | async-done | bytes 2097184 | tf_op jit(solution)/shard_map/all_to_all | solution.py:662
  111.2 3.0 %select.1 = (f32[32,32,256]{2,1,0:T(8,128)}, f32[32,32,256]{2,1,0:T(8,128)}) custom-call(s32[1,128]{1,0:T(1,128)S(1)} %copy-done.17, f32[128,16,256]{2,1,0:T(8,128)} %all-to-all-done.1.recv_hbm, f32[2,32,32,256]{3,2,1,0:T(8,128)S(1)} %copy-done.6), custom_call_target="tpu_custom_call" | custom-call | flops 1048576 | bytes 7340032 | tf_op jit(solution)/shard_map/select/pallas_call | solution.py:643
  (25 shorter events, 0.1 us)
Async XLA Ops:
  0.6 1.9 %copy-start = (f32[3,32,32,256]{3,2,1,0:T(8,128)S(1)}, f32[3,32,32,256]{3,2,1,0:T(8,128)}, u32[]{:S(2)}) copy-start(f32[3,32,32,256]{3,2,1,0:T(8,128)} %refs_0_.3) | copy-start | bytes 9437188
  2.5 5.1 %copy-start.1 = (f32[3,32,32,256]{3,2,1,0:T(8,128)S(1)}, f32[3,32,32,256]{3,2,1,0:T(8,128)}, u32[]{:S(2)}) copy-start(f32[3,32,32,256]{3,2,1,0:T(8,128)} %refs_0_.3) | copy-start | bytes 9437188
  2.5 5.2 %copy-start.11 = (f32[3,32,32,256]{3,2,1,0:T(8,128)S(1)}, f32[3,32,32,256]{3,2,1,0:T(8,128)}, u32[]{:S(2)}) copy-start(f32[3,32,32,256]{3,2,1,0:T(8,128)} %refs_1_.1) | copy-start | bytes 9437188
  2.6 6.1 %collective-permute-start = (f32[2,32,256]{2,1,0:T(8,128)S(1)}, f32[2,32,256]{2,1,0:T(8,128)S(1)}, u32[]{:S(2)}, u32[]{:S(2)}) collective-permute-start(f32[2,32,256]{2,1,0:T(8,128)S(1)} %get-tuple-element.47), channel_id=1, source_target_pairs={{8,0},{16,8},{24,16},{32,24},{40,32},{48,40},{56,48},{64,56},{72,6... | collective-permute-start | bytes 196616 | tf_op jit(solution)/shard_map/ppermute | solution.py:21
  4.2 13.5 %copy-start.2 = (f32[32,32,256]{2,1,0:T(8,128)S(1)}, f32[32,32,256]{2,1,0:T(8,128)}, u32[]{:S(2)}) copy-start(f32[32,32,256]{2,1,0:T(8,128)} %eps_ref.1) | copy-start | bytes 3145732
  4.2 13.5 %copy-start.3 = (f32[32,32,256]{2,1,0:T(8,128)S(1)}, f32[32,32,256]{2,1,0:T(8,128)}, u32[]{:S(2)}) copy-start(f32[32,32,256]{2,1,0:T(8,128)} %sig_ref.1) | copy-start | bytes 3145732
  4.2 7.0 %collective-permute-start.1 = (f32[2,32,256]{2,1,0:T(8,128)S(1)}, f32[2,32,256]{2,1,0:T(8,128)S(1)}, u32[]{:S(2)}, u32[]{:S(2)}) collective-permute-start(f32[2,32,256]{2,1,0:T(8,128)S(1)} %get-tuple-element.48), channel_id=1, source_target_pairs={{1,0},{2,1},{3,2},{4,3},{5,4},{6,5},{7,6},{9,8},{10,9},{11,10},{12... | collective-permute-start | bytes 196616 | tf_op jit(solution)/shard_map/ppermute | solution.py:21
  11.2 7.9 %collective-permute-start.2 = (f32[2,32,256]{2,1,0:T(8,128)S(1)}, f32[2,32,256]{2,1,0:T(8,128)S(1)}, u32[]{:S(2)}, u32[]{:S(2)}) collective-permute-start(f32[2,32,256]{2,1,0:T(8,128)S(1)} %get-tuple-element.49.refs_2_.refs_4_), channel_id=1, source_target_pairs={{0,8},{8,16},{16,24},{24,32},{32,40},{40,48},{48,56},{56,64},{64,7... | collective-permute-start | bytes 196616 | tf_op jit(solution)/shard_map/ppermute | solution.py:21
  15.5 3.6 %collective-permute-start.3 = (f32[2,32,256]{2,1,0:T(8,128)S(1)}, f32[2,32,256]{2,1,0:T(8,128)S(1)}, u32[]{:S(2)}, u32[]{:S(2)}) collective-permute-start(f32[2,32,256]{2,1,0:T(8,128)S(1)} %get-tuple-element.50.refs_3_.refs_5_), channel_id=1, source_target_pairs={{0,1},{1,2},{2,3},{3,4},{4,5},{5,6},{6,7},{8,9},{9,10},{10,11},{11... | collective-permute-start | bytes 196616 | tf_op jit(solution)/shard_map/ppermute | solution.py:21
  19.2 5.5 %collective-permute-start.4 = (f32[2,32,256]{2,1,0:T(8,128)S(1)}, f32[2,32,256]{2,1,0:T(8,128)S(1)}, u32[]{:S(2)}, u32[]{:S(2)}) collective-permute-start(f32[2,32,256]{2,1,0:T(8,128)S(1)} %get-tuple-element.54.refs_1_), channel_id=1, source_target_pairs={{8,0},{16,8},{24,16},{32,24},{40,32},{48,40},{56,48},{64,56},{72,6... | collective-permute-start | bytes 196616 | tf_op jit(solution)/shard_map/ppermute | solution.py:21
  20.5 6.1 %collective-permute-start.5 = (f32[2,32,256]{2,1,0:T(8,128)S(1)}, f32[2,32,256]{2,1,0:T(8,128)S(1)}, u32[]{:S(2)}, u32[]{:S(2)}) collective-permute-start(f32[2,32,256]{2,1,0:T(8,128)S(1)} %get-tuple-element.55.refs_2_), channel_id=1, source_target_pairs={{1,0},{2,1},{3,2},{4,3},{5,4},{6,5},{7,6},{9,8},{10,9},{11,10},{12... | collective-permute-start | bytes 196616 | tf_op jit(solution)/shard_map/ppermute | solution.py:21
  26.5 10.4 %collective-permute-start.6 = (f32[2,32,256]{2,1,0:T(8,128)S(1)}, f32[2,32,256]{2,1,0:T(8,128)S(1)}, u32[]{:S(2)}, u32[]{:S(2)}) collective-permute-start(f32[2,32,256]{2,1,0:T(8,128)S(1)} %get-tuple-element.59.refs_4_.hl_ref), channel_id=1, source_target_pairs={{0,8},{8,16},{16,24},{24,32},{32,40},{40,48},{48,56},{56,64},{64,7... | collective-permute-start | bytes 196616 | tf_op jit(solution)/shard_map/ppermute | solution.py:21
  30.8 6.2 %collective-permute-start.7 = (f32[2,32,256]{2,1,0:T(8,128)S(1)}, f32[2,32,256]{2,1,0:T(8,128)S(1)}, u32[]{:S(2)}, u32[]{:S(2)}) collective-permute-start(f32[2,32,256]{2,1,0:T(8,128)S(1)} %get-tuple-element.60.refs_5_.hr_ref), channel_id=1, source_target_pairs={{0,1},{1,2},{2,3},{3,4},{4,5},{5,6},{6,7},{8,9},{9,10},{10,11},{11... | collective-permute-start | bytes 196616 | tf_op jit(solution)/shard_map/ppermute | solution.py:21
  34.2 2.8 %copy-start.17 = (s32[1,128]{1,0:T(1,128)S(1)}, s32[1,128]{1,0:T(1,128)}, u32[]{:S(2)}) copy-start(s32[1,128]{1,0:T(1,128)} %dest.3) | copy-start | bytes 1540
  36.9 15.0 %copy-start.7 = (f32[128,8,256]{2,1,0:T(8,128)S(1)}, f32[128,8,256]{2,1,0:T(8,128)}, u32[]{:S(2)}) copy-start(f32[128,8,256]{2,1,0:T(8,128)} %t_ref.2) | copy-start | bytes 3145732
  36.9 15.0 %copy-start.16 = (f32[4,16]{1,0:T(4,128)S(1)}, f32[4,16]{1,0:T(4,128)}, u32[]{:S(2)}) copy-start(f32[4,16]{1,0:T(4,128)} %lines.1) | copy-start | bytes 772
  36.9 15.0 %copy-start.18 = (s32[1,128]{1,0:T(1,128)S(1)}, s32[1,128]{1,0:T(1,128)}, u32[]{:S(2)}) copy-start(s32[1,128]{1,0:T(1,128)} %arrive.3) | copy-start | bytes 1540
  38.8 32.1 %all-to-all-start = ((f32[128,8,256]{2,1,0:T(8,128)}), f32[128,8,256]{2,1,0:T(8,128)}, u32[]{:S(2)}, u32[]{:S(2)}) async-start(f32[128,8,256]{2,1,0:T(8,128)} %get-tuple-element.64), calls=%async_computation | async-start | bytes 2097152 | tf_op jit(solution)/shard_map/all_to_all | solution.py:662
  52.0 1.2 %copy-start.9 = (f32[128,8,256]{2,1,0:T(8,128)S(1)}, f32[128,8,256]{2,1,0:T(8,128)}, u32[]{:S(2)}) copy-start(f32[128,8,256]{2,1,0:T(8,128)} %w_ref.2) | copy-start | bytes 3145732
  53.2 1.2 %copy-start.14 = (s32[128,8,256]{2,1,0:T(8,128)S(1)}, s32[128,8,256]{2,1,0:T(8,128)}, u32[]{:S(2)}) copy-start(s32[128,8,256]{2,1,0:T(8,128)} %c_ref) | copy-start | bytes 3145732
  75.1 5.9 %copy-start.4 = (f32[32,32,256]{2,1,0:T(8,128)S(1)}, f32[32,32,256]{2,1,0:T(8,128)}, u32[]{:S(2)}) copy-start(f32[32,32,256]{2,1,0:T(8,128)} %sig_ref.1) | copy-start | bytes 3145732
  75.1 36.1 %all-to-all-start.1 = ((f32[128,16,256]{2,1,0:T(8,128)}), f32[128,16,256]{2,1,0:T(8,128)}, u32[]{:S(2)}, u32[]{:S(2)}) async-start(f32[128,16,256]{2,1,0:T(8,128)} %thermal.1), calls=%async_computation.1 | async-start | bytes 4194304 | tf_op jit(solution)/shard_map/all_to_all | solution.py:662
  81.0 3.1 %copy-start.12 = (f32[3,32,32,256]{3,2,1,0:T(8,128)S(1)}, f32[3,32,32,256]{3,2,1,0:T(8,128)}, u32[]{:S(2)}) copy-start(f32[3,32,32,256]{3,2,1,0:T(8,128)} %get-tuple-element.73.h_ref) | copy-start | bytes 9437188
  81.0 1.4 %copy-start.15 = (s32[32,32,256]{2,1,0:T(8,128)S(1)}, s32[32,32,256]{2,1,0:T(8,128)}, u32[]{:S(2)}) copy-start(s32[32,32,256]{2,1,0:T(8,128)} %lab_ref) | copy-start | bytes 3145732
  82.7 1.3 %copy-start.5 = (f32[2,32,32,256]{3,2,1,0:T(8,128)}, f32[2,32,32,256]{3,2,1,0:T(8,128)S(1)}, u32[]{:S(2)}) copy-start(f32[2,32,32,256]{3,2,1,0:T(8,128)S(1)} %near.1.kept) | copy-start | bytes 6291460
  84.1 1.9 %copy-start.13 = (f32[3,32,32,256]{3,2,1,0:T(8,128)S(1)}, f32[3,32,32,256]{3,2,1,0:T(8,128)}, u32[]{:S(2)}) copy-start(f32[3,32,32,256]{3,2,1,0:T(8,128)} %get-tuple-element.70.e_ref) | copy-start | bytes 9437188
  86.0 3.2 %copy-start.8 = (f32[128,8,256]{2,1,0:T(8,128)S(1)}, f32[128,8,256]{2,1,0:T(8,128)}, u32[]{:S(2)}) copy-start(f32[128,8,256]{2,1,0:T(8,128)} %t_ref.2) | copy-start | bytes 3145732
  86.0 3.2 %copy-start.10 = (f32[128,8,256]{2,1,0:T(8,128)S(1)}, f32[128,8,256]{2,1,0:T(8,128)}, u32[]{:S(2)}) copy-start(f32[128,8,256]{2,1,0:T(8,128)} %w_ref.2) | copy-start | bytes 3145732
  89.2 22.1 %copy-start.6 = (f32[2,32,32,256]{3,2,1,0:T(8,128)S(1)}, f32[2,32,32,256]{3,2,1,0:T(8,128)}, u32[]{:S(2)}) copy-start(f32[2,32,32,256]{3,2,1,0:T(8,128)} %copy-done.5) | copy-start | bytes 6291460
